TPU v7x, 256 devices: a whole 4x4x8 slice. The times are simulated.
256 devices in a mesh: rep: 4 (over z_hi), fsdp: 64 (over y, z_lo, x, core).
Axes of the slice: x: 4, y: 4, z: 8 (z_hi: 4, z_lo: 2; z = z_hi * 2 + z_lo), core: 2. Of those that a mesh axis runs over, the one named last changes fastest.
Arguments:
- activations: bfloat16 [49152, 8192], P(('rep', 'fsdp')), may hold values from -6 to 6
- cotangent: bfloat16 [49152, 14336], P(('rep', 'fsdp')), may hold values from -0.109375 to 0.109375
- projector: bfloat16 [8192, 256], P('fsdp'), may hold values from -0.0625 to 0.0625
- moment1: float32 [256, 14336], P(None, 'fsdp'), may hold values from -4 to 4
- moment2: float32 [256, 14336], P(None, 'fsdp'), may hold values from 0.1 to 4
Outputs:
- moment1_new: float32 [256, 14336], P(None, 'fsdp')
- moment2_new: float32 [256, 14336], P(None, 'fsdp')
- update: bfloat16 [8192, 14336], P(None, 'fsdp')
All inputs are finite; a program needn't handle non-finite values.
Results may differ from a plain program's by a relative error of at most 0.0051.
Values may be sent and summed in bfloat16 or wider, within the bound.
A program may use at most 128 MiB of HBM per device.

v0:
```python
import jax
import jax.numpy as jnp
from jax import lax
from jax.sharding import PartitionSpec as P

STEP = 100


def adam_moments(grad, moment1, moment2):
    return (0.9 * moment1 + 0.1 * grad, 0.999 * moment2 + 0.001 * grad * grad)


def body(activations, cotangent, projector, moment1, moment2):
    low = jnp.dot(
        activations,
        lax.all_gather(projector, "fsdp", axis=0, tiled=True),
        preferred_element_type=jnp.float32,
    ).astype(jnp.bfloat16)
    group_grad = lax.psum_scatter(
        lax.dot_general(
            cotangent, low, (((0,), (0,)), ((), ())), preferred_element_type=jnp.float32
        ),
        "fsdp",
        scatter_dimension=0,
        tiled=True,
    ).T
    grad = lax.psum(group_grad, "rep")
    moment1_new, moment2_new = adam_moments(grad, moment1, moment2)
    first_fix = 1.0 - 0.9**STEP
    second_fix = 1.0 - 0.999**STEP
    direction = (moment1_new / first_fix / (jnp.sqrt(moment2_new / second_fix) + 1e-08)).astype(
        jnp.bfloat16
    )
    update = jnp.dot(
        lax.all_gather(projector, "fsdp", axis=0, tiled=True),
        direction,
        preferred_element_type=jnp.float32,
    )
    return (moment1_new, moment2_new, update.astype(jnp.bfloat16))


def solution(mesh):
    return jax.shard_map(
        body,
        mesh=mesh,
        in_specs=(
            P(("rep", "fsdp"), None),
            P(("rep", "fsdp"), None),
            P("fsdp", None),
            P(None, "fsdp"),
            P(None, "fsdp"),
        ),
        out_specs=(P(None, "fsdp"), P(None, "fsdp"), P(None, "fsdp")),
        check_vma=False,
    )
```

profile of v0, /device:TPU:2, one launch (start us, length us, event | category | flops | bytes accessed | tf_op | source)
XLA Modules:
  0.0 528.2 jit_solution(4577761439493059855)
XLA Ops:
  7.2 0.0 copy-start
  7.2 0.0 all-gather.2.cloned.1.call-start
  7.2 0.7 all-gather.2.cloned.1.call-update
  7.9 0.0 reduce-scatter.4.cloned.1.call-start
  8.0 111.9 %all-gather.2.cloned.1.call-done = bf16[8192,256]{1,0:T(8,128)(2,1)} async-done(((bf16[128,256]{1,0:T(8,128)(2,1)}), bf16[8192,256]{1,0:T(8,128)(2,1)}) %all-gather.2.cloned.1.call-update) | async-done | bytes 4194320 | tf_op jit(solution)/shard_map/all_gather | solution.py:16
  119.8 0.0 copy-done
  119.8 13.7 %convolution_bitcast_fusion = f32[14336,256]{0,1:T(8,128)} fusion(bf16[192,14336]{1,0:T(8,128)(2,1)} %param.6, bf16[192,8192]{1,0:T(8,128)(2,1)S(1)} %copy-done, bf16[8192,256]{1,0:T(8,128)(2,1)} %all-gather.2.cloned.1.call-done), kind=kOutput, calls=%fused_computation | convolution fusion | flops 2214641664 | bytes 27525120 | tf_op jit(solution)/shard_map/dot_general | solution.py:20
  133.5 15.2 %copy.16 = f32[14336,256]{1,0:T(8,128)} copy(f32[14336,256]{0,1:T(8,128)} %convolution_bitcast_fusion) | data formatting | bytes 29360128
  148.7 0.0 copy-start.1
  148.7 0.0 reduce-scatter.4.cloned.1.call-update
  148.7 0.0 all-reduce.2.cloned.1.call-start
  148.7 306.7 %reduce-scatter.4.cloned.1.call-done = f32[224,256]{1,0:T(8,128)} async-done(((f32[14336,256]{1,0:T(8,128)}), f32[224,256]{1,0:T(8,128)}) %reduce-scatter.4.cloned.1.call-update) | async-done | bytes 229392
  455.4 1.8 copy.17
  457.2 0.0 all-reduce.2.cloned.1.call-update
  457.2 0.0 copy-done.1
  457.2 0.8 copy.12
  458.1 1.8 copy.13
  459.9 51.7 %all-reduce.2.cloned.1.call-done = f32[256,224]{1,0:T(8,128)} async-done(((f32[256,224]{1,0:T(8,128)}), f32[256,224]{1,0:T(8,128)}) %all-reduce.2.cloned.1.call-update) | async-done | bytes 229392 | tf_op jit(solution)/shard_map/psum | solution.py:27
  511.5 1.9 fusion.1
  513.4 1.8 copy.14
  515.2 0.8 copy.15
  516.0 5.6 %fusion = bf16[8192,224]{0,1:T(8,128)(2,1)} fusion(bf16[8192,256]{1,0:T(8,128)(2,1)} %all-gather.2.cloned.1.call-done, f32[256,224]{1,0:T(8,128)S(1)} %get-tuple-element.9, f32[256,224]{1,0:T(8,128)} %get-tuple-element.10), kind=kOutput, calls=%fused_computation.2 | convolution fusion | flops 941645824 | bytes 8323072 | tf_op jit(solution)/shard_map/dot_general | solution.py:34
Async XLA Ops:
  7.2 112.7 %copy-start = (bf16[192,8192]{1,0:T(8,128)(2,1)S(1)}, bf16[192,8192]{1,0:T(8,128)(2,1)}, u32[]{:S(2)}) copy-start(bf16[192,8192]{1,0:T(8,128)(2,1)} %param.5) | copy-start | bytes 9437188
  7.2 112.6 %all-gather.2.cloned.1.call-start = ((), (), s32[]{:S(2)}) async-start(), calls=%async_computation.1 | async-start | bytes 4259840 | tf_op jit(solution)/shard_map/all_gather | solution.py:16
  7.9 447.5 %reduce-scatter.4.cloned.1.call-start = ((), (), s32[]{:S(2)}) async-start(), calls=%async_computation.3 | async-start | bytes 14909440
  148.7 308.6 %copy-start.1 = (f32[256,224]{0,1:T(8,128)S(1)}, f32[256,224]{0,1:T(8,128)}, u32[]{:S(2)}) copy-start(f32[256,224]{0,1:T(8,128)} %param.8) | copy-start | bytes 688132
  148.7 362.8 %all-reduce.2.cloned.1.call-start = ((), (), s32[]{:S(2)}) async-start(), calls=%async_computation.2 | async-start | bytes 524288 | tf_op jit(solution)/shard_map/psum | solution.py:27
Sparse Core Ops, SparseCore 0:
  9.8 109.9 all-gather.1
  148.8 306.5 reduce-scatter.3
  458.6 52.8 all-reduce.1
where the time goes:
time: 529 us; the launch traced here: 528 us
  waiting for transfers between devices  471 us (89%)
  local copies, waits for them, and re-layouts  22.1 us (4%)
  matrix products  19.3 us (4%)
  between operations  13.8 us (3%)
    unnamed x4, waiting for transfers between devices  307 us
    all_gather x1, waiting for transfers between devices, body(): lax.all_gather(projector, 'fsdp', axis=0, tiled=True)  112 us
    psum x1, waiting for transfers between devices, body(): grad = lax.psum(group_grad, 'rep')  51.7 us
    unnamed x10, local copies, waits for them, and re-layouts  22.1 us
    dot_general x1, matrix products, body(): lax.dot_general(cotangent, low, (((0,), (0,)), ((), ())), preferred_eleme...  13.7 us
  transfers between devices with their start and end apart: 3, of which 3 were waited for; matrix products, arithmetic and copies ran while one was open for 0% of the time, Pallas kernels for 0%

commit v1 on v0

v1 whole, which is shorter than its diff:
```python
import jax
import jax.numpy as jnp
from jax import lax
from jax.sharding import Mesh
from jax.sharding import PartitionSpec as P

STEP = 100

SUB = ("y", "zl", "x", "core")


def adam_moments(grad, moment1, moment2):
    return (0.9 * moment1 + 0.1 * grad, 0.999 * moment2 + 0.001 * grad * grad)


def gather_projector(projector, sizes):
    rows, width = projector.shape
    full = projector
    for name in ("y", "x", "zl", "core"):
        full = lax.all_gather(full, name, axis=0, tiled=False)
    full = jnp.transpose(full, (3, 1, 2, 0, 4, 5))
    return full.reshape(-1, width)


def body(activations, cotangent, projector, moment1, moment2):
    sizes = {n: lax.axis_size(n) for n in SUB}
    proj_full = gather_projector(projector, sizes)
    low = jnp.dot(activations, proj_full, preferred_element_type=jnp.float32).astype(jnp.bfloat16)
    terms = lax.dot_general(
        cotangent, low, (((0,), (0,)), ((), ())), preferred_element_type=jnp.float32
    )
    ff, rank = terms.shape
    cols = ff // (sizes["y"] * sizes["zl"] * sizes["x"] * sizes["core"])
    terms = terms.reshape(sizes["y"], sizes["zl"], sizes["x"], sizes["core"], cols, rank)
    terms = jnp.transpose(terms, (3, 2, 1, 0, 4, 5))
    for name in ("core", "x", "zl", "y"):
        terms = terms.reshape(sizes[name], -1, rank)
        terms = lax.psum_scatter(terms, name, scatter_dimension=0, tiled=True)
    group_grad = terms.reshape(cols, rank).T
    grad = lax.psum(group_grad, "rep")
    moment1_new, moment2_new = adam_moments(grad, moment1, moment2)
    first_fix = 1.0 - 0.9**STEP
    second_fix = 1.0 - 0.999**STEP
    direction = (moment1_new / first_fix / (jnp.sqrt(moment2_new / second_fix) + 1e-08)).astype(
        jnp.bfloat16
    )
    update = jnp.dot(proj_full, direction, preferred_element_type=jnp.float32)
    return (moment1_new, moment2_new, update.astype(jnp.bfloat16))


def solution(mesh):
    rep = mesh.shape["rep"]
    fsdp_devices = mesh.devices.reshape(rep, -1)
    n = fsdp_devices.shape[1]
    y, x, core = 4, 4, 2
    zl = n // (y * x * core)
    fine = Mesh(mesh.devices.reshape(rep, y, zl, x, core), ("rep",) + SUB)
    tok = ("rep",) + SUB
    return jax.shard_map(
        body,
        mesh=fine,
        in_specs=(
            P(tok, None),
            P(tok, None),
            P(SUB, None),
            P(None, SUB),
            P(None, SUB),
        ),
        out_specs=(P(None, SUB), P(None, SUB), P(None, SUB)),
        check_vma=False,
    )
```

time: 529 us -> 400 us (0.76)
  waiting for transfers between devices: 471 us -> 318 us
  blocking collectives: 0 us -> 14.7 us
  local copies, waits for them, and re-layouts: 22.1 us -> 31.9 us
    unnamed x4 -> x8, waiting for transfers between devices: 307 us -> 0.13 us
    reduce_scatter x0 -> x4, waiting for transfers between devices: none -> 175 us  [body(): terms = lax.psum_scatter(terms, name, scatter_dimension=0, tiled=True)]
    all_gather x1 -> x3, waiting for transfers between devices: 112 us -> 89.7 us  [gather_projector(): full = lax.all_gather(full, name, axis=0, tiled=False)]
    unnamed x10 -> x12, local copies, waits for them, and re-layouts: 22.1 us -> 0.04 us
    transpose x0 -> x2, local copies, waits for them, and re-layouts: none -> 16.7 us  [the longest x1 12.1 us: body(): terms = jnp.transpose(terms, (3, 2, 1, 0, 4, 5))]
    dot_general x0 -> x1, local copies, waits for them, and re-layouts: none -> 15.2 us  [body(): lax.dot_general(cotangent, low, (((0,), (0,)), ((), ())), preferred_eleme...]
    all_gather x0 -> x1, blocking collectives: none -> 14.7 us  [gather_projector(): full = lax.all_gather(full, name, axis=0, tiled=False)]
  transfers between devices with their start and end apart: 3 -> 8, of which waited for: 3 -> 8; matrix products, arithmetic and copies ran while one was open for 0% -> 0% of each run, Pallas kernels for 0% -> 0%
where the time goes in v1:
time: 400 us
  waiting for transfers between devices  318 us (80%)
  local copies, waits for them, and re-layouts  31.9 us (8%)
  matrix products  19.4 us (5%)
  blocking collectives  14.7 us (4%)
  between operations  14.2 us (4%)
    reduce_scatter x4, waiting for transfers between devices, body(): terms = lax.psum_scatter(terms, name, scatter_dimension=0, tiled=True)  175 us
    all_gather x3, waiting for transfers between devices, gather_projector(): full = lax.all_gather(full, name, axis=0, tiled=False)  89.7 us
    psum x1, waiting for transfers between devices, body(): grad = lax.psum(group_grad, 'rep')  53.2 us
    dot_general x1, local copies, waits for them, and re-layouts, body(): lax.dot_general(cotangent, low, (((0,), (0,)), ((), ())), preferred_eleme...  15.2 us
    all_gather x1, blocking collectives, gather_projector(): full = lax.all_gather(full, name, axis=0, tiled=False)  14.7 us
    dot_general x1, matrix products, body(): lax.dot_general(cotangent, low, (((0,), (0,)), ((), ())), preferred_eleme...  13.7 us
    transpose x1, local copies, waits for them, and re-layouts, body(): terms = jnp.transpose(terms, (3, 2, 1, 0, 4, 5))  12.1 us
  transfers between devices with their start and end apart: 8, of which 8 were waited for; matrix products, arithmetic and copies ran while one was open for 0% of the time, Pallas kernels for 0%

profile of v1, /device:TPU:2, one launch (start us, length us, event | category | flops | bytes accessed | tf_op | source)
XLA Modules:
  0.0 399.8 jit_solution(15152701274888904489)
XLA Ops:
  7.2 0.0 copy-start
  7.2 0.0 all-gather.8.cloned.1.call-start
  7.2 14.7 %all-gather = bf16[512,256]{1,0:T(8,128)(2,1)} all-gather(bf16[128,256]{1,0:T(8,128)(2,1)} %param.7), channel_id=2, replica_groups=mesh['rep'=4,'y'=4,'zl'=2,'x'=4,'core'=2] {'y'}, dimensions={0}, use_global_device_ids=true | all-gather | bytes 327680 | tf_op jit(solution)/shard_map/all_gather | solution.py:20
  21.9 0.0 all-gather.8.cloned.1.call-update
  22.0 0.0 all-gather.10.cloned.1.call-start
  22.0 27.0 %all-gather.8.cloned.1.call-done = bf16[16,128,256]{2,1,0:T(8,128)(2,1)} async-done(((bf16[4,128,256]{2,1,0:T(8,128)(2,1)}), bf16[16,128,256]{2,1,0:T(8,128)(2,1)}) %all-gather.8.cloned.1.call-update) | async-done | bytes 1048592 | tf_op jit(solution)/shard_map/all_gather | solution.py:20
  49.0 0.0 all-gather.10.cloned.1.call-update
  49.0 0.0 all-gather.12.cloned.1.call-start
  49.1 41.5 %all-gather.10.cloned.1.call-done = bf16[8,4,128,256]{3,2,1,0:T(8,128)(2,1)} async-done(((bf16[4,4,128,256]{3,2,1,0:T(8,128)(2,1)}), bf16[8,4,128,256]{3,2,1,0:T(8,128)(2,1)}) %all-gather.10.cloned.1.call-update) | async-done | bytes 2097168 | tf_op jit(solution)/shard_map/all_gather | solution.py:20
  90.6 0.0 all-gather.12.cloned.1.call-update
  90.6 0.0 reduce-scatter.5.cloned.1.call-start
  90.7 21.2 %all-gather.12.cloned.1.call-done = bf16[4,4,4,128,256]{4,3,2,1,0:T(8,128)(2,1)} async-done(((bf16[2,4,4,128,256]{4,3,2,1,0:T(8,128)(2,1)}), bf16[4,4,4,128,256]{4,3,2,1,0:T(8,128)(2,1)}) %all-gather.12.cloned.1.call-update) | async-done | bytes 4194320 | tf_op jit(solution)/shard_map/all_gather | solution.py:20
  111.8 4.6 %copy.13 = bf16[4,2,4,2,128,256]{5,4,3,2,1,0:T(8,128)(2,1)} copy(bf16[4,2,4,2,128,256]{5,4,0,2,1,3:T(8,128)(2,1)} %bitcast.39) | data formatting | bytes 8388608 | tf_op jit(solution)/shard_map/transpose | solution.py:21
  116.5 0.0 copy-done
  116.5 13.7 %convolution_bitcast_fusion = f32[14336,256]{0,1:T(8,128)} fusion(bf16[192,14336]{1,0:T(8,128)(2,1)} %param.6, bf16[192,8192]{1,0:T(8,128)(2,1)S(1)} %copy-done, bf16[8192,256]{1,0:T(8,128)(2,1)} %bitcast.36), kind=kOutput, calls=%fused_computation | convolution fusion | flops 2214641664 | bytes 27525120 | tf_op jit(solution)/shard_map/dot_general | solution.py:29
  130.1 15.2 %copy.14 = f32[14336,256]{1,0:T(8,128)} copy(f32[14336,256]{0,1:T(8,128)} %convolution_bitcast_fusion) | data formatting | bytes 29360128 | tf_op jit(solution)/shard_map/dot_general | solution.py:29
  145.3 12.1 %copy.15 = f32[2,4,2,4,224,256]{5,4,3,2,1,0:T(8,128)} copy(f32[2,4,2,4,224,256]{5,4,0,1,2,3:T(8,128)} %bitcast.35) | data formatting | bytes 29360128 | tf_op jit(solution)/shard_map/transpose | solution.py:35
  157.4 0.0 reduce-scatter.5.cloned.1.call-update
  157.4 0.0 reduce-scatter.7.cloned.1.call-start
  157.4 31.7 %reduce-scatter.5.cloned.1.call-done = f32[1,7168,256]{2,1,0:T(8,128)} async-done(((f32[2,7168,256]{2,1,0:T(8,128)}), f32[1,7168,256]{2,1,0:T(8,128)}) %reduce-scatter.5.cloned.1.call-update) | async-done | bytes 7340048 | tf_op jit(solution)/shard_map/reduce_scatter | solution.py:38
  189.1 0.0 copy-start.4
  189.1 0.0 copy-start.5
  189.1 0.0 reduce-scatter.7.cloned.1.call-update
  189.1 0.0 reduce-scatter.9.cloned.1.call-start
  189.2 77.5 %reduce-scatter.7.cloned.1.call-done = f32[1,1792,256]{2,1,0:T(8,128)} async-done(((f32[4,1792,256]{2,1,0:T(8,128)}), f32[1,1792,256]{2,1,0:T(8,128)}) %reduce-scatter.7.cloned.1.call-update) | async-done | bytes 1835024 | tf_op jit(solution)/shard_map/reduce_scatter | solution.py:38
  266.6 0.0 reduce-scatter.9.cloned.1.call-update
  266.7 0.0 reduce-scatter.11.cloned.1.call-start
  266.7 37.5 %reduce-scatter.9.cloned.1.call-done = f32[1,896,256]{2,1,0:T(8,128)} async-done(((f32[2,896,256]{2,1,0:T(8,128)}), f32[1,896,256]{2,1,0:T(8,128)}) %reduce-scatter.9.cloned.1.call-update) | async-done | bytes 917520 | tf_op jit(solution)/shard_map/reduce_scatter | solution.py:38
  304.2 0.0 reduce-scatter.11.cloned.1.call-update
  304.3 0.0 all-reduce.2.cloned.1.call-start
  304.3 28.6 %reduce-scatter.11.cloned.1.call-done = f32[1,224,256]{2,1,0:T(8,128)} async-done(((f32[4,224,256]{2,1,0:T(8,128)}), f32[1,224,256]{2,1,0:T(8,128)}) %reduce-scatter.11.cloned.1.call-update) | async-done | bytes 229392 | tf_op jit(solution)/shard_map/reduce_scatter | solution.py:38
  332.9 0.0 all-reduce.2.cloned.1.call-update
  332.9 53.2 %all-reduce.2.cloned.1.call-done = f32[256,224]{0,1:T(8,128)} async-done(((f32[256,224]{0,1:T(8,128)}), f32[256,224]{0,1:T(8,128)}) %all-reduce.2.cloned.1.call-update) | async-done | bytes 229392 | tf_op jit(solution)/shard_map/psum | solution.py:40
  386.1 0.0 copy-done.4
  386.1 0.0 copy-done.5
  386.1 1.0 fusion.1
  387.1 0.0 copy-start.2
  387.2 0.0 copy-start.3
  387.2 0.0 copy-start.1
  387.2 5.7 %fusion = bf16[8192,224]{0,1:T(8,128)(2,1)} fusion(bf16[8192,256]{1,0:T(8,128)(2,1)} %bitcast.37, f32[256,224]{0,1:T(8,128)S(1)} %get-tuple-element.3, f32[256,224]{0,1:T(8,128)S(1)} %get-tuple-element.4), kind=kOutput, calls=%fused_computation.2 | convolution fusion | flops 941645824 | bytes 8323072 | tf_op jit(solution)/shard_map/dot_general | solution.py:47
  392.9 0.0 copy-done.2
  392.9 0.0 copy-done.3
  392.9 0.0 copy-done.1
Async XLA Ops:
  7.2 109.3 %copy-start = (bf16[192,8192]{1,0:T(8,128)(2,1)S(1)}, bf16[192,8192]{1,0:T(8,128)(2,1)}, u32[]{:S(2)}) copy-start(bf16[192,8192]{1,0:T(8,128)(2,1)} %param.5) | copy-start | bytes 9437188
  7.2 41.8 %all-gather.8.cloned.1.call-start = ((), (), s32[]{:S(2)}) async-start(), calls=%async_computation.9 | async-start | bytes 1310720 | tf_op jit(solution)/shard_map/all_gather | solution.py:20
  22.0 68.7 %all-gather.10.cloned.1.call-start = ((), (), s32[]{:S(2)}) async-start(), calls=%async_computation.10 | async-start | bytes 3145728 | tf_op jit(solution)/shard_map/all_gather | solution.py:20
  49.0 62.8 %all-gather.12.cloned.1.call-start = ((), (), s32[]{:S(2)}) async-start(), calls=%async_computation.11 | async-start | bytes 6291456 | tf_op jit(solution)/shard_map/all_gather | solution.py:20
  90.6 98.5 %reduce-scatter.5.cloned.1.call-start = ((), (), s32[]{:S(2)}) async-start(), calls=%async_computation.4 | async-start | bytes 22020096 | tf_op jit(solution)/shard_map/reduce_scatter | solution.py:38
  157.4 109.3 %reduce-scatter.7.cloned.1.call-start = ((), (), s32[]{:S(2)}) async-start(), calls=%async_computation.5 | async-start | bytes 9175040 | tf_op jit(solution)/shard_map/reduce_scatter | solution.py:38
  189.1 197.1 %copy-start.4 = (f32[256,224]{0,1:T(8,128)S(1)}, f32[256,224]{0,1:T(8,128)}, u32[]{:S(2)}) copy-start(f32[256,224]{0,1:T(8,128)} %param.9) | copy-start | bytes 688132
  189.1 197.1 %copy-start.5 = (f32[256,224]{0,1:T(8,128)S(1)}, f32[256,224]{0,1:T(8,128)}, u32[]{:S(2)}) copy-start(f32[256,224]{0,1:T(8,128)} %param.8) | copy-start | bytes 688132
  189.1 115.1 %reduce-scatter.9.cloned.1.call-start = ((), (), s32[]{:S(2)}) async-start(), calls=%async_computation.6 | async-start | bytes 2752512 | tf_op jit(solution)/shard_map/reduce_scatter | solution.py:38
  266.7 66.3 %reduce-scatter.11.cloned.1.call-start = ((), (), s32[]{:S(2)}) async-start(), calls=%async_computation.7 | async-start | bytes 1146880 | tf_op jit(solution)/shard_map/reduce_scatter | solution.py:38
  304.3 81.9 %all-reduce.2.cloned.1.call-start = ((), (), s32[]{:S(2)}) async-start(), calls=%async_computation.8 | async-start | bytes 458752 | tf_op jit(solution)/shard_map/psum | solution.py:40
  387.1 5.8 %copy-start.2 = (f32[256,224]{0,1:T(8,128)}, f32[256,224]{0,1:T(8,128)S(1)}, u32[]{:S(2)}) copy-start(f32[256,224]{0,1:T(8,128)S(1)} %get-tuple-element.3) | copy-start | bytes 688132
  387.2 5.8 %copy-start.3 = (f32[256,224]{0,1:T(8,128)}, f32[256,224]{0,1:T(8,128)S(1)}, u32[]{:S(2)}) copy-start(f32[256,224]{0,1:T(8,128)S(1)} %get-tuple-element.4) | copy-start | bytes 688132
  387.2 5.8 %copy-start.1 = (bf16[192,8192]{1,0:T(8,128)(2,1)S(1)}, bf16[192,8192]{1,0:T(8,128)(2,1)}, u32[]{:S(2)}) copy-start(bf16[192,8192]{1,0:T(8,128)(2,1)} %param.5) | copy-start | bytes 9437188
Sparse Core Ops, SparseCore 0:
  22.1 26.8 all-gather.7
  50.8 39.7 all-gather.9
  92.4 19.3 all-gather.11
  157.5 31.5 reduce-scatter.4
  191.5 75.1 reduce-scatter.6
  269.0 35.1 reduce-scatter.8
  306.8 26.0 reduce-scatter.10
  335.5 50.5 all-reduce.1

commit v2 on v1

--- a/solution.py
+++ b/solution.py
@@ -13,31 +13,53 @@
     return (0.9 * moment1 + 0.1 * grad, 0.999 * moment2 + 0.001 * grad * grad)
 
 
+def pair_swap(x, name):
+    return lax.ppermute(x, name, [(0, 1), (1, 0)])
+
+
 def gather_projector(projector, sizes):
     rows, width = projector.shape
-    full = projector
-    for name in ("y", "x", "zl", "core"):
-        full = lax.all_gather(full, name, axis=0, tiled=False)
+    full = lax.all_gather(projector, "y", axis=0, tiled=False)
+    full = lax.all_gather(full, "x", axis=0, tiled=False)
+    other = pair_swap(full, "zl")
+    first = lax.axis_index("zl") == 0
+    full = jnp.stack([jnp.where(first, full, other), jnp.where(first, other, full)])
+    full = lax.all_gather(full, "core", axis=0, tiled=False)
     full = jnp.transpose(full, (3, 1, 2, 0, 4, 5))
     return full.reshape(-1, width)
+
+
+def all_sum_rep(x):
+    size = lax.axis_size("rep")
+    step = 1
+    while step < size:
+        x = x + lax.ppermute(x, "rep", [(i, i ^ step) for i in range(size)])
+        step *= 2
+    return x
 
 
 def body(activations, cotangent, projector, moment1, moment2):
     sizes = {n: lax.axis_size(n) for n in SUB}
     proj_full = gather_projector(projector, sizes)
     low = jnp.dot(activations, proj_full, preferred_element_type=jnp.float32).astype(jnp.bfloat16)
-    terms = lax.dot_general(
-        cotangent, low, (((0,), (0,)), ((), ())), preferred_element_type=jnp.float32
-    )
-    ff, rank = terms.shape
+    tok, ff = cotangent.shape
     cols = ff // (sizes["y"] * sizes["zl"] * sizes["x"] * sizes["core"])
-    terms = terms.reshape(sizes["y"], sizes["zl"], sizes["x"], sizes["core"], cols, rank)
-    terms = jnp.transpose(terms, (3, 2, 1, 0, 4, 5))
-    for name in ("core", "x", "zl", "y"):
+    cot = cotangent.reshape(tok, sizes["y"], sizes["zl"], sizes["x"], sizes["core"], cols)
+    cot = jnp.transpose(cot, (0, 4, 3, 2, 1, 5)).reshape(tok, ff)
+    terms = lax.dot_general(cot, low, (((0,), (0,)), ((), ())), preferred_element_type=jnp.float32)
+    rank = terms.shape[1]
+    for name in ("core", "x"):
         terms = terms.reshape(sizes[name], -1, rank)
         terms = lax.psum_scatter(terms, name, scatter_dimension=0, tiled=True)
+    terms = terms.reshape(sizes["zl"], -1, rank)
+    z = lax.axis_index("zl")
+    mine = lax.dynamic_index_in_dim(terms, z, 0, keepdims=False)
+    theirs = lax.dynamic_index_in_dim(terms, 1 - z, 0, keepdims=False)
+    terms = mine + pair_swap(theirs, "zl")
+    terms = terms.reshape(sizes["y"], -1, rank)
+    terms = lax.psum_scatter(terms, "y", scatter_dimension=0, tiled=True)
     group_grad = terms.reshape(cols, rank).T
-    grad = lax.psum(group_grad, "rep")
+    grad = all_sum_rep(group_grad)
     moment1_new, moment2_new = adam_moments(grad, moment1, moment2)
     first_fix = 1.0 - 0.9**STEP
     second_fix = 1.0 - 0.999**STEP

time: 400 us -> 350 us (0.88)
  waiting for transfers between devices: 318 us -> 224 us
  local copies, waits for them, and re-layouts: 31.9 us -> 58.5 us
  starting transfers between devices: 0.31 us -> 11.8 us
  other arithmetic: 1.01 us -> 6.44 us
    reduce_scatter x4 -> x2, waiting for transfers between devices: 175 us -> 109 us  [body(): terms = lax.psum_scatter(terms, name, scatter_dimension=0, tiled=True)]
    all_gather x3 -> x2, waiting for transfers between devices: 89.7 us -> 27 us  [the longest x1 27 us: gather_projector(): full = lax.all_gather(full, 'x', axis=0, tiled=False)]
    ppermute x0 -> x4, waiting for transfers between devices: none -> 60.7 us  [the longest x2 42.5 us: pair_swap(): return lax.ppermute(x, name, [(0, 1), (1, 0)])]
    psum x1 -> x0, waiting for transfers between devices: 53.2 us -> none  [body(): grad = lax.psum(group_grad, 'rep')]
    reshape x0 -> x4, local copies, waits for them, and re-layouts: none -> 52.6 us  [the longest x2 25 us: body(): cotangent.reshape(tok, sizes['y'], sizes['zl'], sizes['x'], sizes['core']...]
    reduce_scatter x0 -> x1, waiting for transfers between devices: none -> 26.9 us  [body(): terms = lax.psum_scatter(terms, 'y', scatter_dimension=0, tiled=True)]
    dot_general x1 -> x0, local copies, waits for them, and re-layouts: 15.2 us -> none  [body(): lax.dot_general(cotangent, low, (((0,), (0,)), ((), ())), preferred_eleme...]
    transpose x1 -> x0, local copies, waits for them, and re-layouts: 12.1 us -> none  [body(): terms = jnp.transpose(terms, (3, 2, 1, 0, 4, 5))]
  transfers between devices with their start and end apart: 8 -> 9, of which waited for: 8 -> 8; matrix products, arithmetic and copies ran while one was open for 0% -> 11% of each run, Pallas kernels for 0% -> 0%
where the time goes in v2:
time: 350 us; the launch traced here: 349 us
  waiting for transfers between devices  224 us (64%)
  local copies, waits for them, and re-layouts  58.5 us (17%)
  matrix products  19.5 us (6%)
  blocking collectives  14.7 us (4%)
  between operations  13.9 us (4%)
  starting transfers between devices  11.8 us (3%)
  other arithmetic  6.44 us (2%)
    reduce_scatter x2, waiting for transfers between devices, body(): terms = lax.psum_scatter(terms, name, scatter_dimension=0, tiled=True)  109 us
    ppermute x2, waiting for transfers between devices, pair_swap(): return lax.ppermute(x, name, [(0, 1), (1, 0)])  42.5 us
    all_gather x1, waiting for transfers between devices, gather_projector(): full = lax.all_gather(full, 'x', axis=0, tiled=False)  27 us
    reduce_scatter x1, waiting for transfers between devices, body(): terms = lax.psum_scatter(terms, 'y', scatter_dimension=0, tiled=True)  26.9 us
    reshape x2, local copies, waits for them, and re-layouts, body(): cotangent.reshape(tok, sizes['y'], sizes['zl'], sizes['x'], sizes['core']...  25 us
    ppermute x2, waiting for transfers between devices, all_sum_rep(): x = x + lax.ppermute(x, 'rep', [(i, i ^ step) for i in range(size)])  18.2 us
    reshape x1, local copies, waits for them, and re-layouts, body(): terms = terms.reshape(sizes[name], -1, rank)  15.1 us
    all_gather x1, blocking collectives, gather_projector(): full = lax.all_gather(projector, 'y', axis=0, tiled=False)  14.7 us
  transfers between devices with their start and end apart: 9, of which 8 were waited for; matrix products, arithmetic and copies ran while one was open for 11% of the time, Pallas kernels for 0%

profile of v2, /device:TPU:2, one launch (start us, length us, event | category | flops | bytes accessed | tf_op | source)
XLA Modules:
  0.0 348.9 jit_solution(16407955329658504821)
XLA Ops:
  7.2 0.0 copy-start
  7.2 0.0 all-gather.6.cloned.1.call-start
  7.2 14.7 %all-gather = bf16[512,256]{1,0:T(8,128)(2,1)} all-gather(bf16[128,256]{1,0:T(8,128)(2,1)} %param.7), channel_id=2, replica_groups=mesh['rep'=4,'y'=4,'zl'=2,'x'=4,'core'=2] {'y'}, dimensions={0}, use_global_device_ids=true | all-gather | bytes 327680 | tf_op jit(solution)/shard_map/all_gather | solution.py:22
  21.9 0.0 all-gather.6.cloned.1.call-update
  21.9 0.0 all-gather.8.cloned.1.call-start
  22.0 27.0 %all-gather.6.cloned.1.call-done = bf16[16,128,256]{2,1,0:T(8,128)(2,1)} async-done(((bf16[4,128,256]{2,1,0:T(8,128)(2,1)}), bf16[16,128,256]{2,1,0:T(8,128)(2,1)}) %all-gather.6.cloned.1.call-update) | async-done | bytes 1048592 | tf_op jit(solution)/shard_map/all_gather | solution.py:23
  49.0 1.6 collective-permute-start
  50.6 22.1 %collective-permute-done = bf16[4,4,128,256]{3,2,1,0:T(8,128)(2,1)} collective-permute-done((bf16[4,4,128,256]{3,2,1,0:T(8,128)(2,1)}, bf16[4,4,128,256]{3,2,1,0:T(8,128)(2,1)}, u32[]{:S(2)}, u32[]{:S(2)}) %collective-permute-start) | collective-permute-done | bytes 1048608 | tf_op jit(solution)/shard_map/ppermute | solution.py:17
  72.6 1.7 select_bitcast_fusion.1
  74.3 1.5 pad_maximum_fusion
  75.8 0.0 all-gather.8.cloned.1.call-update
  75.8 0.0 reduce-scatter.4.cloned.1.call-start
  75.9 12.4 %reshape.31 = bf16[192,4,2,4,2,224]{5,4,3,2,1,0:T(2,128)(2,1)} reshape(bf16[192,14336]{1,0:T(8,128)(2,1)} %param.6) | data formatting | bytes 11010048 | tf_op jit(solution)/shard_map/reshape | solution.py:47
  88.3 12.6 %copy.22 = bf16[192,4,2,4,2,224]{5,1,2,3,4,0:T(4,128)(2,1)} copy(bf16[192,4,2,4,2,224]{5,4,3,2,1,0:T(2,128)(2,1)} %reshape.31) | data formatting | bytes 11010048 | tf_op jit(solution)/shard_map/reshape | solution.py:47
  100.9 12.4 %reshape.32 = bf16[192,14336]{1,0:T(8,128)(2,1)} reshape(bf16[192,2,4,2,4,224]{5,4,3,2,1,0:T(4,128)(2,1)} %bitcast.43) | data formatting | bytes 11010048 | tf_op jit(solution)/shard_map/reshape | solution.py:48
  113.3 0.0 all-gather.8.cloned.1.call-done
  113.3 4.6 %copy.17 = bf16[4,2,4,2,128,256]{5,4,3,2,1,0:T(8,128)(2,1)} copy(bf16[4,2,4,2,128,256]{5,4,0,2,1,3:T(8,128)(2,1)} %bitcast.45) | data formatting | bytes 8388608 | tf_op jit(solution)/shard_map/transpose | solution.py:28
  118.0 0.0 copy-done
  118.0 13.7 %convolution_bitcast_fusion = f32[14336,256]{0,1:T(8,128)} fusion(bf16[192,14336]{1,0:T(8,128)(2,1)} %reshape.32, bf16[192,8192]{1,0:T(8,128)(2,1)S(1)} %copy-done, bf16[8192,256]{1,0:T(8,128)(2,1)} %bitcast.41), kind=kOutput, calls=%fused_computation | convolution fusion | flops 2214641664 | bytes 27525120 | tf_op jit(solution)/shard_map/dot_general | solution.py:49
  131.7 15.1 %copy.20 = f32[14336,256]{1,0:T(8,128)} copy(f32[14336,256]{0,1:T(8,128)} %convolution_bitcast_fusion) | data formatting | bytes 29360128 | tf_op jit(solution)/shard_map/reshape | solution.py:52
  146.8 0.0 reduce-scatter.4.cloned.1.call-update
  146.9 0.0 reduce-scatter.6.cloned.1.call-start
  146.9 32.0 %reduce-scatter.4.cloned.1.call-done = f32[1,7168,256]{2,1,0:T(8,128)} async-done(((f32[2,7168,256]{2,1,0:T(8,128)}), f32[1,7168,256]{2,1,0:T(8,128)}) %reduce-scatter.4.cloned.1.call-update) | async-done | bytes 7340048 | tf_op jit(solution)/shard_map/reduce_scatter | solution.py:53
  178.9 0.0 reduce-scatter.6.cloned.1.call-update
  179.0 0.0 copy-start.4
  179.0 0.0 copy-start.5
  179.0 0.0 reduce-scatter.8.cloned.1.call-start
  179.0 77.5 %reduce-scatter.6.cloned.1.call-done = f32[1,1792,256]{2,1,0:T(8,128)} async-done(((f32[4,1792,256]{2,1,0:T(8,128)}), f32[1,1792,256]{2,1,0:T(8,128)}) %reduce-scatter.6.cloned.1.call-update) | async-done | bytes 1835024 | tf_op jit(solution)/shard_map/reduce_scatter | solution.py:53
  256.5 1.2 dynamic-slice_bitcast_fusion
  257.7 1.6 collective-permute-start.1
  259.4 20.5 %collective-permute-done.1 = f32[896,256]{1,0:T(8,128)S(1)} collective-permute-done((f32[896,256]{1,0:T(8,128)S(1)}, f32[896,256]{1,0:T(8,128)S(1)}, u32[]{:S(2)}, u32[]{:S(2)}) %collective-permute-start.1) | collective-permute-done | bytes 917536 | tf_op jit(solution)/shard_map/ppermute | solution.py:17
  279.9 2.2 bitcast_add_fusion
  282.1 0.0 reduce-scatter.8.cloned.1.call-update
  282.1 26.9 %reduce-scatter.8.cloned.1.call-done = f32[1,224,256]{2,1,0:T(8,128)} async-done(((f32[4,224,256]{2,1,0:T(8,128)}), f32[1,224,256]{2,1,0:T(8,128)}) %reduce-scatter.8.cloned.1.call-update) | async-done | bytes 229392 | tf_op jit(solution)/shard_map/reduce_scatter | solution.py:60
  309.0 2.5 collective-permute-start.2
  311.5 9.5 %collective-permute-done.2 = f32[256,224]{0,1:T(8,128)S(1)} collective-permute-done((f32[256,224]{0,1:T(8,128)}, f32[256,224]{0,1:T(8,128)S(1)}, u32[]{:S(2)}, u32[]{:S(2)}) %collective-permute-start.2) | collective-permute-done | bytes 229408 | tf_op jit(solution)/shard_map/ppermute | solution.py:36
  321.0 1.0 bitcast_add_fusion.1
  322.0 5.8 %collective-permute-start.3 = (f32[256,224]{0,1:T(8,128)S(1)}, f32[256,224]{0,1:T(8,128)S(1)}, u32[]{:S(2)}, u32[]{:S(2)}) collective-permute-start(f32[256,224]{0,1:T(8,128)S(1)} %bitcast_add_fusion.1), channel_id=1, source_target_pairs={{0,128},{64,192},{128,0},{192,64},{1,129},{65,193},{129,1},{193,65... | collective-permute-start | bytes 688136 | tf_op jit(solution)/shard_map/ppermute | solution.py:36
  327.8 8.6 %collective-permute-done.3 = f32[256,224]{0,1:T(8,128)S(1)} collective-permute-done((f32[256,224]{0,1:T(8,128)S(1)}, f32[256,224]{0,1:T(8,128)S(1)}, u32[]{:S(2)}, u32[]{:S(2)}) %collective-permute-start.3) | collective-permute-done | bytes 229408 | tf_op jit(solution)/shard_map/ppermute | solution.py:36
  336.5 0.0 copy-done.4
  336.5 0.0 copy-done.5
  336.5 0.1 fusion
  336.5 0.0 copy-start.2
  336.6 0.0 copy-start.3
  336.6 0.0 copy-start.1
  336.6 5.7 %convolution_convert_fusion = bf16[8192,224]{0,1:T(8,128)(2,1)} fusion(bf16[8192,256]{1,0:T(8,128)(2,1)} %bitcast.42, f32[256,224]{0,1:T(8,128)S(1)} %get-tuple-element.5, f32[256,224]{0,1:T(8,128)S(1)} %get-tuple-element.6), kind=kOutput, calls=%fused_computation.1 | convolution fusion | flops 941645824 | bytes 8323072 | tf_op jit(solution)/shard_map/dot_general | solution.py:69
  342.3 0.0 copy-done.2
  342.3 0.0 copy-done.3
  342.3 0.0 copy-done.1
Async XLA Ops:
  7.2 110.8 %copy-start = (bf16[192,8192]{1,0:T(8,128)(2,1)S(1)}, bf16[192,8192]{1,0:T(8,128)(2,1)}, u32[]{:S(2)}) copy-start(bf16[192,8192]{1,0:T(8,128)(2,1)} %param.5) | copy-start | bytes 9437188
  7.2 41.8 %all-gather.6.cloned.1.call-start = ((), (), s32[]{:S(2)}) async-start(), calls=%async_computation.6 | async-start | bytes 1310720 | tf_op jit(solution)/shard_map/all_gather | solution.py:23
  21.9 91.4 %all-gather.8.cloned.1.call-start = ((), (), s32[]{:S(2)}) async-start(), calls=%async_computation.7 | async-start | bytes 6291456 | tf_op jit(solution)/shard_map/all_gather | solution.py:27
  49.0 23.6 %collective-permute-start = (bf16[4,4,128,256]{3,2,1,0:T(8,128)(2,1)}, bf16[4,4,128,256]{3,2,1,0:T(8,128)(2,1)}, u32[]{:S(2)}, u32[]{:S(2)}) collective-permute-start(bf16[4,4,128,256]{3,2,1,0:T(8,128)(2,1)} %bitcast.49), channel_id=1, source_target_pairs={{0,8},{8,0},{1,9},{9,1},{2,10},{10,2},{3,11},{11,3},{4,12},{12,4},... | collective-permute-start | bytes 3145736 | tf_op jit(solution)/shard_map/ppermute | solution.py:17
  75.8 103.1 %reduce-scatter.4.cloned.1.call-start = ((), (), s32[]{:S(2)}) async-start(), calls=%async_computation.3 | async-start | bytes 22020096 | tf_op jit(solution)/shard_map/reduce_scatter | solution.py:53
  146.9 109.6 %reduce-scatter.6.cloned.1.call-start = ((), (), s32[]{:S(2)}) async-start(), calls=%async_computation.4 | async-start | bytes 9175040 | tf_op jit(solution)/shard_map/reduce_scatter | solution.py:53
  179.0 157.5 %copy-start.4 = (f32[256,224]{0,1:T(8,128)S(1)}, f32[256,224]{0,1:T(8,128)}, u32[]{:S(2)}) copy-start(f32[256,224]{0,1:T(8,128)} %param.9) | copy-start | bytes 688132
  179.0 157.5 %copy-start.5 = (f32[256,224]{0,1:T(8,128)S(1)}, f32[256,224]{0,1:T(8,128)}, u32[]{:S(2)}) copy-start(f32[256,224]{0,1:T(8,128)} %param.8) | copy-start | bytes 688132
  179.0 130.0 %reduce-scatter.8.cloned.1.call-start = ((), (), s32[]{:S(2)}) async-start(), calls=%async_computation.5 | async-start | bytes 1146880 | tf_op jit(solution)/shard_map/reduce_scatter | solution.py:60
  257.7 22.1 %collective-permute-start.1 = (f32[896,256]{1,0:T(8,128)S(1)}, f32[896,256]{1,0:T(8,128)S(1)}, u32[]{:S(2)}, u32[]{:S(2)}) collective-permute-start(f32[896,256]{1,0:T(8,128)S(1)} %dynamic-slice_bitcast_fusion), channel_id=1, source_target_pairs={{0,8},{8,0},{1,9},{9,1},{2,10},{10,2},{3,11},{11,3},{4,12},{12,4},... | collective-permute-start | bytes 2752520 | tf_op jit(solution)/shard_map/ppermute | solution.py:17
  309.0 12.1 %collective-permute-start.2 = (f32[256,224]{0,1:T(8,128)}, f32[256,224]{0,1:T(8,128)S(1)}, u32[]{:S(2)}, u32[]{:S(2)}) collective-permute-start(f32[256,224]{0,1:T(8,128)} %bitcast.52), channel_id=1, source_target_pairs={{0,64},{64,0},{128,192},{192,128},{1,65},{65,1},{129,193},{193,129... | collective-permute-start | bytes 688136 | tf_op jit(solution)/shard_map/ppermute | solution.py:36
  322.0 14.5 %collective-permute-start.3 = (f32[256,224]{0,1:T(8,128)S(1)}, f32[256,224]{0,1:T(8,128)S(1)}, u32[]{:S(2)}, u32[]{:S(2)}) collective-permute-start(f32[256,224]{0,1:T(8,128)S(1)} %bitcast_add_fusion.1), channel_id=1, source_target_pairs={{0,128},{64,192},{128,0},{192,64},{1,129},{65,193},{129,1},{193,65... | collective-permute-start | bytes 688136 | tf_op jit(solution)/shard_map/ppermute | solution.py:36
  336.5 5.8 %copy-start.2 = (f32[256,224]{0,1:T(8,128)}, f32[256,224]{0,1:T(8,128)S(1)}, u32[]{:S(2)}) copy-start(f32[256,224]{0,1:T(8,128)S(1)} %get-tuple-element.5) | copy-start | bytes 688132
  336.6 5.8 %copy-start.3 = (f32[256,224]{0,1:T(8,128)}, f32[256,224]{0,1:T(8,128)S(1)}, u32[]{:S(2)}) copy-start(f32[256,224]{0,1:T(8,128)S(1)} %get-tuple-element.6) | copy-start | bytes 688132
  336.6 5.8 %copy-start.1 = (bf16[192,8192]{1,0:T(8,128)(2,1)S(1)}, bf16[192,8192]{1,0:T(8,128)(2,1)}, u32[]{:S(2)}) copy-start(bf16[192,8192]{1,0:T(8,128)(2,1)} %param.5) | copy-start | bytes 9437188
Sparse Core Ops, SparseCore 0:
  22.1 26.8 all-gather.5
  75.9 20.5 all-gather.7
  147.0 31.9 reduce-scatter.3
  181.3 75.1 reduce-scatter.5
  282.2 26.6 reduce-scatter.7

commit v3 on v1

--- a/solution.py
+++ b/solution.py
@@ -7,6 +7,7 @@
 STEP = 100
 
 SUB = ("y", "zl", "x", "core")
+CHIPS = ("y", "zl", "x")
 
 
 def adam_moments(grad, moment1, moment2):
@@ -15,29 +16,38 @@
 
 def gather_projector(projector, sizes):
     rows, width = projector.shape
-    full = projector
-    for name in ("y", "x", "zl", "core"):
-        full = lax.all_gather(full, name, axis=0, tiled=False)
-    full = jnp.transpose(full, (3, 1, 2, 0, 4, 5))
+    full = lax.all_gather(projector, CHIPS, axis=0, tiled=False)
+    full = lax.all_gather(full, "core", axis=0, tiled=False)
+    full = jnp.transpose(full, (1, 0, 2, 3))
     return full.reshape(-1, width)
+
+
+def all_sum_rep(x):
+    size = lax.axis_size("rep")
+    step = 1
+    while step < size:
+        x = x + lax.ppermute(x, "rep", [(i, i ^ step) for i in range(size)])
+        step *= 2
+    return x
 
 
 def body(activations, cotangent, projector, moment1, moment2):
     sizes = {n: lax.axis_size(n) for n in SUB}
+    chips = sizes["y"] * sizes["zl"] * sizes["x"]
     proj_full = gather_projector(projector, sizes)
     low = jnp.dot(activations, proj_full, preferred_element_type=jnp.float32).astype(jnp.bfloat16)
     terms = lax.dot_general(
         cotangent, low, (((0,), (0,)), ((), ())), preferred_element_type=jnp.float32
     )
     ff, rank = terms.shape
-    cols = ff // (sizes["y"] * sizes["zl"] * sizes["x"] * sizes["core"])
-    terms = terms.reshape(sizes["y"], sizes["zl"], sizes["x"], sizes["core"], cols, rank)
-    terms = jnp.transpose(terms, (3, 2, 1, 0, 4, 5))
-    for name in ("core", "x", "zl", "y"):
-        terms = terms.reshape(sizes[name], -1, rank)
-        terms = lax.psum_scatter(terms, name, scatter_dimension=0, tiled=True)
+    cols = ff // (chips * sizes["core"])
+    terms = terms.reshape(chips, sizes["core"], cols, rank)
+    terms = jnp.transpose(terms, (1, 0, 2, 3)).reshape(sizes["core"], -1, rank)
+    terms = lax.psum_scatter(terms, "core", scatter_dimension=0, tiled=True)
+    terms = terms.reshape(chips, cols, rank)
+    terms = lax.psum_scatter(terms, CHIPS, scatter_dimension=0, tiled=True)
     group_grad = terms.reshape(cols, rank).T
-    grad = lax.psum(group_grad, "rep")
+    grad = all_sum_rep(group_grad)
     moment1_new, moment2_new = adam_moments(grad, moment1, moment2)
     first_fix = 1.0 - 0.9**STEP
     second_fix = 1.0 - 0.999**STEP

time: 400 us -> 487 us (1.22); the launches traced: 400 us -> 478 us
  waiting for transfers between devices: 318 us -> 403 us
  blocking collectives: 14.7 us -> 0 us
  starting transfers between devices: 0.31 us -> 8.55 us
    all_gather x3 -> x2, waiting for transfers between devices: 89.7 us -> 180 us  [the longest x1 160 us: gather_projector(): full = lax.all_gather(projector, CHIPS, axis=0, tiled=False)]
    psum x1 -> x0, waiting for transfers between devices: 53.2 us -> none  [body(): grad = lax.psum(group_grad, 'rep')]
    reduce_scatter x4 -> x2, waiting for transfers between devices: 175 us -> 213 us  [the longest x1 181 us: body(): terms = lax.psum_scatter(terms, CHIPS, scatter_dimension=0, tiled=True)]
    all_gather x1 -> x0, blocking collectives: 14.7 us -> none  [gather_projector(): full = lax.all_gather(full, name, axis=0, tiled=False)]
    ppermute x0 -> x2, waiting for transfers between devices: none -> 9.45 us  [all_sum_rep(): x = x + lax.ppermute(x, 'rep', [(i, i ^ step) for i in range(size)])]
    ppermute x0 -> x2, starting transfers between devices: none -> 8.4 us  [all_sum_rep(): x = x + lax.ppermute(x, 'rep', [(i, i ^ step) for i in range(size)])]
  transfers between devices with their start and end apart: 8 -> 6, of which waited for: 8 -> 6; matrix products, arithmetic and copies ran while one was open for 0% -> 0% of each run, Pallas kernels for 0% -> 0%
where the time goes in v3:
time: 487 us; the launch traced here: 478 us
  waiting for transfers between devices  403 us (83%)
  local copies, waits for them, and re-layouts  31.9 us (7%)
  matrix products  19.4 us (4%)
  between operations  13.8 us (3%)
  starting transfers between devices  8.55 us (2%)
    reduce_scatter x1, waiting for transfers between devices, body(): terms = lax.psum_scatter(terms, CHIPS, scatter_dimension=0, tiled=True)  181 us
    all_gather x1, waiting for transfers between devices, gather_projector(): full = lax.all_gather(projector, CHIPS, axis=0, tiled=False)  160 us
    reduce_scatter x1, waiting for transfers between devices, body(): terms = lax.psum_scatter(terms, 'core', scatter_dimension=0, tiled=True)  31.6 us
    all_gather x1, waiting for transfers between devices, gather_projector(): full = lax.all_gather(full, 'core', axis=0, tiled=False)  20.5 us
    dot_general x1, local copies, waits for them, and re-layouts, body(): lax.dot_general(cotangent, low, (((0,), (0,)), ((), ())), preferred_eleme...  15.1 us
    dot_general x1, matrix products, body(): lax.dot_general(cotangent, low, (((0,), (0,)), ((), ())), preferred_eleme...  13.7 us
    transpose x1, local copies, waits for them, and re-layouts, body(): terms = jnp.transpose(terms, (1, 0, 2, 3)).reshape(sizes['core'], -1, rank)  12.1 us
  transfers between devices with their start and end apart: 6, of which 6 were waited for; matrix products, arithmetic and copies ran while one was open for 0% of the time, Pallas kernels for 0%

profile of v3, /device:TPU:2, one launch (start us, length us, event | category | flops | bytes accessed | tf_op | source)
XLA Modules:
  0.0 477.7 jit_solution(11071153862208899327)
XLA Ops:
  7.2 0.0 copy-start
  7.2 0.0 all-gather.5.cloned.1.call-start
  7.2 0.7 all-gather.5.cloned.1.call-update
  7.9 0.0 all-gather.7.cloned.1.call-start
  8.0 159.7 %all-gather.5.cloned.1.call-done = bf16[4096,256]{1,0:T(8,128)(2,1)} async-done(((bf16[128,256]{1,0:T(8,128)(2,1)}), bf16[4096,256]{1,0:T(8,128)(2,1)}) %all-gather.5.cloned.1.call-update) | async-done | bytes 2097168 | tf_op jit(solution)/shard_map/all_gather | solution.py:19
  167.6 0.0 all-gather.7.cloned.1.call-update
  167.7 0.0 reduce-scatter.3.cloned.1.call-start
  167.7 20.5 %all-gather.7.cloned.1.call-done = bf16[64,128,256]{2,1,0:T(8,128)(2,1)} async-done(((bf16[32,128,256]{2,1,0:T(8,128)(2,1)}), bf16[64,128,256]{2,1,0:T(8,128)(2,1)}) %all-gather.7.cloned.1.call-update) | async-done | bytes 4194320 | tf_op jit(solution)/shard_map/all_gather | solution.py:20
  188.2 4.6 copy.13
  192.8 0.0 copy-done
  192.8 13.7 %convolution_bitcast_fusion = f32[14336,256]{0,1:T(8,128)} fusion(bf16[192,14336]{1,0:T(8,128)(2,1)} %param.6, bf16[192,8192]{1,0:T(8,128)(2,1)S(1)} %copy-done, bf16[8192,256]{1,0:T(8,128)(2,1)} %bitcast.33), kind=kOutput, calls=%fused_computation | convolution fusion | flops 2214641664 | bytes 27525120 | tf_op jit(solution)/shard_map/dot_general | solution.py:39
  206.5 15.1 %copy.14 = f32[14336,256]{1,0:T(8,128)} copy(f32[14336,256]{0,1:T(8,128)} %convolution_bitcast_fusion) | data formatting | bytes 29360128 | tf_op jit(solution)/shard_map/dot_general | solution.py:39
  221.7 12.1 %copy.15 = f32[2,32,224,256]{3,2,1,0:T(8,128)} copy(f32[2,32,224,256]{3,2,0,1:T(8,128)} %bitcast.32) | data formatting | bytes 29360128 | tf_op jit(solution)/shard_map/transpose | solution.py:45
  233.7 0.0 reduce-scatter.3.cloned.1.call-update
  233.7 0.0 copy-start.4
  233.8 0.0 copy-start.5
  233.8 0.0 reduce-scatter.5.cloned.1.call-start
  233.8 31.6 %reduce-scatter.3.cloned.1.call-done = f32[1,7168,256]{2,1,0:T(8,128)} async-done(((f32[2,7168,256]{2,1,0:T(8,128)}), f32[1,7168,256]{2,1,0:T(8,128)}) %reduce-scatter.3.cloned.1.call-update) | async-done | bytes 7340048 | tf_op jit(solution)/shard_map/reduce_scatter | solution.py:46
  265.4 0.0 reduce-scatter.5.cloned.1.call-update
  265.5 181.0 %reduce-scatter.5.cloned.1.call-done = f32[1,224,256]{2,1,0:T(8,128)} async-done(((f32[32,224,256]{2,1,0:T(8,128)}), f32[1,224,256]{2,1,0:T(8,128)}) %reduce-scatter.5.cloned.1.call-update) | async-done | bytes 229392 | tf_op jit(solution)/shard_map/reduce_scatter | solution.py:48
  446.5 3.5 collective-permute-start
  450.0 4.2 collective-permute-done
  454.2 1.0 bitcast_add_fusion
  455.2 4.9 %collective-permute-start.1 = (f32[256,224]{0,1:T(8,128)S(1)}, f32[256,224]{0,1:T(8,128)S(1)}, u32[]{:S(2)}, u32[]{:S(2)}) collective-permute-start(f32[256,224]{0,1:T(8,128)S(1)} %bitcast_add_fusion), channel_id=1, source_target_pairs={{0,128},{64,192},{128,0},{192,64},{1,129},{65,193},{129,1},{193,65... | collective-permute-start | bytes 688136 | tf_op jit(solution)/shard_map/ppermute | solution.py:29
  460.1 5.2 %collective-permute-done.1 = f32[256,224]{0,1:T(8,128)S(1)} collective-permute-done((f32[256,224]{0,1:T(8,128)S(1)}, f32[256,224]{0,1:T(8,128)S(1)}, u32[]{:S(2)}, u32[]{:S(2)}) %collective-permute-start.1) | collective-permute-done | bytes 229408 | tf_op jit(solution)/shard_map/ppermute | solution.py:29
  465.3 0.0 copy-done.4
  465.3 0.0 copy-done.5
  465.3 0.1 fusion.1
  465.4 0.0 copy-start.2
  465.4 0.0 copy-start.3
  465.4 0.0 copy-start.1
  465.4 5.7 %fusion = bf16[8192,224]{0,1:T(8,128)(2,1)} fusion(bf16[8192,256]{1,0:T(8,128)(2,1)} %bitcast.34, f32[256,224]{0,1:T(8,128)S(1)} %get-tuple-element.3, f32[256,224]{0,1:T(8,128)S(1)} %get-tuple-element.4), kind=kOutput, calls=%fused_computation.2 | convolution fusion | flops 941645824 | bytes 8323072 | tf_op jit(solution)/shard_map/dot_general | solution.py:57
  471.2 0.0 copy-done.2
  471.2 0.0 copy-done.3
  471.2 0.0 copy-done.1
Async XLA Ops:
  7.2 185.7 %copy-start = (bf16[192,8192]{1,0:T(8,128)(2,1)S(1)}, bf16[192,8192]{1,0:T(8,128)(2,1)}, u32[]{:S(2)}) copy-start(bf16[192,8192]{1,0:T(8,128)(2,1)} %param.5) | copy-start | bytes 9437188
  7.2 160.4 %all-gather.5.cloned.1.call-start = ((), (), s32[]{:S(2)}) async-start(), calls=%async_computation.4 | async-start | bytes 2162688 | tf_op jit(solution)/shard_map/all_gather | solution.py:19
  7.9 180.3 %all-gather.7.cloned.1.call-start = ((), (), s32[]{:S(2)}) async-start(), calls=%async_computation.5 | async-start | bytes 6291456 | tf_op jit(solution)/shard_map/all_gather | solution.py:20
  167.7 97.8 %reduce-scatter.3.cloned.1.call-start = ((), (), s32[]{:S(2)}) async-start(), calls=%async_computation.2 | async-start | bytes 22020096 | tf_op jit(solution)/shard_map/reduce_scatter | solution.py:46
  233.7 231.6 %copy-start.4 = (f32[256,224]{0,1:T(8,128)S(1)}, f32[256,224]{0,1:T(8,128)}, u32[]{:S(2)}) copy-start(f32[256,224]{0,1:T(8,128)} %param.9) | copy-start | bytes 688132
  233.8 231.6 %copy-start.5 = (f32[256,224]{0,1:T(8,128)S(1)}, f32[256,224]{0,1:T(8,128)}, u32[]{:S(2)}) copy-start(f32[256,224]{0,1:T(8,128)} %param.8) | copy-start | bytes 688132
  233.8 212.7 %reduce-scatter.5.cloned.1.call-start = ((), (), s32[]{:S(2)}) async-start(), calls=%async_computation.3 | async-start | bytes 7569408 | tf_op jit(solution)/shard_map/reduce_scatter | solution.py:48
  446.5 7.7 %collective-permute-start = (f32[256,224]{0,1:T(8,128)}, f32[256,224]{0,1:T(8,128)S(1)}, u32[]{:S(2)}, u32[]{:S(2)}) collective-permute-start(f32[256,224]{0,1:T(8,128)} %bitcast.38), channel_id=1, source_target_pairs={{0,64},{64,0},{128,192},{192,128},{1,65},{65,1},{129,193},{193,129... | collective-permute-start | bytes 688136 | tf_op jit(solution)/shard_map/ppermute | solution.py:29
  455.2 10.1 %collective-permute-start.1 = (f32[256,224]{0,1:T(8,128)S(1)}, f32[256,224]{0,1:T(8,128)S(1)}, u32[]{:S(2)}, u32[]{:S(2)}) collective-permute-start(f32[256,224]{0,1:T(8,128)S(1)} %bitcast_add_fusion), channel_id=1, source_target_pairs={{0,128},{64,192},{128,0},{192,64},{1,129},{65,193},{129,1},{193,65... | collective-permute-start | bytes 688136 | tf_op jit(solution)/shard_map/ppermute | solution.py:29
  465.4 5.8 %copy-start.2 = (f32[256,224]{0,1:T(8,128)}, f32[256,224]{0,1:T(8,128)S(1)}, u32[]{:S(2)}) copy-start(f32[256,224]{0,1:T(8,128)S(1)} %get-tuple-element.3) | copy-start | bytes 688132
  465.4 5.8 %copy-start.3 = (f32[256,224]{0,1:T(8,128)}, f32[256,224]{0,1:T(8,128)S(1)}, u32[]{:S(2)}) copy-start(f32[256,224]{0,1:T(8,128)S(1)} %get-tuple-element.4) | copy-start | bytes 688132
  465.4 5.8 %copy-start.1 = (bf16[192,8192]{1,0:T(8,128)(2,1)S(1)}, bf16[192,8192]{1,0:T(8,128)(2,1)}, u32[]{:S(2)}) copy-start(bf16[192,8192]{1,0:T(8,128)(2,1)} %param.5) | copy-start | bytes 9437188
Sparse Core Ops, SparseCore 0:
  9.8 157.8 all-gather.4
  169.4 18.7 all-gather.6
  233.9 31.5 reduce-scatter.2
  267.9 178.5 reduce-scatter.4

commit v4 on v3

--- a/solution.py
+++ b/solution.py
@@ -7,18 +7,36 @@
 STEP = 100
 
 SUB = ("y", "zl", "x", "core")
-CHIPS = ("y", "zl", "x")
 
 
 def adam_moments(grad, moment1, moment2):
     return (0.9 * moment1 + 0.1 * grad, 0.999 * moment2 + 0.001 * grad * grad)
 
 
+def pair_swap(x, name):
+    return lax.ppermute(x, name, [(0, 1), (1, 0)])
+
+
+def swap_stack(x, name):
+    other = pair_swap(x, name)
+    first = lax.axis_index(name) == 0
+    return jnp.stack([jnp.where(first, x, other), jnp.where(first, other, x)])
+
+
+def pair_sum_scatter(terms, name):
+    i = lax.axis_index(name)
+    mine = lax.dynamic_index_in_dim(terms, i, 0, keepdims=False)
+    theirs = lax.dynamic_index_in_dim(terms, 1 - i, 0, keepdims=False)
+    return mine + pair_swap(theirs, name)
+
+
 def gather_projector(projector, sizes):
     rows, width = projector.shape
-    full = lax.all_gather(projector, CHIPS, axis=0, tiled=False)
-    full = lax.all_gather(full, "core", axis=0, tiled=False)
-    full = jnp.transpose(full, (1, 0, 2, 3))
+    full = lax.all_gather(projector, "y", axis=0, tiled=False)
+    full = lax.all_gather(full, "x", axis=0, tiled=False)
+    full = swap_stack(full, "zl")
+    full = swap_stack(full, "core")
+    full = jnp.transpose(full, (3, 1, 2, 0, 4, 5))
     return full.reshape(-1, width)
 
 
@@ -33,19 +51,21 @@
 
 def body(activations, cotangent, projector, moment1, moment2):
     sizes = {n: lax.axis_size(n) for n in SUB}
-    chips = sizes["y"] * sizes["zl"] * sizes["x"]
     proj_full = gather_projector(projector, sizes)
     low = jnp.dot(activations, proj_full, preferred_element_type=jnp.float32).astype(jnp.bfloat16)
     terms = lax.dot_general(
         cotangent, low, (((0,), (0,)), ((), ())), preferred_element_type=jnp.float32
     )
     ff, rank = terms.shape
-    cols = ff // (chips * sizes["core"])
-    terms = terms.reshape(chips, sizes["core"], cols, rank)
-    terms = jnp.transpose(terms, (1, 0, 2, 3)).reshape(sizes["core"], -1, rank)
-    terms = lax.psum_scatter(terms, "core", scatter_dimension=0, tiled=True)
-    terms = terms.reshape(chips, cols, rank)
-    terms = lax.psum_scatter(terms, CHIPS, scatter_dimension=0, tiled=True)
+    cols = ff // (sizes["y"] * sizes["zl"] * sizes["x"] * sizes["core"])
+    terms = terms.reshape(sizes["y"], sizes["zl"], sizes["x"], sizes["core"], cols, rank)
+    terms = jnp.transpose(terms, (3, 2, 1, 0, 4, 5)).reshape(sizes["core"], -1, rank)
+    terms = pair_sum_scatter(terms, "core")
+    terms = terms.reshape(sizes["x"], -1, rank)
+    terms = lax.psum_scatter(terms, "x", scatter_dimension=0, tiled=True)
+    terms = pair_sum_scatter(terms.reshape(sizes["zl"], -1, rank), "zl")
+    terms = terms.reshape(sizes["y"], -1, rank)
+    terms = lax.psum_scatter(terms, "y", scatter_dimension=0, tiled=True)
     group_grad = terms.reshape(cols, rank).T
     grad = all_sum_rep(group_grad)
     moment1_new, moment2_new = adam_moments(grad, moment1, moment2)

time: 487 us -> 324 us (0.67); the launches traced: 478 us -> 323 us
  waiting for transfers between devices: 403 us -> 207 us
  other arithmetic: 1.04 us -> 18.3 us
  blocking collectives: 0 us -> 14.7 us
  local copies, waits for them, and re-layouts: 31.9 us -> 38.2 us
    all_gather x2 -> x1, waiting for transfers between devices: 180 us -> 27 us  [gather_projector(): full = lax.all_gather(full, 'x', axis=0, tiled=False)]
    reduce_scatter x2, waiting for transfers between devices: 213 us -> 102 us  [the longest x1 75.5 us: body(): terms = lax.psum_scatter(terms, 'x', scatter_dimension=0, tiled=True)]
    ppermute x0 -> x4, waiting for transfers between devices: none -> 58.9 us  [pair_swap(): return lax.ppermute(x, name, [(0, 1), (1, 0)])]
    all_gather x0 -> x1, blocking collectives: none -> 14.7 us  [gather_projector(): full = lax.all_gather(projector, 'y', axis=0, tiled=False)]
    add x0 -> x2, other arithmetic: none -> 11.3 us  [pair_sum_scatter(): return mine + pair_swap(theirs, name)]
    ppermute x2, waiting for transfers between devices: 9.45 us -> 18.2 us  [all_sum_rep(): x = x + lax.ppermute(x, 'rep', [(i, i ^ step) for i in range(size)])]
    squeeze x0 -> x2, local copies, waits for them, and re-layouts: none -> 7.73 us  [pair_sum_scatter(): theirs = lax.dynamic_index_in_dim(terms, 1 - i, 0, keepdims=False)]
    another operation x0 -> x3, other arithmetic: none -> 5.63 us  [swap_stack(): return jnp.stack([jnp.where(first, x, other), jnp.where(first, other, x)])]
  transfers between devices with their start and end apart: 6 -> 9, of which waited for: 6 -> 9; matrix products, arithmetic and copies ran while one was open for 0% -> 0% of each run, Pallas kernels for 0% -> 0%
where the time goes in v4:
time: 324 us; the launch traced here: 323 us
  waiting for transfers between devices  207 us (64%)
  local copies, waits for them, and re-layouts  38.2 us (12%)
  matrix products  19.5 us (6%)
  other arithmetic  18.3 us (6%)
  blocking collectives  14.7 us (5%)
  between operations  13.9 us (4%)
  starting transfers between devices  11.8 us (4%)
    reduce_scatter x1, waiting for transfers between devices, body(): terms = lax.psum_scatter(terms, 'x', scatter_dimension=0, tiled=True)  75.5 us
    ppermute x4, waiting for transfers between devices, pair_swap(): return lax.ppermute(x, name, [(0, 1), (1, 0)])  58.9 us
    all_gather x1, waiting for transfers between devices, gather_projector(): full = lax.all_gather(full, 'x', axis=0, tiled=False)  27 us
    reduce_scatter x1, waiting for transfers between devices, body(): terms = lax.psum_scatter(terms, 'y', scatter_dimension=0, tiled=True)  26.9 us
    ppermute x2, waiting for transfers between devices, all_sum_rep(): x = x + lax.ppermute(x, 'rep', [(i, i ^ step) for i in range(size)])  18.2 us
    dot_general x1, local copies, waits for them, and re-layouts, body(): lax.dot_general(cotangent, low, (((0,), (0,)), ((), ())), preferred_eleme...  15.1 us
    all_gather x1, blocking collectives, gather_projector(): full = lax.all_gather(projector, 'y', axis=0, tiled=False)  14.7 us
    dot_general x1, matrix products, body(): lax.dot_general(cotangent, low, (((0,), (0,)), ((), ())), preferred_eleme...  13.7 us
  transfers between devices with their start and end apart: 9, of which 9 were waited for; matrix products, arithmetic and copies ran while one was open for 0% of the time, Pallas kernels for 0%

profile of v4, /device:TPU:2, one launch (start us, length us, event | category | flops | bytes accessed | tf_op | source)
XLA Modules:
  0.0 322.9 jit_solution(16812247509207439601)
XLA Ops:
  7.2 0.0 copy-start
  7.2 0.0 all-gather.4.cloned.1.call-start
  7.2 14.7 %all-gather = bf16[512,256]{1,0:T(8,128)(2,1)} all-gather(bf16[128,256]{1,0:T(8,128)(2,1)} %param.7), channel_id=2, replica_groups=mesh['rep'=4,'y'=4,'zl'=2,'x'=4,'core'=2] {'y'}, dimensions={0}, use_global_device_ids=true | all-gather | bytes 327680 | tf_op jit(solution)/shard_map/all_gather | solution.py:35
  21.9 0.0 all-gather.4.cloned.1.call-update
  22.0 0.0 reduce-scatter.3.cloned.1.call-start
  22.0 27.0 %all-gather.4.cloned.1.call-done = bf16[16,128,256]{2,1,0:T(8,128)(2,1)} async-done(((bf16[4,128,256]{2,1,0:T(8,128)(2,1)}), bf16[16,128,256]{2,1,0:T(8,128)(2,1)}) %all-gather.4.cloned.1.call-update) | async-done | bytes 1048592 | tf_op jit(solution)/shard_map/all_gather | solution.py:36
  49.0 1.6 collective-permute-start
  50.6 22.1 %collective-permute-done = bf16[4,4,128,256]{3,2,1,0:T(8,128)(2,1)} collective-permute-done((bf16[4,4,128,256]{3,2,1,0:T(8,128)(2,1)}, bf16[4,4,128,256]{3,2,1,0:T(8,128)(2,1)}, u32[]{:S(2)}, u32[]{:S(2)}) %collective-permute-start) | collective-permute-done | bytes 1048608 | tf_op jit(solution)/shard_map/ppermute | solution.py:17
  72.6 1.7 select_bitcast_fusion.3
  74.3 0.0 copy-start.2
  74.3 0.0 copy-start.3
  74.3 1.0 copy-done.2
  75.3 1.5 pad_maximum_fusion
  76.8 0.0 copy-done.3
  76.8 0.0 collective-permute-start.1
  76.8 4.5 %collective-permute-done.1 = bf16[2,4,4,128,256]{4,3,2,1,0:T(8,128)(2,1)} collective-permute-done((bf16[2,4,4,128,256]{4,3,2,1,0:T(8,128)(2,1)}, bf16[2,4,4,128,256]{4,3,2,1,0:T(8,128)(2,1)}, u32[]{:S(2)}, u32[]{:S(2)}) %collective-permute-start.1) | collective-permute-done | bytes 2097184 | tf_op jit(solution)/shard_map/ppermute | solution.py:17
  81.3 2.4 select_bitcast_fusion.1
  83.7 0.4 maximum_bitcast_fusion
  84.1 2.2 copy.15
  86.3 0.0 copy-done
  86.3 13.7 %convolution_bitcast_fusion = f32[14336,256]{0,1:T(8,128)} fusion(bf16[192,14336]{1,0:T(8,128)(2,1)} %param.6, bf16[192,8192]{1,0:T(8,128)(2,1)S(1)} %copy-done, bf16[8192,256]{1,0:T(8,128)(2,1)} %bitcast.50), kind=kOutput, calls=%fused_computation | convolution fusion | flops 2214641664 | bytes 27525120 | tf_op jit(solution)/shard_map/dot_general | solution.py:56
  100.1 15.1 %copy.16 = f32[14336,256]{1,0:T(8,128)} copy(f32[14336,256]{0,1:T(8,128)} %convolution_bitcast_fusion) | data formatting | bytes 29360128 | tf_op jit(solution)/shard_map/dot_general | solution.py:56
  115.2 12.1 %copy.17 = f32[2,4,2,4,224,256]{5,4,3,2,1,0:T(8,128)} copy(f32[2,4,2,4,224,256]{5,4,0,1,2,3:T(8,128)} %bitcast.49) | data formatting | bytes 29360128 | tf_op jit(solution)/shard_map/transpose | solution.py:62
  127.4 6.5 %dynamic-slice_bitcast_fusion = f32[7168,256]{1,0:T(8,128)} fusion(f32[2,7168,256]{2,1,0:T(8,128)} %bitcast.47, s32[]{:T(128)S(6)} %select_n.45), kind=kLoop, calls=%fused_computation.3 | loop fusion | bytes 14680068 | tf_op jit(solution)/shard_map/jit(dynamic_index_in_dim)/squeeze | solution.py:29
  133.8 0.1 collective-permute-start.2
  134.0 11.9 %collective-permute-done.2 = f32[7168,256]{1,0:T(8,128)} collective-permute-done((f32[7168,256]{1,0:T(8,128)}, f32[7168,256]{1,0:T(8,128)}, u32[]{:S(2)}, u32[]{:S(2)}) %collective-permute-start.2) | collective-permute-done | bytes 7340064 | tf_op jit(solution)/shard_map/ppermute | solution.py:17
  145.8 9.1 %bitcast_add_fusion = f32[7168,256]{1,0:T(8,128)} fusion(f32[7168,256]{1,0:T(8,128)} %collective-permute-done.2, f32[2,7168,256]{2,1,0:T(8,128)} %bitcast.48, s32[]{:T(128)S(6)} %select_n.44), kind=kLoop, calls=%fused_computation.2 | loop fusion | flops 1835008 | bytes 22020100 | tf_op jit(solution)/shard_map/add | solution.py:30
  154.9 0.0 reduce-scatter.3.cloned.1.call-update
  154.9 0.0 copy-start.6
  154.9 0.0 copy-start.7
  154.9 0.0 reduce-scatter.5.cloned.1.call-start
  155.0 75.5 %reduce-scatter.3.cloned.1.call-done = f32[1,1792,256]{2,1,0:T(8,128)} async-done(((f32[4,1792,256]{2,1,0:T(8,128)}), f32[1,1792,256]{2,1,0:T(8,128)}) %reduce-scatter.3.cloned.1.call-update) | async-done | bytes 1835024 | tf_op jit(solution)/shard_map/reduce_scatter | solution.py:65
  230.5 1.2 dynamic-slice_bitcast_fusion.1
  231.8 1.6 collective-permute-start.3
  233.4 20.5 %collective-permute-done.3 = f32[896,256]{1,0:T(8,128)S(1)} collective-permute-done((f32[896,256]{1,0:T(8,128)S(1)}, f32[896,256]{1,0:T(8,128)S(1)}, u32[]{:S(2)}, u32[]{:S(2)}) %collective-permute-start.3) | collective-permute-done | bytes 917536 | tf_op jit(solution)/shard_map/ppermute | solution.py:17
  253.9 2.2 bitcast_add_fusion.1
  256.1 0.0 reduce-scatter.5.cloned.1.call-update
  256.1 26.9 %reduce-scatter.5.cloned.1.call-done = f32[1,224,256]{2,1,0:T(8,128)} async-done(((f32[4,224,256]{2,1,0:T(8,128)}), f32[1,224,256]{2,1,0:T(8,128)}) %reduce-scatter.5.cloned.1.call-update) | async-done | bytes 229392 | tf_op jit(solution)/shard_map/reduce_scatter | solution.py:68
  283.0 2.5 collective-permute-start.4
  285.5 9.6 %collective-permute-done.4 = f32[256,224]{0,1:T(8,128)S(1)} collective-permute-done((f32[256,224]{0,1:T(8,128)}, f32[256,224]{0,1:T(8,128)S(1)}, u32[]{:S(2)}, u32[]{:S(2)}) %collective-permute-start.4) | collective-permute-done | bytes 229408 | tf_op jit(solution)/shard_map/ppermute | solution.py:47
  295.1 1.0 bitcast_add_fusion.2
  296.1 5.8 %collective-permute-start.5 = (f32[256,224]{0,1:T(8,128)S(1)}, f32[256,224]{0,1:T(8,128)S(1)}, u32[]{:S(2)}, u32[]{:S(2)}) collective-permute-start(f32[256,224]{0,1:T(8,128)S(1)} %bitcast_add_fusion.2), channel_id=1, source_target_pairs={{0,128},{64,192},{128,0},{192,64},{1,129},{65,193},{129,1},{193,65... | collective-permute-start | bytes 688136 | tf_op jit(solution)/shard_map/ppermute | solution.py:47
  301.9 8.6 %collective-permute-done.5 = f32[256,224]{0,1:T(8,128)S(1)} collective-permute-done((f32[256,224]{0,1:T(8,128)S(1)}, f32[256,224]{0,1:T(8,128)S(1)}, u32[]{:S(2)}, u32[]{:S(2)}) %collective-permute-start.5) | collective-permute-done | bytes 229408 | tf_op jit(solution)/shard_map/ppermute | solution.py:47
  310.5 0.0 copy-done.6
  310.5 0.0 copy-done.7
  310.5 0.1 fusion
  310.6 0.0 copy-start.4
  310.6 0.0 copy-start.5
  310.6 0.0 copy-start.1
  310.6 5.7 %convolution_convert_fusion = bf16[8192,224]{0,1:T(8,128)(2,1)} fusion(bf16[8192,256]{1,0:T(8,128)(2,1)} %bitcast.51, f32[256,224]{0,1:T(8,128)S(1)} %get-tuple-element.7, f32[256,224]{0,1:T(8,128)S(1)} %get-tuple-element.8), kind=kOutput, calls=%fused_computation.1 | convolution fusion | flops 941645824 | bytes 8323072 | tf_op jit(solution)/shard_map/dot_general | solution.py:77
  316.4 0.0 copy-done.4
  316.4 0.0 copy-done.5
  316.4 0.0 copy-done.1
Async XLA Ops:
  7.2 79.2 %copy-start = (bf16[192,8192]{1,0:T(8,128)(2,1)S(1)}, bf16[192,8192]{1,0:T(8,128)(2,1)}, u32[]{:S(2)}) copy-start(bf16[192,8192]{1,0:T(8,128)(2,1)} %param.5) | copy-start | bytes 9437188
  7.2 41.8 %all-gather.4.cloned.1.call-start = ((), (), s32[]{:S(2)}) async-start(), calls=%async_computation.4 | async-start | bytes 1310720 | tf_op jit(solution)/shard_map/all_gather | solution.py:36
  22.0 208.6 %reduce-scatter.3.cloned.1.call-start = ((), (), s32[]{:S(2)}) async-start(), calls=%async_computation.2 | async-start | bytes 9175040 | tf_op jit(solution)/shard_map/reduce_scatter | solution.py:65
  49.0 23.6 %collective-permute-start = (bf16[4,4,128,256]{3,2,1,0:T(8,128)(2,1)}, bf16[4,4,128,256]{3,2,1,0:T(8,128)(2,1)}, u32[]{:S(2)}, u32[]{:S(2)}) collective-permute-start(bf16[4,4,128,256]{3,2,1,0:T(8,128)(2,1)} %bitcast.56), channel_id=1, source_target_pairs={{0,8},{8,0},{1,9},{9,1},{2,10},{10,2},{3,11},{11,3},{4,12},{12,4},... | collective-permute-start | bytes 3145736 | tf_op jit(solution)/shard_map/ppermute | solution.py:17
  74.3 1.0 copy-start.2
  74.3 2.5 copy-start.3
  76.8 4.5 %collective-permute-start.1 = (bf16[2,4,4,128,256]{4,3,2,1,0:T(8,128)(2,1)}, bf16[2,4,4,128,256]{4,3,2,1,0:T(8,128)(2,1)}, u32[]{:S(2)}, u32[]{:S(2)}) collective-permute-start(bf16[2,4,4,128,256]{4,3,2,1,0:T(8,128)(2,1)} %pad_maximum_fusion), channel_id=1, source_target_pairs={{0,1},{1,0},{2,3},{3,2},{4,5},{5,4},{6,7},{7,6},{8,9},{9,8},{10,11... | collective-permute-start | bytes 6291464 | tf_op jit(solution)/shard_map/ppermute | solution.py:17
  133.8 12.0 %collective-permute-start.2 = (f32[7168,256]{1,0:T(8,128)}, f32[7168,256]{1,0:T(8,128)}, u32[]{:S(2)}, u32[]{:S(2)}) collective-permute-start(f32[7168,256]{1,0:T(8,128)} %dynamic-slice_bitcast_fusion), channel_id=1, source_target_pairs={{0,1},{1,0},{2,3},{3,2},{4,5},{5,4},{6,7},{7,6},{8,9},{9,8},{10,11... | collective-permute-start | bytes 22020104 | tf_op jit(solution)/shard_map/ppermute | solution.py:17
  154.9 155.6 %copy-start.6 = (f32[256,224]{0,1:T(8,128)S(1)}, f32[256,224]{0,1:T(8,128)}, u32[]{:S(2)}) copy-start(f32[256,224]{0,1:T(8,128)} %param.9) | copy-start | bytes 688132
  154.9 155.6 %copy-start.7 = (f32[256,224]{0,1:T(8,128)S(1)}, f32[256,224]{0,1:T(8,128)}, u32[]{:S(2)}) copy-start(f32[256,224]{0,1:T(8,128)} %param.8) | copy-start | bytes 688132
  154.9 128.0 %reduce-scatter.5.cloned.1.call-start = ((), (), s32[]{:S(2)}) async-start(), calls=%async_computation.3 | async-start | bytes 1146880 | tf_op jit(solution)/shard_map/reduce_scatter | solution.py:68
  231.8 22.1 %collective-permute-start.3 = (f32[896,256]{1,0:T(8,128)S(1)}, f32[896,256]{1,0:T(8,128)S(1)}, u32[]{:S(2)}, u32[]{:S(2)}) collective-permute-start(f32[896,256]{1,0:T(8,128)S(1)} %dynamic-slice_bitcast_fusion.1), channel_id=1, source_target_pairs={{0,8},{8,0},{1,9},{9,1},{2,10},{10,2},{3,11},{11,3},{4,12},{12,4},... | collective-permute-start | bytes 2752520 | tf_op jit(solution)/shard_map/ppermute | solution.py:17
  283.0 12.1 %collective-permute-start.4 = (f32[256,224]{0,1:T(8,128)}, f32[256,224]{0,1:T(8,128)S(1)}, u32[]{:S(2)}, u32[]{:S(2)}) collective-permute-start(f32[256,224]{0,1:T(8,128)} %bitcast.59), channel_id=1, source_target_pairs={{0,64},{64,0},{128,192},{192,128},{1,65},{65,1},{129,193},{193,129... | collective-permute-start | bytes 688136 | tf_op jit(solution)/shard_map/ppermute | solution.py:47
  296.1 14.5 %collective-permute-start.5 = (f32[256,224]{0,1:T(8,128)S(1)}, f32[256,224]{0,1:T(8,128)S(1)}, u32[]{:S(2)}, u32[]{:S(2)}) collective-permute-start(f32[256,224]{0,1:T(8,128)S(1)} %bitcast_add_fusion.2), channel_id=1, source_target_pairs={{0,128},{64,192},{128,0},{192,64},{1,129},{65,193},{129,1},{193,65... | collective-permute-start | bytes 688136 | tf_op jit(solution)/shard_map/ppermute | solution.py:47
  310.6 5.8 %copy-start.4 = (f32[256,224]{0,1:T(8,128)}, f32[256,224]{0,1:T(8,128)S(1)}, u32[]{:S(2)}) copy-start(f32[256,224]{0,1:T(8,128)S(1)} %get-tuple-element.7) | copy-start | bytes 688132
  310.6 5.8 %copy-start.5 = (f32[256,224]{0,1:T(8,128)}, f32[256,224]{0,1:T(8,128)S(1)}, u32[]{:S(2)}) copy-start(f32[256,224]{0,1:T(8,128)S(1)} %get-tuple-element.8) | copy-start | bytes 688132
  310.6 5.8 %copy-start.1 = (bf16[192,8192]{1,0:T(8,128)(2,1)S(1)}, bf16[192,8192]{1,0:T(8,128)(2,1)}, u32[]{:S(2)}) copy-start(bf16[192,8192]{1,0:T(8,128)(2,1)} %param.5) | copy-start | bytes 9437188
Sparse Core Ops, SparseCore 0:
  22.1 26.8 all-gather.3
  155.0 75.4 reduce-scatter.2
  256.2 26.6 reduce-scatter.4

commit v5 on v4

--- a/solution.py
+++ b/solution.py
@@ -49,13 +49,7 @@
     return x
 
 
-def body(activations, cotangent, projector, moment1, moment2):
-    sizes = {n: lax.axis_size(n) for n in SUB}
-    proj_full = gather_projector(projector, sizes)
-    low = jnp.dot(activations, proj_full, preferred_element_type=jnp.float32).astype(jnp.bfloat16)
-    terms = lax.dot_general(
-        cotangent, low, (((0,), (0,)), ((), ())), preferred_element_type=jnp.float32
-    )
+def reduce_terms(terms, sizes):
     ff, rank = terms.shape
     cols = ff // (sizes["y"] * sizes["zl"] * sizes["x"] * sizes["core"])
     terms = terms.reshape(sizes["y"], sizes["zl"], sizes["x"], sizes["core"], cols, rank)
@@ -66,8 +60,26 @@
     terms = pair_sum_scatter(terms.reshape(sizes["zl"], -1, rank), "zl")
     terms = terms.reshape(sizes["y"], -1, rank)
     terms = lax.psum_scatter(terms, "y", scatter_dimension=0, tiled=True)
-    group_grad = terms.reshape(cols, rank).T
-    grad = all_sum_rep(group_grad)
+    return terms.reshape(cols, rank)
+
+
+def body(activations, cotangent, projector, moment1, moment2):
+    sizes = {n: lax.axis_size(n) for n in SUB}
+    proj_full = gather_projector(projector, sizes)
+    low = jnp.dot(activations, proj_full, preferred_element_type=jnp.float32).astype(jnp.bfloat16)
+    rank = low.shape[1]
+    chunks = 2
+    width = rank // chunks
+    parts = []
+    for k in range(chunks):
+        terms = lax.dot_general(
+            cotangent,
+            low[:, k * width : (k + 1) * width],
+            (((0,), (0,)), ((), ())),
+            preferred_element_type=jnp.float32,
+        )
+        parts.append(all_sum_rep(reduce_terms(terms, sizes)))
+    grad = jnp.concatenate(parts, axis=1).T
     moment1_new, moment2_new = adam_moments(grad, moment1, moment2)
     first_fix = 1.0 - 0.9**STEP
     second_fix = 1.0 - 0.999**STEP

time: 324 us -> 305 us (0.941)
  waiting for transfers between devices: 207 us -> 176 us
  starting transfers between devices: 11.8 us -> 26.4 us
    reduce_scatter x2 -> x4, waiting for transfers between devices: 102 us -> 85.9 us  [the longest x2 49.7 us: reduce_terms(): terms = lax.psum_scatter(terms, 'x', scatter_dimension=0, tiled=True)]
    ppermute x2 -> x4, waiting for transfers between devices: 18.2 us -> 2.76 us  [all_sum_rep(): x = x + lax.ppermute(x, 'rep', [(i, i ^ step) for i in range(size)])]
    ppermute x2 -> x4, starting transfers between devices: 8.37 us -> 20.9 us  [all_sum_rep(): x = x + lax.ppermute(x, 'rep', [(i, i ^ step) for i in range(size)])]
    unnamed x16 -> x24, local copies, waits for them, and re-layouts: 1.02 us -> 5.73 us
    transpose x1 -> x2, local copies, waits for them, and re-layouts: 12.1 us -> 7.43 us  [reduce_terms(): jnp.transpose(terms, (3, 2, 1, 0, 4, 5)).reshape(sizes['core'], -1, rank)]
    squeeze x2 -> x4, local copies, waits for them, and re-layouts: 7.73 us -> 4.6 us  [pair_sum_scatter(): theirs = lax.dynamic_index_in_dim(terms, 1 - i, 0, keepdims=False)]
    dot_general x1 -> x2, local copies, waits for them, and re-layouts: 15.1 us -> 17.3 us  [body(): lax.dot_general(cotangent, low[:, k * width:(k + 1) * width], (((0,), (0,...]
    dot_general x1 -> x3, matrix products: 13.7 us -> 11.8 us  [the longest x2 10.7 us: body(): lax.dot_general(cotangent, low[:, k * width:(k + 1) * width], (((0,), (0,...]
  transfers between devices with their start and end apart: 9 -> 15, of which waited for: 9 -> 12; matrix products, arithmetic and copies ran while one was open for 0% -> 10% of each run, Pallas kernels for 0% -> 0%
where the time goes in v5:
time: 305 us; the launch traced here: 304 us
  waiting for transfers between devices  176 us (58%)
  local copies, waits for them, and re-layouts  35.6 us (12%)
  starting transfers between devices  26.4 us (9%)
  other arithmetic  19.1 us (6%)
  matrix products  17.5 us (6%)
  blocking collectives  14.7 us (5%)
  between operations  14 us (5%)
    ppermute x6, waiting for transfers between devices, pair_swap(): return lax.ppermute(x, name, [(0, 1), (1, 0)])  60.7 us
    reduce_scatter x2, waiting for transfers between devices, reduce_terms(): terms = lax.psum_scatter(terms, 'x', scatter_dimension=0, tiled=True)  49.7 us
    reduce_scatter x2, waiting for transfers between devices, reduce_terms(): terms = lax.psum_scatter(terms, 'y', scatter_dimension=0, tiled=True)  36.2 us
    all_gather x1, waiting for transfers between devices, gather_projector(): full = lax.all_gather(full, 'x', axis=0, tiled=False)  27 us
    ppermute x4, starting transfers between devices, all_sum_rep(): x = x + lax.ppermute(x, 'rep', [(i, i ^ step) for i in range(size)])  20.9 us
    dot_general x2, local copies, waits for them, and re-layouts, body(): lax.dot_general(cotangent, low[:, k * width:(k + 1) * width], (((0,), (0,...  17.3 us
    all_gather x1, blocking collectives, gather_projector(): full = lax.all_gather(projector, 'y', axis=0, tiled=False)  14.7 us
    add x4, other arithmetic, pair_sum_scatter(): return mine + pair_swap(theirs, name)  11.2 us
  transfers between devices with their start and end apart: 15, of which 12 were waited for; matrix products, arithmetic and copies ran while one was open for 10% of the time, Pallas kernels for 0%

profile of v5, /device:TPU:2, one launch (start us, length us, event | category | flops | bytes accessed | tf_op | source)
XLA Modules:
  0.0 303.7 jit_solution(644665768367671421)
XLA Ops:
  7.2 0.0 copy-start
  7.2 0.0 all-gather.4.cloned.1.call-start
  7.2 14.7 %all-gather = bf16[512,256]{1,0:T(8,128)(2,1)} all-gather(bf16[128,256]{1,0:T(8,128)(2,1)} %param.7), channel_id=2, replica_groups=mesh['rep'=4,'y'=4,'zl'=2,'x'=4,'core'=2] {'y'}, dimensions={0}, use_global_device_ids=true | all-gather | bytes 327680 | tf_op jit(solution)/shard_map/all_gather | solution.py:35
  21.9 0.0 all-gather.4.cloned.1.call-update
  22.0 0.0 reduce-scatter.9.cloned.1.call-start
  22.0 27.0 %all-gather.4.cloned.1.call-done = bf16[16,128,256]{2,1,0:T(8,128)(2,1)} async-done(((bf16[4,128,256]{2,1,0:T(8,128)(2,1)}), bf16[16,128,256]{2,1,0:T(8,128)(2,1)}) %all-gather.4.cloned.1.call-update) | async-done | bytes 1048592 | tf_op jit(solution)/shard_map/all_gather | solution.py:36
  49.0 1.6 collective-permute-start
  50.6 22.1 %collective-permute-done = bf16[4,4,128,256]{3,2,1,0:T(8,128)(2,1)} collective-permute-done((bf16[4,4,128,256]{3,2,1,0:T(8,128)(2,1)}, bf16[4,4,128,256]{3,2,1,0:T(8,128)(2,1)}, u32[]{:S(2)}, u32[]{:S(2)}) %collective-permute-start) | collective-permute-done | bytes 1048608 | tf_op jit(solution)/shard_map/ppermute | solution.py:17
  72.6 1.7 select_bitcast_fusion.3
  74.3 0.9 copy-done.4
  75.3 1.5 pad_maximum_fusion
  76.8 4.5 %collective-permute-done.1 = bf16[2,4,4,128,256]{4,3,2,1,0:T(8,128)(2,1)} collective-permute-done((bf16[2,4,4,128,256]{4,3,2,1,0:T(8,128)(2,1)}, bf16[2,4,4,128,256]{4,3,2,1,0:T(8,128)(2,1)}, u32[]{:S(2)}, u32[]{:S(2)}) %collective-permute-start.1) | collective-permute-done | bytes 2097184 | tf_op jit(solution)/shard_map/ppermute | solution.py:17
  81.3 2.4 select_bitcast_fusion.1
  83.7 0.4 maximum_bitcast_fusion
  84.1 0.5 copy.19
  84.6 0.0 slice-start
  84.6 1.1 fusion
  85.7 1.0 copy-done.2
  86.7 1.6 slice-done
  88.3 0.4 slice-done.1
  88.7 4.1 %convolution_bitcast_fusion = f32[14336,128]{0,1:T(8,128)} fusion(bf16[192,14336]{1,0:T(8,128)(2,1)S(1)} %bitcast.67, bf16[192,256]{1,0:T(8,128)(2,1)S(1)} %fusion), kind=kOutput, calls=%fused_computation | convolution fusion | flops 704643072 | bytes 12894208 | tf_op jit(solution)/shard_map/dot_general | solution.py:75
  92.8 8.6 %copy.22 = f32[14336,128]{1,0:T(8,128)} copy(f32[14336,128]{0,1:T(8,128)} %convolution_bitcast_fusion) | data formatting | bytes 14680064 | tf_op jit(solution)/shard_map/dot_general | solution.py:75
  101.4 3.7 %copy.23 = f32[2,4,2,4,224,128]{5,4,3,2,1,0:T(8,128)S(1)} copy(f32[2,4,2,4,224,128]{5,4,0,1,2,3:T(8,128)} %bitcast.68) | data formatting | bytes 14680064 | tf_op jit(solution)/shard_map/transpose | solution.py:56
  105.1 2.3 dynamic-slice_bitcast_fusion
  107.4 1.8 copy-done.3
  109.1 0.2 collective-permute-start.6
  109.3 6.6 %collective-permute-done.6 = f32[7168,128]{1,0:T(8,128)} collective-permute-done((f32[7168,128]{1,0:T(8,128)}, f32[7168,128]{1,0:T(8,128)}, u32[]{:S(2)}, u32[]{:S(2)}) %collective-permute-start.6) | collective-permute-done | bytes 3670048 | tf_op jit(solution)/shard_map/ppermute | solution.py:17
  115.9 5.4 %bitcast_add_fusion = f32[7168,128]{1,0:T(8,128)} fusion(f32[7168,128]{1,0:T(8,128)} %collective-permute-done.6, f32[2,7168,128]{2,1,0:T(8,128)} %bitcast.71, s32[]{:T(128)S(6)} %select_n.48), kind=kLoop, calls=%fused_computation.4 | loop fusion | flops 917504 | bytes 11010052 | tf_op jit(solution)/shard_map/add | solution.py:30
  121.3 0.0 reduce-scatter.9.cloned.1.call-update
  121.3 0.0 reduce-scatter.5.cloned.1.call-start
  121.3 6.6 %convolution_bitcast_fusion.1 = f32[14336,128]{0,1:T(8,128)} fusion(bf16[192,14336]{1,0:T(8,128)(2,1)} %param.6, bf16[192,256]{1,0:T(8,128)(2,1)S(1)} %fusion), kind=kOutput, calls=%fused_computation.1 | convolution fusion | flops 704643072 | bytes 12894208 | tf_op jit(solution)/shard_map/dot_general | solution.py:75
  128.0 8.7 %copy.20 = f32[14336,128]{1,0:T(8,128)} copy(f32[14336,128]{0,1:T(8,128)} %convolution_bitcast_fusion.1) | data formatting | bytes 14680064 | tf_op jit(solution)/shard_map/dot_general | solution.py:75
  136.7 3.7 %copy.21 = f32[2,4,2,4,224,128]{5,4,3,2,1,0:T(8,128)S(1)} copy(f32[2,4,2,4,224,128]{5,4,0,1,2,3:T(8,128)} %bitcast.69) | data formatting | bytes 14680064 | tf_op jit(solution)/shard_map/transpose | solution.py:56
  140.4 0.2 dynamic-slice_bitcast_fusion.1
  140.6 0.3 collective-permute-start.2
  140.9 6.2 %collective-permute-done.2 = f32[7168,128]{1,0:T(8,128)S(1)} collective-permute-done((f32[7168,128]{1,0:T(8,128)S(1)}, f32[7168,128]{1,0:T(8,128)S(1)}, u32[]{:S(2)}, u32[]{:S(2)}) %collective-permute-start.2) | collective-permute-done | bytes 3670048 | tf_op jit(solution)/shard_map/ppermute | solution.py:17
  147.1 2.1 bitcast_add_fusion.1
  149.3 0.0 reduce-scatter.5.cloned.1.call-update
  149.3 0.0 reduce-scatter.11.cloned.1.call-start
  149.4 17.5 %reduce-scatter.9.cloned.1.call-done = f32[1,1792,128]{2,1,0:T(8,128)} async-done(((f32[4,1792,128]{2,1,0:T(8,128)}), f32[1,1792,128]{2,1,0:T(8,128)}) %reduce-scatter.9.cloned.1.call-update) | async-done | bytes 917520 | tf_op jit(solution)/shard_map/reduce_scatter | solution.py:59
  166.9 1.0 dynamic-slice_bitcast_fusion.2
  167.9 1.6 collective-permute-start.7
  169.6 10.7 %collective-permute-done.7 = f32[896,128]{1,0:T(8,128)S(1)} collective-permute-done((f32[896,128]{1,0:T(8,128)S(1)}, f32[896,128]{1,0:T(8,128)S(1)}, u32[]{:S(2)}, u32[]{:S(2)}) %collective-permute-start.7) | collective-permute-done | bytes 458784 | tf_op jit(solution)/shard_map/ppermute | solution.py:17
  180.2 1.8 bitcast_add_fusion.2
  182.1 0.0 reduce-scatter.11.cloned.1.call-update
  182.1 0.0 reduce-scatter.7.cloned.1.call-start
  182.2 32.2 %reduce-scatter.5.cloned.1.call-done = f32[1,1792,128]{2,1,0:T(8,128)} async-done(((f32[4,1792,128]{2,1,0:T(8,128)}), f32[1,1792,128]{2,1,0:T(8,128)}) %reduce-scatter.5.cloned.1.call-update) | async-done | bytes 917520 | tf_op jit(solution)/shard_map/reduce_scatter | solution.py:59
  214.3 1.0 dynamic-slice_bitcast_fusion.3
  215.4 1.6 collective-permute-start.3
  217.0 10.7 %collective-permute-done.3 = f32[896,128]{1,0:T(8,128)S(1)} collective-permute-done((f32[896,128]{1,0:T(8,128)S(1)}, f32[896,128]{1,0:T(8,128)S(1)}, u32[]{:S(2)}, u32[]{:S(2)}) %collective-permute-start.3) | collective-permute-done | bytes 458784 | tf_op jit(solution)/shard_map/ppermute | solution.py:17
  227.7 1.8 bitcast_add_fusion.3
  229.5 0.0 reduce-scatter.7.cloned.1.call-update
  229.6 12.7 %reduce-scatter.11.cloned.1.call-done = f32[1,224,128]{2,1,0:T(8,128)} async-done(((f32[4,224,128]{2,1,0:T(8,128)}), f32[1,224,128]{2,1,0:T(8,128)}) %reduce-scatter.11.cloned.1.call-update) | async-done | bytes 114704 | tf_op jit(solution)/shard_map/reduce_scatter | solution.py:62
  242.3 2.6 collective-permute-start.8
  244.8 23.5 %reduce-scatter.7.cloned.1.call-done = f32[1,224,128]{2,1,0:T(8,128)} async-done(((f32[4,224,128]{2,1,0:T(8,128)}), f32[1,224,128]{2,1,0:T(8,128)}) %reduce-scatter.7.cloned.1.call-update) | async-done | bytes 114704 | tf_op jit(solution)/shard_map/reduce_scatter | solution.py:62
  268.4 2.5 collective-permute-start.4
  270.9 0.9 bitcast_add_fusion.4
  271.8 4.0 %collective-permute-start.9 = (f32[224,128]{1,0:T(8,128)S(1)}, f32[224,128]{1,0:T(8,128)S(1)}, u32[]{:S(2)}, u32[]{:S(2)}) collective-permute-start(f32[224,128]{1,0:T(8,128)S(1)} %bitcast_add_fusion.4), channel_id=1, source_target_pairs={{0,128},{64,192},{128,0},{192,64},{1,129},{65,193},{129,1},{193,65... | collective-permute-start | bytes 344072 | tf_op jit(solution)/shard_map/ppermute | solution.py:47
  275.9 0.9 bitcast_add_fusion.5
  276.8 11.7 %collective-permute-start.5 = (f32[224,128]{1,0:T(8,128)S(1)}, f32[224,128]{1,0:T(8,128)S(1)}, u32[]{:S(2)}, u32[]{:S(2)}) collective-permute-start(f32[224,128]{1,0:T(8,128)S(1)} %bitcast_add_fusion.5), channel_id=1, source_target_pairs={{0,128},{64,192},{128,0},{192,64},{1,129},{65,193},{129,1},{193,65... | collective-permute-start | bytes 344072 | tf_op jit(solution)/shard_map/ppermute | solution.py:47
  288.5 2.8 collective-permute-done.5
  291.3 0.1 fusion.1
  291.4 0.0 copy-start.6
  291.4 5.7 %convolution_convert_fusion = bf16[8192,224]{0,1:T(8,128)(2,1)} fusion(bf16[8192,256]{1,0:T(8,128)(2,1)} %bitcast.65, f32[256,224]{0,1:T(8,128)S(1)} %get-tuple-element.7, f32[256,224]{0,1:T(8,128)S(1)} %get-tuple-element.8), kind=kOutput, calls=%fused_computation.2 | convolution fusion | flops 941645824 | bytes 8323072 | tf_op jit(solution)/shard_map/dot_general | solution.py:89
  (23 shorter events, 0.1 us)
Async XLA Ops:
  7.2 77.5 %copy-start = (bf16[192,8192]{1,0:T(8,128)(2,1)S(1)}, bf16[192,8192]{1,0:T(8,128)(2,1)}, u32[]{:S(2)}) copy-start(bf16[192,8192]{1,0:T(8,128)(2,1)} %param.5) | copy-start | bytes 9437188
  7.2 41.8 %all-gather.4.cloned.1.call-start = ((), (), s32[]{:S(2)}) async-start(), calls=%async_computation.8 | async-start | bytes 1310720 | tf_op jit(solution)/shard_map/all_gather | solution.py:36
  22.0 144.9 %reduce-scatter.9.cloned.1.call-start = ((), (), s32[]{:S(2)}) async-start(), calls=%async_computation.6 | async-start | bytes 4587520 | tf_op jit(solution)/shard_map/reduce_scatter | solution.py:59
  49.0 23.6 %collective-permute-start = (bf16[4,4,128,256]{3,2,1,0:T(8,128)(2,1)}, bf16[4,4,128,256]{3,2,1,0:T(8,128)(2,1)}, u32[]{:S(2)}, u32[]{:S(2)}) collective-permute-start(bf16[4,4,128,256]{3,2,1,0:T(8,128)(2,1)} %bitcast.78), channel_id=1, source_target_pairs={{0,8},{8,0},{1,9},{9,1},{2,10},{10,2},{3,11},{11,3},{4,12},{12,4},... | collective-permute-start | bytes 3145736 | tf_op jit(solution)/shard_map/ppermute | solution.py:17
  74.3 1.0 copy-start.4
  74.3 2.5 copy-start.5
  76.8 4.5 %collective-permute-start.1 = (bf16[2,4,4,128,256]{4,3,2,1,0:T(8,128)(2,1)}, bf16[2,4,4,128,256]{4,3,2,1,0:T(8,128)(2,1)}, u32[]{:S(2)}, u32[]{:S(2)}) collective-permute-start(bf16[2,4,4,128,256]{4,3,2,1,0:T(8,128)(2,1)} %pad_maximum_fusion), channel_id=1, source_target_pairs={{0,1},{1,0},{2,3},{3,2},{4,5},{5,4},{6,7},{7,6},{8,9},{9,8},{10,11... | collective-permute-start | bytes 6291464 | tf_op jit(solution)/shard_map/ppermute | solution.py:17
  84.6 2.1 copy-start.2
  84.6 3.7 %slice-start = ((s8[5505024]{0:T(1024)(128)(4,1)}), s8[4194304]{0:T(1024)(128)(4,1)S(1)}, s32[]{:S(2)}) async-start(s8[5505024]{0:T(1024)(128)(4,1)} %bitcast.66), calls=%async_computation.9 | async-start | bytes 8388608
  84.6 4.1 %slice-start.1 = ((s8[5505024]{0:T(1024)(128)(4,1)}), s8[1310720]{0:T(1024)(128)(4,1)S(1)}, s32[]{:S(2)}) async-start(s8[5505024]{0:T(1024)(128)(4,1)} %bitcast.66), calls=%async_computation.10 | async-start | bytes 2621440
  105.1 4.0 %copy-start.3 = (f32[2,4,2,4,224,128]{5,4,3,2,1,0:T(8,128)}, f32[2,4,2,4,224,128]{5,4,3,2,1,0:T(8,128)S(1)}, u32[]{:S(2)}) copy-start(f32[2,4,2,4,224,128]{5,4,3,2,1,0:T(8,128)S(1)} %copy.23) | copy-start | bytes 22020100
  109.1 6.8 %collective-permute-start.6 = (f32[7168,128]{1,0:T(8,128)}, f32[7168,128]{1,0:T(8,128)}, u32[]{:S(2)}, u32[]{:S(2)}) collective-permute-start(f32[7168,128]{1,0:T(8,128)} %dynamic-slice_bitcast_fusion), channel_id=1, source_target_pairs={{0,1},{1,0},{2,3},{3,2},{4,5},{5,4},{6,7},{7,6},{8,9},{9,8},{10,11... | collective-permute-start | bytes 11010056 | tf_op jit(solution)/shard_map/ppermute | solution.py:17
  121.3 93.0 %reduce-scatter.5.cloned.1.call-start = ((), (), s32[]{:S(2)}) async-start(), calls=%async_computation.4 | async-start | bytes 4587520 | tf_op jit(solution)/shard_map/reduce_scatter | solution.py:59
  140.6 6.5 %collective-permute-start.2 = (f32[7168,128]{1,0:T(8,128)S(1)}, f32[7168,128]{1,0:T(8,128)S(1)}, u32[]{:S(2)}, u32[]{:S(2)}) collective-permute-start(f32[7168,128]{1,0:T(8,128)S(1)} %dynamic-slice_bitcast_fusion.1), channel_id=1, source_target_pairs={{0,1},{1,0},{2,3},{3,2},{4,5},{5,4},{6,7},{7,6},{8,9},{9,8},{10,11... | collective-permute-start | bytes 11010056 | tf_op jit(solution)/shard_map/ppermute | solution.py:17
  149.3 142.0 %copy-start.8 = (f32[256,224]{0,1:T(8,128)S(1)}, f32[256,224]{0,1:T(8,128)}, u32[]{:S(2)}) copy-start(f32[256,224]{0,1:T(8,128)} %param.9) | copy-start | bytes 688132
  149.3 142.0 %copy-start.9 = (f32[256,224]{0,1:T(8,128)S(1)}, f32[256,224]{0,1:T(8,128)}, u32[]{:S(2)}) copy-start(f32[256,224]{0,1:T(8,128)} %param.8) | copy-start | bytes 688132
  149.3 92.9 %reduce-scatter.11.cloned.1.call-start = ((), (), s32[]{:S(2)}) async-start(), calls=%async_computation.7 | async-start | bytes 573440 | tf_op jit(solution)/shard_map/reduce_scatter | solution.py:62
  167.9 12.3 %collective-permute-start.7 = (f32[896,128]{1,0:T(8,128)S(1)}, f32[896,128]{1,0:T(8,128)S(1)}, u32[]{:S(2)}, u32[]{:S(2)}) collective-permute-start(f32[896,128]{1,0:T(8,128)S(1)} %dynamic-slice_bitcast_fusion.2), channel_id=1, source_target_pairs={{0,8},{8,0},{1,9},{9,1},{2,10},{10,2},{3,11},{11,3},{4,12},{12,4},... | collective-permute-start | bytes 1376264 | tf_op jit(solution)/shard_map/ppermute | solution.py:17
  182.1 86.3 %reduce-scatter.7.cloned.1.call-start = ((), (), s32[]{:S(2)}) async-start(), calls=%async_computation.5 | async-start | bytes 573440 | tf_op jit(solution)/shard_map/reduce_scatter | solution.py:62
  215.4 12.3 %collective-permute-start.3 = (f32[896,128]{1,0:T(8,128)S(1)}, f32[896,128]{1,0:T(8,128)S(1)}, u32[]{:S(2)}, u32[]{:S(2)}) collective-permute-start(f32[896,128]{1,0:T(8,128)S(1)} %dynamic-slice_bitcast_fusion.3), channel_id=1, source_target_pairs={{0,8},{8,0},{1,9},{9,1},{2,10},{10,2},{3,11},{11,3},{4,12},{12,4},... | collective-permute-start | bytes 1376264 | tf_op jit(solution)/shard_map/ppermute | solution.py:17
  242.3 28.6 %collective-permute-start.8 = (f32[224,128]{1,0:T(8,128)}, f32[224,128]{1,0:T(8,128)S(1)}, u32[]{:S(2)}, u32[]{:S(2)}) collective-permute-start(f32[224,128]{1,0:T(8,128)} %bitcast.85), channel_id=1, source_target_pairs={{0,64},{64,0},{128,192},{192,128},{1,65},{65,1},{129,193},{193,129... | collective-permute-start | bytes 344072 | tf_op jit(solution)/shard_map/ppermute | solution.py:47
  268.4 7.5 %collective-permute-start.4 = (f32[224,128]{1,0:T(8,128)}, f32[224,128]{1,0:T(8,128)S(1)}, u32[]{:S(2)}, u32[]{:S(2)}) collective-permute-start(f32[224,128]{1,0:T(8,128)} %bitcast.86), channel_id=1, source_target_pairs={{0,64},{64,0},{128,192},{192,128},{1,65},{65,1},{129,193},{193,129... | collective-permute-start | bytes 344072 | tf_op jit(solution)/shard_map/ppermute | solution.py:47
  271.8 16.7 %collective-permute-start.9 = (f32[224,128]{1,0:T(8,128)S(1)}, f32[224,128]{1,0:T(8,128)S(1)}, u32[]{:S(2)}, u32[]{:S(2)}) collective-permute-start(f32[224,128]{1,0:T(8,128)S(1)} %bitcast_add_fusion.4), channel_id=1, source_target_pairs={{0,128},{64,192},{128,0},{192,64},{1,129},{65,193},{129,1},{193,65... | collective-permute-start | bytes 344072 | tf_op jit(solution)/shard_map/ppermute | solution.py:47
  276.8 14.5 %collective-permute-start.5 = (f32[224,128]{1,0:T(8,128)S(1)}, f32[224,128]{1,0:T(8,128)S(1)}, u32[]{:S(2)}, u32[]{:S(2)}) collective-permute-start(f32[224,128]{1,0:T(8,128)S(1)} %bitcast_add_fusion.5), channel_id=1, source_target_pairs={{0,128},{64,192},{128,0},{192,64},{1,129},{65,193},{129,1},{193,65... | collective-permute-start | bytes 344072 | tf_op jit(solution)/shard_map/ppermute | solution.py:47
  291.4 5.8 %copy-start.6 = (f32[256,224]{0,1:T(8,128)}, f32[256,224]{0,1:T(8,128)S(1)}, u32[]{:S(2)}) copy-start(f32[256,224]{0,1:T(8,128)S(1)} %get-tuple-element.7) | copy-start | bytes 688132
  291.4 5.8 %copy-start.7 = (f32[256,224]{0,1:T(8,128)}, f32[256,224]{0,1:T(8,128)S(1)}, u32[]{:S(2)}) copy-start(f32[256,224]{0,1:T(8,128)S(1)} %get-tuple-element.8) | copy-start | bytes 688132
  291.4 5.8 %copy-start.1 = (bf16[192,8192]{1,0:T(8,128)(2,1)S(1)}, bf16[192,8192]{1,0:T(8,128)(2,1)}, u32[]{:S(2)}) copy-start(bf16[192,8192]{1,0:T(8,128)(2,1)} %param.5) | copy-start | bytes 9437188
Sparse Core Ops, SparseCore 0:
  22.1 26.8 all-gather.3
  121.4 45.4 reduce-scatter.8
  169.4 44.8 reduce-scatter.4
  217.3 24.9 reduce-scatter.10
  244.7 23.6 reduce-scatter.6

commit v6 on v5

--- a/solution.py
+++ b/solution.py
@@ -13,29 +13,31 @@
     return (0.9 * moment1 + 0.1 * grad, 0.999 * moment2 + 0.001 * grad * grad)
 
 
-def pair_swap(x, name):
-    return lax.ppermute(x, name, [(0, 1), (1, 0)])
+def pair_swap(x, name, bit=1):
+    size = lax.axis_size(name)
+    return lax.ppermute(x, name, [(i, i ^ bit) for i in range(size)])
 
 
-def swap_stack(x, name):
-    other = pair_swap(x, name)
-    first = lax.axis_index(name) == 0
+def swap_stack(x, name, bit=1):
+    other = pair_swap(x, name, bit)
+    first = (lax.axis_index(name) // bit) % 2 == 0
     return jnp.stack([jnp.where(first, x, other), jnp.where(first, other, x)])
 
 
-def pair_sum_scatter(terms, name):
-    i = lax.axis_index(name)
+def pair_sum_scatter(terms, name, bit=1):
+    i = (lax.axis_index(name) // bit) % 2
     mine = lax.dynamic_index_in_dim(terms, i, 0, keepdims=False)
     theirs = lax.dynamic_index_in_dim(terms, 1 - i, 0, keepdims=False)
-    return mine + pair_swap(theirs, name)
+    return mine + pair_swap(theirs, name, bit)
 
 
 def gather_projector(projector, sizes):
     rows, width = projector.shape
-    full = lax.all_gather(projector, "y", axis=0, tiled=False)
-    full = lax.all_gather(full, "x", axis=0, tiled=False)
+    full = swap_stack(swap_stack(projector, "y", 1), "y", 2)
+    full = swap_stack(swap_stack(full, "x", 1), "x", 2)
     full = swap_stack(full, "zl")
     full = swap_stack(full, "core")
+    full = full.reshape(sizes["core"], sizes["zl"], sizes["x"], sizes["y"], rows, width)
     full = jnp.transpose(full, (3, 1, 2, 0, 4, 5))
     return full.reshape(-1, width)
 
@@ -58,8 +60,8 @@
     terms = terms.reshape(sizes["x"], -1, rank)
     terms = lax.psum_scatter(terms, "x", scatter_dimension=0, tiled=True)
     terms = pair_sum_scatter(terms.reshape(sizes["zl"], -1, rank), "zl")
-    terms = terms.reshape(sizes["y"], -1, rank)
-    terms = lax.psum_scatter(terms, "y", scatter_dimension=0, tiled=True)
+    terms = pair_sum_scatter(terms.reshape(2, -1, rank), "y", 2)
+    terms = pair_sum_scatter(terms.reshape(2, -1, rank), "y", 1)
     return terms.reshape(cols, rank)
 
 

time: 305 us -> 276 us (0.905); the launches traced: 304 us -> 271 us
  waiting for transfers between devices: 176 us -> 144 us
  blocking collectives: 14.7 us -> 0 us
  starting transfers between devices: 26.4 us -> 39.2 us
    reduce_scatter x2 -> x0, waiting for transfers between devices: 36.2 us -> none  [reduce_terms(): terms = lax.psum_scatter(terms, 'y', scatter_dimension=0, tiled=True)]
    all_gather x1 -> x0, waiting for transfers between devices: 27 us -> none  [gather_projector(): full = lax.all_gather(full, 'x', axis=0, tiled=False)]
    ppermute x6 -> x14, starting transfers between devices: 5.28 us -> 23.4 us  [pair_swap(): return lax.ppermute(x, name, [(i, i ^ bit) for i in range(size)])]
    all_gather x1 -> x0, blocking collectives: 14.7 us -> none  [gather_projector(): full = lax.all_gather(projector, 'y', axis=0, tiled=False)]
    reduce_scatter x2, waiting for transfers between devices: 49.7 us -> 63.4 us  [reduce_terms(): terms = lax.psum_scatter(terms, 'x', scatter_dimension=0, tiled=True)]
    ppermute x6 -> x14, waiting for transfers between devices: 60.7 us -> 69.8 us  [pair_swap(): return lax.ppermute(x, name, [(i, i ^ bit) for i in range(size)])]
    ppermute x4, waiting for transfers between devices: 2.76 us -> 10.7 us  [all_sum_rep(): x = x + lax.ppermute(x, 'rep', [(i, i ^ step) for i in range(size)])]
    ppermute x4, starting transfers between devices: 20.9 us -> 15.7 us  [all_sum_rep(): x = x + lax.ppermute(x, 'rep', [(i, i ^ step) for i in range(size)])]
  transfers between devices with their start and end apart: 15 -> 20, of which waited for: 12 -> 16; matrix products, arithmetic and copies ran while one was open for 10% -> 10% of each run, Pallas kernels for 0% -> 0%
where the time goes in v6:
time: 276 us; the launch traced here: 271 us
  waiting for transfers between devices  144 us (52%)
  starting transfers between devices  39.2 us (14%)
  local copies, waits for them, and re-layouts  37.6 us (14%)
  other arithmetic  20.9 us (8%)
  matrix products  15.1 us (5%)
  between operations  14.4 us (5%)
    ppermute x14, waiting for transfers between devices, pair_swap(): return lax.ppermute(x, name, [(i, i ^ bit) for i in range(size)])  69.8 us
    reduce_scatter x2, waiting for transfers between devices, reduce_terms(): terms = lax.psum_scatter(terms, 'x', scatter_dimension=0, tiled=True)  63.4 us
    ppermute x14, starting transfers between devices, pair_swap(): return lax.ppermute(x, name, [(i, i ^ bit) for i in range(size)])  23.4 us
    dot_general x2, local copies, waits for them, and re-layouts, body(): lax.dot_general(cotangent, low[:, k * width:(k + 1) * width], (((0,), (0,...  17.2 us
    ppermute x4, starting transfers between devices, all_sum_rep(): x = x + lax.ppermute(x, 'rep', [(i, i ^ step) for i in range(size)])  15.7 us
    ppermute x4, waiting for transfers between devices, all_sum_rep(): x = x + lax.ppermute(x, 'rep', [(i, i ^ step) for i in range(size)])  10.7 us
    dot_general x2, matrix products, body(): lax.dot_general(cotangent, low[:, k * width:(k + 1) * width], (((0,), (0,...  10.6 us
    add x8, other arithmetic, pair_sum_scatter(): return mine + pair_swap(theirs, name, bit)  9.79 us
  transfers between devices with their start and end apart: 20, of which 16 were waited for; matrix products, arithmetic and copies ran while one was open for 10% of the time, Pallas kernels for 0%

profile of v6, /device:TPU:2, one launch (start us, length us, event | category | flops | bytes accessed | tf_op | source)
XLA Modules:
  0.0 271.1 jit_solution(16203954995116605943)
XLA Ops:
  7.2 1.7 collective-permute-start
  8.9 2.9 %collective-permute-done = bf16[128,256]{1,0:T(8,128)(2,1)S(1)} collective-permute-done((bf16[128,256]{1,0:T(8,128)(2,1)}, bf16[128,256]{1,0:T(8,128)(2,1)S(1)}, u32[]{:S(2)}, u32[]{:S(2)}) %collective-permute-start) | collective-permute-done | bytes 65568 | tf_op jit(solution)/shard_map/ppermute | solution.py:18
  11.8 0.9 select_bitcast_fusion.9
  12.7 3.3 %collective-permute-start.1 = (bf16[2,128,256]{2,1,0:T(8,128)(2,1)S(1)}, bf16[2,128,256]{2,1,0:T(8,128)(2,1)S(1)}, u32[]{:S(2)}, u32[]{:S(2)}) collective-permute-start(bf16[2,128,256]{2,1,0:T(8,128)(2,1)S(1)} %pad_maximum_fusion.5), channel_id=1, source_target_pairs={{0,32},{16,48},{32,0},{48,16},{1,33},{17,49},{33,1},{49,17},{2,34}... | collective-permute-start | bytes 393224 | tf_op jit(solution)/shard_map/ppermute | solution.py:18
  15.9 3.3 %collective-permute-done.1 = bf16[2,128,256]{2,1,0:T(8,128)(2,1)S(1)} collective-permute-done((bf16[2,128,256]{2,1,0:T(8,128)(2,1)S(1)}, bf16[2,128,256]{2,1,0:T(8,128)(2,1)S(1)}, u32[]{:S(2)}, u32[]{:S(2)}) %collective-permute-start.1) | collective-permute-done | bytes 131104 | tf_op jit(solution)/shard_map/ppermute | solution.py:18
  19.3 0.6 copy-done.10
  19.9 2.3 collective-permute-start.2
  22.3 4.5 %collective-permute-done.2 = bf16[2,2,128,256]{3,2,1,0:T(8,128)(2,1)} collective-permute-done((bf16[2,2,128,256]{3,2,1,0:T(8,128)(2,1)S(1)}, bf16[2,2,128,256]{3,2,1,0:T(8,128)(2,1)}, u32[]{:S(2)}, u32[]{:S(2)}) %collective-permute-start.2) | collective-permute-done | bytes 262176 | tf_op jit(solution)/shard_map/ppermute | solution.py:18
  26.7 1.0 select_bitcast_fusion.5
  27.8 0.7 copy-done.9
  28.5 0.8 pad_maximum_fusion.3
  29.3 1.9 collective-permute-start.3
  31.2 9.9 %collective-permute-done.3 = bf16[2,2,2,128,256]{4,3,2,1,0:T(8,128)(2,1)} collective-permute-done((bf16[2,2,2,128,256]{4,3,2,1,0:T(8,128)(2,1)}, bf16[2,2,2,128,256]{4,3,2,1,0:T(8,128)(2,1)}, u32[]{:S(2)}, u32[]{:S(2)}) %collective-permute-start.3) | collective-permute-done | bytes 524320 | tf_op jit(solution)/shard_map/ppermute | solution.py:18
  41.1 1.2 select_bitcast_fusion.3
  42.3 0.8 copy-done.7
  43.1 1.1 pad_maximum_fusion.2
  44.2 1.9 collective-permute-start.4
  46.1 19.2 %collective-permute-done.4 = bf16[2,2,2,2,128,256]{5,4,3,2,1,0:T(8,128)(2,1)} collective-permute-done((bf16[2,2,2,2,128,256]{5,4,3,2,1,0:T(8,128)(2,1)}, bf16[2,2,2,2,128,256]{5,4,3,2,1,0:T(8,128)(2,1)}, u32[]{:S(2)}, u32[]{:S(2)}) %collective-permute-start.4) | collective-permute-done | bytes 1048608 | tf_op jit(solution)/shard_map/ppermute | solution.py:18
  65.3 1.7 select_bitcast_fusion.1
  66.9 1.0 copy-done.5
  67.9 1.5 pad_maximum_fusion.1
  69.4 4.5 %collective-permute-done.5 = bf16[2,2,2,2,2,128,256]{6,5,4,3,2,1,0:T(8,128)(2,1)} collective-permute-done((bf16[2,2,2,2,2,128,256]{6,5,4,3,2,1,0:T(8,128)(2,1)}, bf16[2,2,2,2,2,128,256]{6,5,4,3,2,1,0:T(8,128)(2,1)}, u32[]{:S(2)}, u32[]{:S(2)}) %collective-permute-start.5) | collective-permute-done | bytes 2097184 | tf_op jit(solution)/shard_map/ppermute | solution.py:18
  73.9 2.4 broadcast_select_fusion.1
  76.8 0.4 pad_maximum_fusion
  77.2 1.1 fusion
  78.3 1.0 copy-done.2
  79.3 1.6 slice-done
  80.9 0.4 slice-done.1
  81.3 4.0 %convolution_bitcast_fusion = f32[14336,128]{0,1:T(8,128)} fusion(bf16[192,14336]{1,0:T(8,128)(2,1)S(1)} %bitcast.93, bf16[192,256]{1,0:T(8,128)(2,1)S(1)} %fusion), kind=kOutput, calls=%fused_computation | convolution fusion | flops 704643072 | bytes 12894208 | tf_op jit(solution)/shard_map/dot_general | solution.py:77
  85.3 8.6 %copy.12 = f32[14336,128]{1,0:T(8,128)} copy(f32[14336,128]{0,1:T(8,128)} %convolution_bitcast_fusion) | data formatting | bytes 14680064 | tf_op jit(solution)/shard_map/dot_general | solution.py:77
  94.0 3.7 %copy.13 = f32[2,4,2,4,224,128]{5,4,3,2,1,0:T(8,128)S(1)} copy(f32[2,4,2,4,224,128]{5,4,0,1,2,3:T(8,128)} %bitcast.94) | data formatting | bytes 14680064 | tf_op jit(solution)/shard_map/transpose | solution.py:58
  97.7 2.3 dynamic-slice_bitcast_fusion
  99.9 1.7 copy-done.4
  101.8 6.6 %collective-permute-done.12 = f32[7168,128]{1,0:T(8,128)} collective-permute-done((f32[7168,128]{1,0:T(8,128)}, f32[7168,128]{1,0:T(8,128)}, u32[]{:S(2)}, u32[]{:S(2)}) %collective-permute-start.12) | collective-permute-done | bytes 3670048 | tf_op jit(solution)/shard_map/ppermute | solution.py:18
  108.4 5.4 %bitcast_add_fusion = f32[7168,128]{1,0:T(8,128)} fusion(f32[7168,128]{1,0:T(8,128)} %collective-permute-done.12, f32[2,7168,128]{2,1,0:T(8,128)} %bitcast.97, s32[]{:T(128)S(6)} %select_n.196), kind=kLoop, calls=%fused_computation.4 | loop fusion | flops 917504 | bytes 11010052 | tf_op jit(solution)/shard_map/add | solution.py:31
  113.9 6.6 %convolution_bitcast_fusion.1 = f32[14336,128]{0,1:T(8,128)} fusion(bf16[192,14336]{1,0:T(8,128)(2,1)} %param.6, bf16[192,256]{1,0:T(8,128)(2,1)S(1)} %fusion), kind=kOutput, calls=%fused_computation.1 | convolution fusion | flops 704643072 | bytes 12894208 | tf_op jit(solution)/shard_map/dot_general | solution.py:77
  120.5 8.6 %copy.10 = f32[14336,128]{1,0:T(8,128)} copy(f32[14336,128]{0,1:T(8,128)} %convolution_bitcast_fusion.1) | data formatting | bytes 14680064 | tf_op jit(solution)/shard_map/dot_general | solution.py:77
  129.1 3.7 %copy.11 = f32[2,4,2,4,224,128]{5,4,3,2,1,0:T(8,128)S(1)} copy(f32[2,4,2,4,224,128]{5,4,0,1,2,3:T(8,128)} %bitcast.95) | data formatting | bytes 14680064 | tf_op jit(solution)/shard_map/transpose | solution.py:58
  133.0 0.4 collective-permute-start.6
  133.5 6.2 %collective-permute-done.6 = f32[7168,128]{1,0:T(8,128)S(1)} collective-permute-done((f32[7168,128]{1,0:T(8,128)S(1)}, f32[7168,128]{1,0:T(8,128)S(1)}, u32[]{:S(2)}, u32[]{:S(2)}) %collective-permute-start.6) | collective-permute-done | bytes 3670048 | tf_op jit(solution)/shard_map/ppermute | solution.py:18
  139.7 2.2 bitcast_add_fusion.1
  141.9 18.7 %reduce-scatter.5.cloned.1.call-done = f32[1,1792,128]{2,1,0:T(8,128)} async-done(((f32[4,1792,128]{2,1,0:T(8,128)}), f32[1,1792,128]{2,1,0:T(8,128)}) %reduce-scatter.5.cloned.1.call-update) | async-done | bytes 917520 | tf_op jit(solution)/shard_map/reduce_scatter | solution.py:61
  160.6 1.0 dynamic-slice_bitcast_fusion.2
  161.7 1.6 collective-permute-start.13
  163.3 44.7 %reduce-scatter.3.cloned.1.call-done = f32[1,1792,128]{2,1,0:T(8,128)} async-done(((f32[4,1792,128]{2,1,0:T(8,128)}), f32[1,1792,128]{2,1,0:T(8,128)}) %reduce-scatter.3.cloned.1.call-update) | async-done | bytes 917520 | tf_op jit(solution)/shard_map/reduce_scatter | solution.py:61
  208.1 1.0 dynamic-slice_bitcast_fusion.3
  209.1 1.7 collective-permute-start.7
  210.8 1.1 bitcast_add_fusion.2
  211.9 3.1 %collective-permute-start.14 = (f32[448,128]{1,0:T(8,128)S(1)}, f32[448,128]{1,0:T(8,128)S(1)}, u32[]{:S(2)}, u32[]{:S(2)}) collective-permute-start(f32[448,128]{1,0:T(8,128)S(1)} %dynamic-slice_bitcast_fusion.4), channel_id=1, source_target_pairs={{0,32},{16,48},{32,0},{48,16},{1,33},{17,49},{33,1},{49,17},{2,34}... | collective-permute-start | bytes 688136 | tf_op jit(solution)/shard_map/ppermute | solution.py:18
  215.0 6.4 %collective-permute-done.7 = f32[896,128]{1,0:T(8,128)S(1)} collective-permute-done((f32[896,128]{1,0:T(8,128)S(1)}, f32[896,128]{1,0:T(8,128)S(1)}, u32[]{:S(2)}, u32[]{:S(2)}) %collective-permute-start.7) | collective-permute-done | bytes 458784 | tf_op jit(solution)/shard_map/ppermute | solution.py:18
  221.4 1.1 bitcast_add_fusion.3
  222.5 3.1 %collective-permute-start.8 = (f32[448,128]{1,0:T(8,128)S(1)}, f32[448,128]{1,0:T(8,128)S(1)}, u32[]{:S(2)}, u32[]{:S(2)}) collective-permute-start(f32[448,128]{1,0:T(8,128)S(1)} %dynamic-slice_bitcast_fusion.5), channel_id=1, source_target_pairs={{0,32},{16,48},{32,0},{48,16},{1,33},{17,49},{33,1},{49,17},{2,34}... | collective-permute-start | bytes 688136 | tf_op jit(solution)/shard_map/ppermute | solution.py:18
  225.7 0.7 collective-permute-start.15
  226.3 5.4 %collective-permute-done.8 = f32[448,128]{1,0:T(8,128)S(1)} collective-permute-done((f32[448,128]{1,0:T(8,128)S(1)}, f32[448,128]{1,0:T(8,128)S(1)}, u32[]{:S(2)}, u32[]{:S(2)}) %collective-permute-start.8) | collective-permute-done | bytes 229408 | tf_op jit(solution)/shard_map/ppermute | solution.py:18
  231.8 1.5 collective-permute-start.9
  233.4 0.9 collective-permute-done.15
  234.3 2.6 collective-permute-start.16
  237.0 2.4 collective-permute-start.10
  239.3 3.1 %collective-permute-done.16 = f32[224,128]{1,0:T(8,128)S(1)} collective-permute-done((f32[224,128]{1,0:T(8,128)S(1)}, f32[224,128]{1,0:T(8,128)S(1)}, u32[]{:S(2)}, u32[]{:S(2)}) %collective-permute-start.16) | collective-permute-done | bytes 114720 | tf_op jit(solution)/shard_map/ppermute | solution.py:49
  242.5 9.5 %collective-permute-start.17 = (f32[224,128]{1,0:T(8,128)S(1)}, f32[224,128]{1,0:T(8,128)S(1)}, u32[]{:S(2)}, u32[]{:S(2)}) collective-permute-start(f32[224,128]{1,0:T(8,128)S(1)} %add.149), channel_id=1, source_target_pairs={{0,128},{64,192},{128,0},{192,64},{1,129},{65,193},{129,1},{193,65... | collective-permute-start | bytes 344072 | tf_op jit(solution)/shard_map/ppermute | solution.py:49
  251.9 1.2 collective-permute-start.11
  253.2 4.9 %collective-permute-done.17 = f32[224,128]{1,0:T(8,128)S(1)} collective-permute-done((f32[224,128]{1,0:T(8,128)S(1)}, f32[224,128]{1,0:T(8,128)S(1)}, u32[]{:S(2)}, u32[]{:S(2)}) %collective-permute-start.17) | collective-permute-done | bytes 114720 | tf_op jit(solution)/shard_map/ppermute | solution.py:49
  258.1 2.6 collective-permute-done.11
  260.9 3.3 %convolution_convert_fusion = bf16[8192,224]{0,1:T(8,128)(2,1)} fusion(bf16[8192,256]{1,0:T(8,128)(2,1)S(1)} %bitcast.91, f32[256,224]{0,1:T(8,128)S(1)} %get-tuple-element.13, f32[256,224]{0,1:T(8,128)S(1)} %get-tuple-element.14), kind=kOutput, calls=%fused_computation.2 | convolution fusion | flops 941645824 | bytes 8323072 | tf_op jit(solution)/shard_map/dot_general | solution.py:91
  (56 shorter events, 1.4 us)
Async XLA Ops:
  7.2 70.1 %copy-start = (bf16[192,8192]{1,0:T(8,128)(2,1)S(1)}, bf16[192,8192]{1,0:T(8,128)(2,1)}, u32[]{:S(2)}) copy-start(bf16[192,8192]{1,0:T(8,128)(2,1)} %param.5) | copy-start | bytes 9437188
  7.2 153.4 %reduce-scatter.5.cloned.1.call-start = ((), (), s32[]{:S(2)}) async-start(), calls=%async_computation.3 | async-start | bytes 4587520 | tf_op jit(solution)/shard_map/reduce_scatter | solution.py:61
  7.2 4.6 %collective-permute-start = (bf16[128,256]{1,0:T(8,128)(2,1)}, bf16[128,256]{1,0:T(8,128)(2,1)S(1)}, u32[]{:S(2)}, u32[]{:S(2)}) collective-permute-start(bf16[128,256]{1,0:T(8,128)(2,1)} %param.7), channel_id=1, source_target_pairs={{0,16},{16,0},{32,48},{48,32},{1,17},{17,1},{33,49},{49,33},{2,18}... | collective-permute-start | bytes 196616 | tf_op jit(solution)/shard_map/ppermute | solution.py:18
  12.7 6.6 %collective-permute-start.1 = (bf16[2,128,256]{2,1,0:T(8,128)(2,1)S(1)}, bf16[2,128,256]{2,1,0:T(8,128)(2,1)S(1)}, u32[]{:S(2)}, u32[]{:S(2)}) collective-permute-start(bf16[2,128,256]{2,1,0:T(8,128)(2,1)S(1)} %pad_maximum_fusion.5), channel_id=1, source_target_pairs={{0,32},{16,48},{32,0},{48,16},{1,33},{17,49},{33,1},{49,17},{2,34}... | collective-permute-start | bytes 393224 | tf_op jit(solution)/shard_map/ppermute | solution.py:18
  19.3 0.7 copy-start.10
  19.9 6.8 %collective-permute-start.2 = (bf16[2,2,128,256]{3,2,1,0:T(8,128)(2,1)S(1)}, bf16[2,2,128,256]{3,2,1,0:T(8,128)(2,1)}, u32[]{:S(2)}, u32[]{:S(2)}) collective-permute-start(bf16[2,2,128,256]{3,2,1,0:T(8,128)(2,1)S(1)} %pad_maximum_fusion.4), channel_id=1, source_target_pairs={{0,2},{2,0},{4,6},{6,4},{1,3},{3,1},{5,7},{7,5},{8,10},{10,8},{12,... | collective-permute-start | bytes 786440 | tf_op jit(solution)/shard_map/ppermute | solution.py:18
  27.8 0.7 copy-start.9
  29.3 11.8 %collective-permute-start.3 = (bf16[2,2,2,128,256]{4,3,2,1,0:T(8,128)(2,1)}, bf16[2,2,2,128,256]{4,3,2,1,0:T(8,128)(2,1)}, u32[]{:S(2)}, u32[]{:S(2)}) collective-permute-start(bf16[2,2,2,128,256]{4,3,2,1,0:T(8,128)(2,1)} %pad_maximum_fusion.3), channel_id=1, source_target_pairs={{0,4},{2,6},{4,0},{6,2},{1,5},{3,7},{5,1},{7,3},{8,12},{10,14},{12... | collective-permute-start | bytes 1572872 | tf_op jit(solution)/shard_map/ppermute | solution.py:18
  42.3 0.8 copy-start.7
  42.3 1.9 copy-start.8
  44.2 21.1 %collective-permute-start.4 = (bf16[2,2,2,2,128,256]{5,4,3,2,1,0:T(8,128)(2,1)}, bf16[2,2,2,2,128,256]{5,4,3,2,1,0:T(8,128)(2,1)}, u32[]{:S(2)}, u32[]{:S(2)}) collective-permute-start(bf16[2,2,2,2,128,256]{5,4,3,2,1,0:T(8,128)(2,1)} %pad_maximum_fusion.2), channel_id=1, source_target_pairs={{0,8},{8,0},{1,9},{9,1},{2,10},{10,2},{3,11},{11,3},{4,12},{12,4},... | collective-permute-start | bytes 3145736 | tf_op jit(solution)/shard_map/ppermute | solution.py:18
  66.9 1.0 copy-start.5
  66.9 2.5 copy-start.6
  69.4 4.5 %collective-permute-start.5 = (bf16[2,2,2,2,2,128,256]{6,5,4,3,2,1,0:T(8,128)(2,1)}, bf16[2,2,2,2,2,128,256]{6,5,4,3,2,1,0:T(8,128)(2,1)}, u32[]{:S(2)}, u32[]{:S(2)}) collective-permute-start(bf16[2,2,2,2,2,128,256]{6,5,4,3,2,1,0:T(8,128)(2,1)} %pad_maximum_fusion.1), channel_id=1, source_target_pairs={{0,1},{1,0},{2,3},{3,2},{4,5},{5,4},{6,7},{7,6},{8,9},{9,8},{10,11... | collective-permute-start | bytes 6291464 | tf_op jit(solution)/shard_map/ppermute | solution.py:18
  77.2 2.1 copy-start.2
  77.2 3.7 %slice-start = ((s8[5505024]{0:T(1024)(128)(4,1)}), s8[4194304]{0:T(1024)(128)(4,1)S(1)}, s32[]{:S(2)}) async-start(s8[5505024]{0:T(1024)(128)(4,1)} %bitcast.92), calls=%async_computation.4 | async-start | bytes 8388608
  77.2 4.1 %slice-start.1 = ((s8[5505024]{0:T(1024)(128)(4,1)}), s8[1310720]{0:T(1024)(128)(4,1)S(1)}, s32[]{:S(2)}) async-start(s8[5505024]{0:T(1024)(128)(4,1)} %bitcast.92), calls=%async_computation.5 | async-start | bytes 2621440
  97.7 4.0 %copy-start.4 = (f32[2,4,2,4,224,128]{5,4,3,2,1,0:T(8,128)}, f32[2,4,2,4,224,128]{5,4,3,2,1,0:T(8,128)S(1)}, u32[]{:S(2)}) copy-start(f32[2,4,2,4,224,128]{5,4,3,2,1,0:T(8,128)S(1)} %copy.13) | copy-start | bytes 22020100
  101.7 6.8 %collective-permute-start.12 = (f32[7168,128]{1,0:T(8,128)}, f32[7168,128]{1,0:T(8,128)}, u32[]{:S(2)}, u32[]{:S(2)}) collective-permute-start(f32[7168,128]{1,0:T(8,128)} %dynamic-slice_bitcast_fusion), channel_id=1, source_target_pairs={{0,1},{1,0},{2,3},{3,2},{4,5},{5,4},{6,7},{7,6},{8,9},{9,8},{10,11... | collective-permute-start | bytes 11010056 | tf_op jit(solution)/shard_map/ppermute | solution.py:18
  113.8 94.2 %reduce-scatter.3.cloned.1.call-start = ((), (), s32[]{:S(2)}) async-start(), calls=%async_computation.2 | async-start | bytes 4587520 | tf_op jit(solution)/shard_map/reduce_scatter | solution.py:61
  133.0 6.7 %collective-permute-start.6 = (f32[7168,128]{1,0:T(8,128)S(1)}, f32[7168,128]{1,0:T(8,128)S(1)}, u32[]{:S(2)}, u32[]{:S(2)}) collective-permute-start(f32[7168,128]{1,0:T(8,128)S(1)} %dynamic-slice_bitcast_fusion.1), channel_id=1, source_target_pairs={{0,1},{1,0},{2,3},{3,2},{4,5},{5,4},{6,7},{7,6},{8,9},{9,8},{10,11... | collective-permute-start | bytes 11010056 | tf_op jit(solution)/shard_map/ppermute | solution.py:18
  161.7 49.1 %collective-permute-start.13 = (f32[896,128]{1,0:T(8,128)S(1)}, f32[896,128]{1,0:T(8,128)S(1)}, u32[]{:S(2)}, u32[]{:S(2)}) collective-permute-start(f32[896,128]{1,0:T(8,128)S(1)} %dynamic-slice_bitcast_fusion.2), channel_id=1, source_target_pairs={{0,8},{8,0},{1,9},{9,1},{2,10},{10,2},{3,11},{11,3},{4,12},{12,4},... | collective-permute-start | bytes 1376264 | tf_op jit(solution)/shard_map/ppermute | solution.py:18
  209.1 12.3 %collective-permute-start.7 = (f32[896,128]{1,0:T(8,128)S(1)}, f32[896,128]{1,0:T(8,128)S(1)}, u32[]{:S(2)}, u32[]{:S(2)}) collective-permute-start(f32[896,128]{1,0:T(8,128)S(1)} %dynamic-slice_bitcast_fusion.3), channel_id=1, source_target_pairs={{0,8},{8,0},{1,9},{9,1},{2,10},{10,2},{3,11},{11,3},{4,12},{12,4},... | collective-permute-start | bytes 1376264 | tf_op jit(solution)/shard_map/ppermute | solution.py:18
  210.8 50.0 %copy-start.13 = (f32[256,224]{0,1:T(8,128)S(1)}, f32[256,224]{0,1:T(8,128)}, u32[]{:S(2)}) copy-start(f32[256,224]{0,1:T(8,128)} %param.9) | copy-start | bytes 688132
  210.8 50.0 %copy-start.14 = (f32[256,224]{0,1:T(8,128)S(1)}, f32[256,224]{0,1:T(8,128)}, u32[]{:S(2)}) copy-start(f32[256,224]{0,1:T(8,128)} %param.8) | copy-start | bytes 688132
  211.9 49.0 %copy-start.3 = (bf16[2,2,4,4,128,256]{5,4,0,2,1,3:T(8,128)(2,1)S(1)}, bf16[2,2,4,4,128,256]{5,4,0,2,1,3:T(8,128)(2,1)}, u32[]{:S(2)}) copy-start(bf16[2,2,4,4,128,256]{5,4,0,2,1,3:T(8,128)(2,1)} %copy-done.2) | copy-start | bytes 12582916
  211.9 13.7 %collective-permute-start.14 = (f32[448,128]{1,0:T(8,128)S(1)}, f32[448,128]{1,0:T(8,128)S(1)}, u32[]{:S(2)}, u32[]{:S(2)}) collective-permute-start(f32[448,128]{1,0:T(8,128)S(1)} %dynamic-slice_bitcast_fusion.4), channel_id=1, source_target_pairs={{0,32},{16,48},{32,0},{48,16},{1,33},{17,49},{33,1},{49,17},{2,34}... | collective-permute-start | bytes 688136 | tf_op jit(solution)/shard_map/ppermute | solution.py:18
  222.5 9.3 %collective-permute-start.8 = (f32[448,128]{1,0:T(8,128)S(1)}, f32[448,128]{1,0:T(8,128)S(1)}, u32[]{:S(2)}, u32[]{:S(2)}) collective-permute-start(f32[448,128]{1,0:T(8,128)S(1)} %dynamic-slice_bitcast_fusion.5), channel_id=1, source_target_pairs={{0,32},{16,48},{32,0},{48,16},{1,33},{17,49},{33,1},{49,17},{2,34}... | collective-permute-start | bytes 688136 | tf_op jit(solution)/shard_map/ppermute | solution.py:18
  225.7 8.6 %collective-permute-start.15 = (f32[224,128]{1,0:T(8,128)S(1)}, f32[224,128]{1,0:T(8,128)S(1)}, u32[]{:S(2)}, u32[]{:S(2)}) collective-permute-start(f32[224,128]{1,0:T(8,128)S(1)} %dynamic-slice_bitcast_fusion.6), channel_id=1, source_target_pairs={{0,16},{16,0},{32,48},{48,32},{1,17},{17,1},{33,49},{49,33},{2,18}... | collective-permute-start | bytes 344072 | tf_op jit(solution)/shard_map/ppermute | solution.py:18
  231.8 5.1 %collective-permute-start.9 = (f32[224,128]{1,0:T(8,128)S(1)}, f32[224,128]{1,0:T(8,128)S(1)}, u32[]{:S(2)}, u32[]{:S(2)}) collective-permute-start(f32[224,128]{1,0:T(8,128)S(1)} %dynamic-slice_bitcast_fusion.7), channel_id=1, source_target_pairs={{0,16},{16,0},{32,48},{48,32},{1,17},{17,1},{33,49},{49,33},{2,18}... | collective-permute-start | bytes 344072 | tf_op jit(solution)/shard_map/ppermute | solution.py:18
  234.3 8.1 %collective-permute-start.16 = (f32[224,128]{1,0:T(8,128)S(1)}, f32[224,128]{1,0:T(8,128)S(1)}, u32[]{:S(2)}, u32[]{:S(2)}) collective-permute-start(f32[224,128]{1,0:T(8,128)S(1)} %bitcast_add_fusion.6), channel_id=1, source_target_pairs={{0,64},{64,0},{128,192},{192,128},{1,65},{65,1},{129,193},{193,129... | collective-permute-start | bytes 344072 | tf_op jit(solution)/shard_map/ppermute | solution.py:49
  237.0 15.0 %collective-permute-start.10 = (f32[224,128]{1,0:T(8,128)S(1)}, f32[224,128]{1,0:T(8,128)S(1)}, u32[]{:S(2)}, u32[]{:S(2)}) collective-permute-start(f32[224,128]{1,0:T(8,128)S(1)} %bitcast_add_fusion.7), channel_id=1, source_target_pairs={{0,64},{64,0},{128,192},{192,128},{1,65},{65,1},{129,193},{193,129... | collective-permute-start | bytes 344072 | tf_op jit(solution)/shard_map/ppermute | solution.py:49
  242.5 15.6 %collective-permute-start.17 = (f32[224,128]{1,0:T(8,128)S(1)}, f32[224,128]{1,0:T(8,128)S(1)}, u32[]{:S(2)}, u32[]{:S(2)}) collective-permute-start(f32[224,128]{1,0:T(8,128)S(1)} %add.149), channel_id=1, source_target_pairs={{0,128},{64,192},{128,0},{192,64},{1,129},{65,193},{129,1},{193,65... | collective-permute-start | bytes 344072 | tf_op jit(solution)/shard_map/ppermute | solution.py:49
  251.9 8.8 %collective-permute-start.11 = (f32[224,128]{1,0:T(8,128)S(1)}, f32[224,128]{1,0:T(8,128)S(1)}, u32[]{:S(2)}, u32[]{:S(2)}) collective-permute-start(f32[224,128]{1,0:T(8,128)S(1)} %add.143), channel_id=1, source_target_pairs={{0,128},{64,192},{128,0},{192,64},{1,129},{65,193},{129,1},{193,65... | collective-permute-start | bytes 344072 | tf_op jit(solution)/shard_map/ppermute | solution.py:49
  260.8 3.4 %copy-start.11 = (f32[256,224]{0,1:T(8,128)}, f32[256,224]{0,1:T(8,128)S(1)}, u32[]{:S(2)}) copy-start(f32[256,224]{0,1:T(8,128)S(1)} %get-tuple-element.13) | copy-start | bytes 688132
  260.9 3.4 %copy-start.12 = (f32[256,224]{0,1:T(8,128)}, f32[256,224]{0,1:T(8,128)S(1)}, u32[]{:S(2)}) copy-start(f32[256,224]{0,1:T(8,128)S(1)} %get-tuple-element.14) | copy-start | bytes 688132
  260.9 3.4 %copy-start.1 = (bf16[192,8192]{1,0:T(8,128)(2,1)S(1)}, bf16[192,8192]{1,0:T(8,128)(2,1)}, u32[]{:S(2)}) copy-start(bf16[192,8192]{1,0:T(8,128)(2,1)} %param.5) | copy-start | bytes 9437188
Sparse Core Ops, SparseCore 0:
  113.9 46.6 reduce-scatter.4
  163.2 44.8 reduce-scatter.2

commit v7 on v6

--- a/solution.py
+++ b/solution.py
@@ -51,18 +51,23 @@
     return x
 
 
-def reduce_terms(terms, sizes):
+def reduce_terms(terms, sizes, pieces=2):
     ff, rank = terms.shape
     cols = ff // (sizes["y"] * sizes["zl"] * sizes["x"] * sizes["core"])
     terms = terms.reshape(sizes["y"], sizes["zl"], sizes["x"], sizes["core"], cols, rank)
-    terms = jnp.transpose(terms, (3, 2, 1, 0, 4, 5)).reshape(sizes["core"], -1, rank)
-    terms = pair_sum_scatter(terms, "core")
-    terms = terms.reshape(sizes["x"], -1, rank)
-    terms = lax.psum_scatter(terms, "x", scatter_dimension=0, tiled=True)
-    terms = pair_sum_scatter(terms.reshape(sizes["zl"], -1, rank), "zl")
-    terms = pair_sum_scatter(terms.reshape(2, -1, rank), "y", 2)
-    terms = pair_sum_scatter(terms.reshape(2, -1, rank), "y", 1)
-    return terms.reshape(cols, rank)
+    terms = jnp.transpose(terms, (3, 2, 1, 0, 4, 5))
+    step = cols // pieces
+    out = []
+    for p in range(pieces):
+        part = terms[:, :, :, :, p * step : (p + 1) * step, :].reshape(sizes["core"], -1, rank)
+        part = pair_sum_scatter(part, "core")
+        part = part.reshape(sizes["x"], -1, rank)
+        part = lax.psum_scatter(part, "x", scatter_dimension=0, tiled=True)
+        part = pair_sum_scatter(part.reshape(sizes["zl"], -1, rank), "zl")
+        part = pair_sum_scatter(part.reshape(2, -1, rank), "y", 2)
+        part = pair_sum_scatter(part.reshape(2, -1, rank), "y", 1)
+        out.append(part.reshape(step, rank))
+    return jnp.concatenate(out, axis=0)
 
 
 def body(activations, cotangent, projector, moment1, moment2):

time: 276 us -> 298 us (1.080); the launches traced: 271 us -> 297 us
  local copies, waits for them, and re-layouts: 37.6 us -> 51.1 us
  waiting for transfers between devices: 144 us -> 153 us
  starting transfers between devices: 39.2 us -> 43.1 us
    slice x0 -> x6, local copies, waits for them, and re-layouts: none -> 17 us  [reduce_terms(): terms[:, :, :, :, p * step:(p + 1) * step, :]]
    reduce_scatter x2 -> x4, waiting for transfers between devices: 63.4 us -> 80.2 us  [reduce_terms(): part = lax.psum_scatter(part, 'x', scatter_dimension=0, tiled=True)]
    ppermute x14 -> x22, waiting for transfers between devices: 69.8 us -> 58.5 us  [pair_swap(): return lax.ppermute(x, name, [(i, i ^ bit) for i in range(size)])]
    ppermute x14 -> x22, starting transfers between devices: 23.4 us -> 31.2 us  [pair_swap(): return lax.ppermute(x, name, [(i, i ^ bit) for i in range(size)])]
    transpose x2 -> x0, local copies, waits for them, and re-layouts: 7.43 us -> none  [reduce_terms(): jnp.transpose(terms, (3, 2, 1, 0, 4, 5)).reshape(sizes['core'], -1, rank)]
    ppermute x4, starting transfers between devices: 15.7 us -> 11.8 us  [all_sum_rep(): x = x + lax.ppermute(x, 'rep', [(i, i ^ step) for i in range(size)])]
    ppermute x4, waiting for transfers between devices: 10.7 us -> 13.8 us  [all_sum_rep(): x = x + lax.ppermute(x, 'rep', [(i, i ^ step) for i in range(size)])]
    squeeze x8 -> x16, local copies, waits for them, and re-layouts: 4.68 us -> 7.02 us  [pair_sum_scatter(): theirs = lax.dynamic_index_in_dim(terms, 1 - i, 0, keepdims=False)]
  transfers between devices with their start and end apart: 20 -> 30, of which waited for: 16 -> 20; matrix products, arithmetic and copies ran while one was open for 10% -> 13% of each run, Pallas kernels for 0% -> 0%
where the time goes in v7:
time: 298 us; the launch traced here: 297 us
  waiting for transfers between devices  153 us (51%)
  local copies, waits for them, and re-layouts  51.1 us (17%)
  starting transfers between devices  43.1 us (14%)
  other arithmetic  22.9 us (8%)
  between operations  14.3 us (5%)
  matrix products  12.6 us (4%)
    reduce_scatter x4, waiting for transfers between devices, reduce_terms(): part = lax.psum_scatter(part, 'x', scatter_dimension=0, tiled=True)  80.2 us
    ppermute x22, waiting for transfers between devices, pair_swap(): return lax.ppermute(x, name, [(i, i ^ bit) for i in range(size)])  58.5 us
    ppermute x22, starting transfers between devices, pair_swap(): return lax.ppermute(x, name, [(i, i ^ bit) for i in range(size)])  31.2 us
    dot_general x2, local copies, waits for them, and re-layouts, body(): lax.dot_general(cotangent, low[:, k * width:(k + 1) * width], (((0,), (0,...  17.3 us
    slice x6, local copies, waits for them, and re-layouts, reduce_terms(): terms[:, :, :, :, p * step:(p + 1) * step, :]  17 us
    ppermute x4, waiting for transfers between devices, all_sum_rep(): x = x + lax.ppermute(x, 'rep', [(i, i ^ step) for i in range(size)])  13.8 us
    ppermute x4, starting transfers between devices, all_sum_rep(): x = x + lax.ppermute(x, 'rep', [(i, i ^ step) for i in range(size)])  11.8 us
    add x16, other arithmetic, pair_sum_scatter(): return mine + pair_swap(theirs, name, bit)  11.7 us
  transfers between devices with their start and end apart: 30, of which 20 were waited for; matrix products, arithmetic and copies ran while one was open for 13% of the time, Pallas kernels for 0%

profile of v7, /device:TPU:2, one launch (start us, length us, event | category | flops | bytes accessed | tf_op | source)
XLA Modules:
  0.0 296.7 jit_solution(11492150831261828804)
XLA Ops:
  7.2 1.7 collective-permute-start
  8.9 2.9 collective-permute-done
  12.7 3.3 %collective-permute-start.1 = (bf16[2,128,256]{2,1,0:T(8,128)(2,1)S(1)}, bf16[2,128,256]{2,1,0:T(8,128)(2,1)S(1)}, u32[]{:S(2)}, u32[]{:S(2)}) collective-permute-start(bf16[2,128,256]{2,1,0:T(8,128)(2,1)S(1)} %pad_maximum_fusion.5), channel_id=1, source_target_pairs={{0,32},{16,48},{32,0},{48,16},{1,33},{17,49},{33,1},{49,17},{2,34}... | collective-permute-start | bytes 393224 | tf_op jit(solution)/shard_map/ppermute | solution.py:18
  15.9 3.3 %collective-permute-done.1 = bf16[2,128,256]{2,1,0:T(8,128)(2,1)S(1)} collective-permute-done((bf16[2,128,256]{2,1,0:T(8,128)(2,1)S(1)}, bf16[2,128,256]{2,1,0:T(8,128)(2,1)S(1)}, u32[]{:S(2)}, u32[]{:S(2)}) %collective-permute-start.1) | collective-permute-done | bytes 131104 | tf_op jit(solution)/shard_map/ppermute | solution.py:18
  19.9 2.3 collective-permute-start.2
  22.3 4.5 %collective-permute-done.2 = bf16[2,2,128,256]{3,2,1,0:T(8,128)(2,1)} collective-permute-done((bf16[2,2,128,256]{3,2,1,0:T(8,128)(2,1)S(1)}, bf16[2,2,128,256]{3,2,1,0:T(8,128)(2,1)}, u32[]{:S(2)}, u32[]{:S(2)}) %collective-permute-start.2) | collective-permute-done | bytes 262176 | tf_op jit(solution)/shard_map/ppermute | solution.py:18
  26.7 1.0 select_bitcast_fusion.5
  29.3 1.9 collective-permute-start.3
  31.2 9.9 %collective-permute-done.3 = bf16[2,2,2,128,256]{4,3,2,1,0:T(8,128)(2,1)} collective-permute-done((bf16[2,2,2,128,256]{4,3,2,1,0:T(8,128)(2,1)}, bf16[2,2,2,128,256]{4,3,2,1,0:T(8,128)(2,1)}, u32[]{:S(2)}, u32[]{:S(2)}) %collective-permute-start.3) | collective-permute-done | bytes 524320 | tf_op jit(solution)/shard_map/ppermute | solution.py:18
  41.1 1.2 select_bitcast_fusion.3
  43.1 1.1 pad_maximum_fusion.2
  44.2 1.9 collective-permute-start.4
  46.1 19.2 %collective-permute-done.4 = bf16[2,2,2,2,128,256]{5,4,3,2,1,0:T(8,128)(2,1)} collective-permute-done((bf16[2,2,2,2,128,256]{5,4,3,2,1,0:T(8,128)(2,1)}, bf16[2,2,2,2,128,256]{5,4,3,2,1,0:T(8,128)(2,1)}, u32[]{:S(2)}, u32[]{:S(2)}) %collective-permute-start.4) | collective-permute-done | bytes 1048608 | tf_op jit(solution)/shard_map/ppermute | solution.py:18
  65.3 1.7 select_bitcast_fusion.1
  67.9 1.5 pad_maximum_fusion.1
  69.4 4.5 %collective-permute-done.5 = bf16[2,2,2,2,2,128,256]{6,5,4,3,2,1,0:T(8,128)(2,1)} collective-permute-done((bf16[2,2,2,2,2,128,256]{6,5,4,3,2,1,0:T(8,128)(2,1)}, bf16[2,2,2,2,2,128,256]{6,5,4,3,2,1,0:T(8,128)(2,1)}, u32[]{:S(2)}, u32[]{:S(2)}) %collective-permute-start.5) | collective-permute-done | bytes 2097184 | tf_op jit(solution)/shard_map/ppermute | solution.py:18
  73.9 2.4 broadcast_select_fusion.1
  77.2 1.1 fusion
  78.3 1.0 copy-done.2
  79.3 1.2 slice-done
  80.9 4.0 %convolution_bitcast_fusion = f32[14336,128]{0,1:T(8,128)} fusion(bf16[192,14336]{1,0:T(8,128)(2,1)S(1)} %bitcast.135, bf16[192,256]{1,0:T(8,128)(2,1)S(1)} %fusion), kind=kOutput, calls=%fused_computation | convolution fusion | flops 704643072 | bytes 12894208 | tf_op jit(solution)/shard_map/dot_general | solution.py:82
  84.9 8.6 %copy.13 = f32[14336,128]{1,0:T(8,128)} copy(f32[14336,128]{0,1:T(8,128)} %convolution_bitcast_fusion) | data formatting | bytes 14680064 | tf_op jit(solution)/shard_map/dot_general | solution.py:82
  93.5 5.7 %fusion.13 = (f32[2,4,2,4,112,128]{5,4,0,1,2,3:T(8,128)S(1)}, f32[2,4,2,4,112,128]{5,4,0,1,2,3:T(8,128)}) fusion(f32[2,4,2,4,224,128]{5,4,0,1,2,3:T(8,128)} %bitcast.139), kind=kLoop, calls=%fused_computation.73 | loop fusion | bytes 14680064 | tf_op jit(solution)/shard_map/slice | solution.py:62
  99.6 1.8 copy-done.4
  101.3 1.4 dynamic-slice_bitcast_fusion.1
  102.9 3.8 %collective-permute-done.16 = f32[3584,128]{1,0:T(8,128)S(1)} collective-permute-done((f32[3584,128]{1,0:T(8,128)}, f32[3584,128]{1,0:T(8,128)S(1)}, u32[]{:S(2)}, u32[]{:S(2)}) %collective-permute-start.16) | collective-permute-done | bytes 1835040 | tf_op jit(solution)/shard_map/ppermute | solution.py:18
  106.7 2.9 bitcast_add_fusion.1
  109.7 2.5 copy.15
  112.3 1.8 copy-done.5
  114.1 1.4 dynamic-slice_bitcast_fusion
  115.7 4.1 %convolution_bitcast_fusion.1 = f32[14336,128]{0,1:T(8,128)} fusion(bf16[192,14336]{1,0:T(8,128)(2,1)S(1)} %bitcast.137, bf16[192,256]{1,0:T(8,128)(2,1)S(1)} %fusion), kind=kOutput, calls=%fused_computation.1 | convolution fusion | flops 704643072 | bytes 12894208 | tf_op jit(solution)/shard_map/dot_general | solution.py:82
  119.8 8.7 %copy.10 = f32[14336,128]{1,0:T(8,128)} copy(f32[14336,128]{0,1:T(8,128)} %convolution_bitcast_fusion.1) | data formatting | bytes 14680064 | tf_op jit(solution)/shard_map/dot_general | solution.py:82
  128.5 3.0 %bitcast_add_fusion = f32[3584,128]{1,0:T(8,128)} fusion(f32[3584,128]{1,0:T(8,128)S(1)} %collective-permute-done.20, f32[2,3584,128]{2,1,0:T(8,128)} %bitcast.143, s32[]{:T(128)S(6)} %select_n.236), kind=kLoop, calls=%fused_computation.7 | loop fusion | flops 458752 | bytes 5505028 | tf_op jit(solution)/shard_map/add | solution.py:31
  131.6 5.7 %fusion.12 = (f32[2,4,2,4,112,128]{5,4,0,1,2,3:T(8,128)S(1)}, f32[2,4,2,4,112,128]{5,4,0,1,2,3:T(8,128)}) fusion(f32[2,4,2,4,224,128]{5,4,0,1,2,3:T(8,128)} %bitcast.138), kind=kLoop, calls=%fused_computation.72 | loop fusion | bytes 14680064 | tf_op jit(solution)/shard_map/slice | solution.py:62
  138.2 3.4 %collective-permute-done.6 = f32[3584,128]{1,0:T(8,128)S(1)} collective-permute-done((f32[3584,128]{1,0:T(8,128)S(1)}, f32[3584,128]{1,0:T(8,128)S(1)}, u32[]{:S(2)}, u32[]{:S(2)}) %collective-permute-start.6) | collective-permute-done | bytes 1835040 | tf_op jit(solution)/shard_map/ppermute | solution.py:18
  141.7 1.4 bitcast_add_fusion.3
  143.2 2.4 copy.12
  146.1 3.4 %collective-permute-done.10 = f32[3584,128]{1,0:T(8,128)S(1)} collective-permute-done((f32[3584,128]{1,0:T(8,128)S(1)}, f32[3584,128]{1,0:T(8,128)S(1)}, u32[]{:S(2)}, u32[]{:S(2)}) %collective-permute-start.10) | collective-permute-done | bytes 1835040 | tf_op jit(solution)/shard_map/ppermute | solution.py:18
  149.6 1.4 bitcast_add_fusion.2
  152.0 1.9 collective-permute-start.17
  153.9 20.0 %reduce-scatter.11.cloned.1.call-done = f32[1,896,128]{2,1,0:T(8,128)} async-done(((f32[4,896,128]{2,1,0:T(8,128)}), f32[1,896,128]{2,1,0:T(8,128)}) %reduce-scatter.11.cloned.1.call-update) | async-done | bytes 458768 | tf_op jit(solution)/shard_map/reduce_scatter | solution.py:65
  174.9 1.7 collective-permute-start.21
  176.5 29.9 %reduce-scatter.5.cloned.1.call-done = f32[1,896,128]{2,1,0:T(8,128)} async-done(((f32[4,896,128]{2,1,0:T(8,128)}), f32[1,896,128]{2,1,0:T(8,128)}) %reduce-scatter.5.cloned.1.call-update) | async-done | bytes 458768 | tf_op jit(solution)/shard_map/reduce_scatter | solution.py:65
  207.3 1.7 collective-permute-start.7
  209.0 30.3 %reduce-scatter.7.cloned.1.call-done = f32[1,896,128]{2,1,0:T(8,128)} async-done(((f32[4,896,128]{2,1,0:T(8,128)}), f32[1,896,128]{2,1,0:T(8,128)}) %reduce-scatter.7.cloned.1.call-update) | async-done | bytes 458768 | tf_op jit(solution)/shard_map/reduce_scatter | solution.py:65
  239.3 1.0 dynamic-slice_bitcast_fusion.6
  240.3 1.7 collective-permute-start.11
  242.0 1.0 bitcast_add_fusion.5
  243.0 3.1 %collective-permute-start.18 = (f32[224,128]{1,0:T(8,128)S(1)}, f32[224,128]{1,0:T(8,128)S(1)}, u32[]{:S(2)}, u32[]{:S(2)}) collective-permute-start(f32[224,128]{1,0:T(8,128)S(1)} %dynamic-slice_bitcast_fusion.9), channel_id=1, source_target_pairs={{0,32},{16,48},{32,0},{48,16},{1,33},{17,49},{33,1},{49,17},{2,34}... | collective-permute-start | bytes 344072 | tf_op jit(solution)/shard_map/ppermute | solution.py:18
  246.1 1.0 bitcast_add_fusion.4
  247.7 1.0 bitcast_add_fusion.7
  248.7 3.1 %collective-permute-start.8 = (f32[224,128]{1,0:T(8,128)S(1)}, f32[224,128]{1,0:T(8,128)S(1)}, u32[]{:S(2)}, u32[]{:S(2)}) collective-permute-start(f32[224,128]{1,0:T(8,128)S(1)} %dynamic-slice_bitcast_fusion.11), channel_id=1, source_target_pairs={{0,32},{16,48},{32,0},{48,16},{1,33},{17,49},{33,1},{49,17},{2,34}... | collective-permute-start | bytes 344072 | tf_op jit(solution)/shard_map/ppermute | solution.py:18
  252.5 1.6 collective-permute-start.19
  254.9 1.4 collective-permute-done.8
  256.3 1.6 collective-permute-start.9
  257.9 1.5 collective-permute-done.12
  260.6 2.9 collective-permute-start.24
  263.8 2.6 collective-permute-start.14
  266.4 6.3 %collective-permute-done.24 = f32[224,128]{1,0:T(8,128)S(1)} collective-permute-done((f32[224,128]{1,0:T(8,128)S(1)}, f32[224,128]{1,0:T(8,128)S(1)}, u32[]{:S(2)}, u32[]{:S(2)}) %collective-permute-start.24) | collective-permute-done | bytes 114720 | tf_op jit(solution)/shard_map/ppermute | solution.py:49
  272.7 5.1 %collective-permute-start.25 = (f32[224,128]{1,0:T(8,128)S(1)}, f32[224,128]{1,0:T(8,128)S(1)}, u32[]{:S(2)}, u32[]{:S(2)}) collective-permute-start(f32[224,128]{1,0:T(8,128)S(1)} %fusion.10), channel_id=1, source_target_pairs={{0,128},{64,192},{128,0},{192,64},{1,129},{65,193},{129,1},{193,65... | collective-permute-start | bytes 344072 | tf_op jit(solution)/shard_map/ppermute | solution.py:49
  277.8 1.3 collective-permute-start.15
  279.1 2.7 collective-permute-done.25
  281.8 4.8 %collective-permute-done.15 = f32[224,128]{1,0:T(8,128)S(1)} collective-permute-done((f32[224,128]{1,0:T(8,128)S(1)}, f32[224,128]{1,0:T(8,128)S(1)}, u32[]{:S(2)}, u32[]{:S(2)}) %collective-permute-start.15) | collective-permute-done | bytes 114720 | tf_op jit(solution)/shard_map/ppermute | solution.py:49
  286.8 3.3 %convolution_convert_fusion = bf16[8192,224]{0,1:T(8,128)(2,1)} fusion(bf16[8192,256]{1,0:T(8,128)(2,1)S(1)} %bitcast.133, f32[256,224]{0,1:T(8,128)S(1)} %get-tuple-element.17, f32[256,224]{0,1:T(8,128)S(1)} %get-tuple-element.18), kind=kOutput, calls=%fused_computation.2 | convolution fusion | flops 941645824 | bytes 8323072 | tf_op jit(solution)/shard_map/dot_general | solution.py:96
  (109 shorter events, 15.2 us)
Async XLA Ops:
  7.2 70.0 %copy-start = (bf16[192,8192]{1,0:T(8,128)(2,1)S(1)}, bf16[192,8192]{1,0:T(8,128)(2,1)}, u32[]{:S(2)}) copy-start(bf16[192,8192]{1,0:T(8,128)(2,1)} %param.5) | copy-start | bytes 9437188
  7.2 143.9 %reduce-scatter.9.cloned.1.call-start = ((), (), s32[]{:S(2)}) async-start(), calls=%async_computation.6 | async-start | bytes 2293760 | tf_op jit(solution)/shard_map/reduce_scatter | solution.py:65
  7.2 4.6 %collective-permute-start = (bf16[128,256]{1,0:T(8,128)(2,1)}, bf16[128,256]{1,0:T(8,128)(2,1)S(1)}, u32[]{:S(2)}, u32[]{:S(2)}) collective-permute-start(bf16[128,256]{1,0:T(8,128)(2,1)} %param.7), channel_id=1, source_target_pairs={{0,16},{16,0},{32,48},{48,32},{1,17},{17,1},{33,49},{49,33},{2,18}... | collective-permute-start | bytes 196616 | tf_op jit(solution)/shard_map/ppermute | solution.py:18
  12.7 6.6 %collective-permute-start.1 = (bf16[2,128,256]{2,1,0:T(8,128)(2,1)S(1)}, bf16[2,128,256]{2,1,0:T(8,128)(2,1)S(1)}, u32[]{:S(2)}, u32[]{:S(2)}) collective-permute-start(bf16[2,128,256]{2,1,0:T(8,128)(2,1)S(1)} %pad_maximum_fusion.5), channel_id=1, source_target_pairs={{0,32},{16,48},{32,0},{48,16},{1,33},{17,49},{33,1},{49,17},{2,34}... | collective-permute-start | bytes 393224 | tf_op jit(solution)/shard_map/ppermute | solution.py:18
  19.3 0.7 copy-start.11
  19.9 6.8 %collective-permute-start.2 = (bf16[2,2,128,256]{3,2,1,0:T(8,128)(2,1)S(1)}, bf16[2,2,128,256]{3,2,1,0:T(8,128)(2,1)}, u32[]{:S(2)}, u32[]{:S(2)}) collective-permute-start(bf16[2,2,128,256]{3,2,1,0:T(8,128)(2,1)S(1)} %pad_maximum_fusion.4), channel_id=1, source_target_pairs={{0,2},{2,0},{4,6},{6,4},{1,3},{3,1},{5,7},{7,5},{8,10},{10,8},{12,... | collective-permute-start | bytes 786440 | tf_op jit(solution)/shard_map/ppermute | solution.py:18
  27.8 0.7 copy-start.10
  29.3 11.8 %collective-permute-start.3 = (bf16[2,2,2,128,256]{4,3,2,1,0:T(8,128)(2,1)}, bf16[2,2,2,128,256]{4,3,2,1,0:T(8,128)(2,1)}, u32[]{:S(2)}, u32[]{:S(2)}) collective-permute-start(bf16[2,2,2,128,256]{4,3,2,1,0:T(8,128)(2,1)} %pad_maximum_fusion.3), channel_id=1, source_target_pairs={{0,4},{2,6},{4,0},{6,2},{1,5},{3,7},{5,1},{7,3},{8,12},{10,14},{12... | collective-permute-start | bytes 1572872 | tf_op jit(solution)/shard_map/ppermute | solution.py:18
  42.3 0.8 copy-start.8
  42.3 1.9 copy-start.9
  44.2 21.1 %collective-permute-start.4 = (bf16[2,2,2,2,128,256]{5,4,3,2,1,0:T(8,128)(2,1)}, bf16[2,2,2,2,128,256]{5,4,3,2,1,0:T(8,128)(2,1)}, u32[]{:S(2)}, u32[]{:S(2)}) collective-permute-start(bf16[2,2,2,2,128,256]{5,4,3,2,1,0:T(8,128)(2,1)} %pad_maximum_fusion.2), channel_id=1, source_target_pairs={{0,8},{8,0},{1,9},{9,1},{2,10},{10,2},{3,11},{11,3},{4,12},{12,4},... | collective-permute-start | bytes 3145736 | tf_op jit(solution)/shard_map/ppermute | solution.py:18
  66.9 1.0 copy-start.6
  66.9 2.5 copy-start.7
  69.4 4.5 %collective-permute-start.5 = (bf16[2,2,2,2,2,128,256]{6,5,4,3,2,1,0:T(8,128)(2,1)}, bf16[2,2,2,2,2,128,256]{6,5,4,3,2,1,0:T(8,128)(2,1)}, u32[]{:S(2)}, u32[]{:S(2)}) collective-permute-start(bf16[2,2,2,2,2,128,256]{6,5,4,3,2,1,0:T(8,128)(2,1)} %pad_maximum_fusion.1), channel_id=1, source_target_pairs={{0,1},{1,0},{2,3},{3,2},{4,5},{5,4},{6,7},{7,6},{8,9},{9,8},{10,11... | collective-permute-start | bytes 6291464 | tf_op jit(solution)/shard_map/ppermute | solution.py:18
  76.8 3.7 %slice-start = ((s8[5505024]{0:T(1024)(128)(4,1)}), s8[4194304]{0:T(1024)(128)(4,1)S(1)}, s32[]{:S(2)}) async-start(s8[5505024]{0:T(1024)(128)(4,1)} %bitcast.134), calls=%async_computation.8 | async-start | bytes 8388608
  77.2 2.1 copy-start.2
  77.2 3.7 %slice-start.1 = ((s8[5505024]{0:T(1024)(128)(4,1)}), s8[1310720]{0:T(1024)(128)(4,1)S(1)}, s32[]{:S(2)}) async-start(s8[5505024]{0:T(1024)(128)(4,1)} %bitcast.134), calls=%async_computation.9 | async-start | bytes 2621440
  99.5 1.8 copy-start.4
  102.7 4.0 %collective-permute-start.16 = (f32[3584,128]{1,0:T(8,128)}, f32[3584,128]{1,0:T(8,128)S(1)}, u32[]{:S(2)}, u32[]{:S(2)}) collective-permute-start(f32[3584,128]{1,0:T(8,128)} %dynamic-slice_bitcast_fusion.1), channel_id=1, source_target_pairs={{0,1},{1,0},{2,3},{3,2},{4,5},{5,4},{6,7},{7,6},{8,9},{9,8},{10,11... | collective-permute-start | bytes 5505032 | tf_op jit(solution)/shard_map/ppermute | solution.py:18
  109.6 64.3 %reduce-scatter.11.cloned.1.call-start = ((), (), s32[]{:S(2)}) async-start(), calls=%async_computation.7 | async-start | bytes 2293760 | tf_op jit(solution)/shard_map/reduce_scatter | solution.py:65
  109.7 6.0 %slice-start.2 = ((s8[5505024]{0:T(1024)(128)(4,1)}), s8[4194304]{0:T(1024)(128)(4,1)S(1)}, s32[]{:S(2)}) async-start(s8[5505024]{0:T(1024)(128)(4,1)} %bitcast.136), calls=%async_computation.10 | async-start | bytes 8388608
  109.7 6.0 %slice-start.3 = ((s8[5505024]{0:T(1024)(128)(4,1)}), s8[1310720]{0:T(1024)(128)(4,1)S(1)}, s32[]{:S(2)}) async-start(s8[5505024]{0:T(1024)(128)(4,1)} %bitcast.136), calls=%async_computation.11 | async-start | bytes 2621440
  112.3 1.8 copy-start.5
  115.5 13.0 %collective-permute-start.20 = (f32[3584,128]{1,0:T(8,128)}, f32[3584,128]{1,0:T(8,128)S(1)}, u32[]{:S(2)}, u32[]{:S(2)}) collective-permute-start(f32[3584,128]{1,0:T(8,128)} %dynamic-slice_bitcast_fusion), channel_id=1, source_target_pairs={{0,1},{1,0},{2,3},{3,2},{4,5},{5,4},{6,7},{7,6},{8,9},{9,8},{10,11... | collective-permute-start | bytes 5505032 | tf_op jit(solution)/shard_map/ppermute | solution.py:18
  131.5 74.9 %reduce-scatter.5.cloned.1.call-start = ((), (), s32[]{:S(2)}) async-start(), calls=%async_computation.4 | async-start | bytes 2293760 | tf_op jit(solution)/shard_map/reduce_scatter | solution.py:65
  137.8 3.9 %collective-permute-start.6 = (f32[3584,128]{1,0:T(8,128)S(1)}, f32[3584,128]{1,0:T(8,128)S(1)}, u32[]{:S(2)}, u32[]{:S(2)}) collective-permute-start(f32[3584,128]{1,0:T(8,128)S(1)} %dynamic-slice_bitcast_fusion.3), channel_id=1, source_target_pairs={{0,1},{1,0},{2,3},{3,2},{4,5},{5,4},{6,7},{7,6},{8,9},{9,8},{10,11... | collective-permute-start | bytes 5505032 | tf_op jit(solution)/shard_map/ppermute | solution.py:18
  143.1 96.2 %reduce-scatter.7.cloned.1.call-start = ((), (), s32[]{:S(2)}) async-start(), calls=%async_computation.5 | async-start | bytes 2293760 | tf_op jit(solution)/shard_map/reduce_scatter | solution.py:65
  145.7 3.9 %collective-permute-start.10 = (f32[3584,128]{1,0:T(8,128)S(1)}, f32[3584,128]{1,0:T(8,128)S(1)}, u32[]{:S(2)}, u32[]{:S(2)}) collective-permute-start(f32[3584,128]{1,0:T(8,128)S(1)} %dynamic-slice_bitcast_fusion.2), channel_id=1, source_target_pairs={{0,1},{1,0},{2,3},{3,2},{4,5},{5,4},{6,7},{7,6},{8,9},{9,8},{10,11... | collective-permute-start | bytes 5505032 | tf_op jit(solution)/shard_map/ppermute | solution.py:18
  152.0 89.9 %collective-permute-start.17 = (f32[448,128]{1,0:T(8,128)S(1)}, f32[448,128]{1,0:T(8,128)S(1)}, u32[]{:S(2)}, u32[]{:S(2)}) collective-permute-start(f32[448,128]{1,0:T(8,128)S(1)} %dynamic-slice_bitcast_fusion.5), channel_id=1, source_target_pairs={{0,8},{8,0},{1,9},{9,1},{2,10},{10,2},{3,11},{11,3},{4,12},{12,4},... | collective-permute-start | bytes 688136 | tf_op jit(solution)/shard_map/ppermute | solution.py:18
  174.9 71.2 %collective-permute-start.21 = (f32[448,128]{1,0:T(8,128)S(1)}, f32[448,128]{1,0:T(8,128)S(1)}, u32[]{:S(2)}, u32[]{:S(2)}) collective-permute-start(f32[448,128]{1,0:T(8,128)S(1)} %dynamic-slice_bitcast_fusion.4), channel_id=1, source_target_pairs={{0,8},{8,0},{1,9},{9,1},{2,10},{10,2},{3,11},{11,3},{4,12},{12,4},... | collective-permute-start | bytes 688136 | tf_op jit(solution)/shard_map/ppermute | solution.py:18
  207.3 40.3 %collective-permute-start.7 = (f32[448,128]{1,0:T(8,128)S(1)}, f32[448,128]{1,0:T(8,128)S(1)}, u32[]{:S(2)}, u32[]{:S(2)}) collective-permute-start(f32[448,128]{1,0:T(8,128)S(1)} %dynamic-slice_bitcast_fusion.7), channel_id=1, source_target_pairs={{0,8},{8,0},{1,9},{9,1},{2,10},{10,2},{3,11},{11,3},{4,12},{12,4},... | collective-permute-start | bytes 688136 | tf_op jit(solution)/shard_map/ppermute | solution.py:18
  239.3 12.5 %copy-start.14 = (f32[1,896,128]{2,1,0:T(8,128)S(1)}, f32[1,896,128]{2,1,0:T(8,128)}, u32[]{:S(2)}) copy-start(f32[1,896,128]{2,1,0:T(8,128)} %reduce-scatter.7.cloned.1.call-done) | copy-start | bytes 1376260
  240.3 11.5 %collective-permute-start.11 = (f32[448,128]{1,0:T(8,128)S(1)}, f32[448,128]{1,0:T(8,128)S(1)}, u32[]{:S(2)}, u32[]{:S(2)}) collective-permute-start(f32[448,128]{1,0:T(8,128)S(1)} %dynamic-slice_bitcast_fusion.6), channel_id=1, source_target_pairs={{0,8},{8,0},{1,9},{9,1},{2,10},{10,2},{3,11},{11,3},{4,12},{12,4},... | collective-permute-start | bytes 688136 | tf_op jit(solution)/shard_map/ppermute | solution.py:18
  243.0 9.5 %collective-permute-start.18 = (f32[224,128]{1,0:T(8,128)S(1)}, f32[224,128]{1,0:T(8,128)S(1)}, u32[]{:S(2)}, u32[]{:S(2)}) collective-permute-start(f32[224,128]{1,0:T(8,128)S(1)} %dynamic-slice_bitcast_fusion.9), channel_id=1, source_target_pairs={{0,32},{16,48},{32,0},{48,16},{1,33},{17,49},{33,1},{49,17},{2,34}... | collective-permute-start | bytes 344072 | tf_op jit(solution)/shard_map/ppermute | solution.py:18
  247.1 39.6 %copy-start.15 = (f32[256,224]{0,1:T(8,128)S(1)}, f32[256,224]{0,1:T(8,128)}, u32[]{:S(2)}) copy-start(f32[256,224]{0,1:T(8,128)} %param.9) | copy-start | bytes 688132
  247.1 39.6 %copy-start.16 = (f32[256,224]{0,1:T(8,128)S(1)}, f32[256,224]{0,1:T(8,128)}, u32[]{:S(2)}) copy-start(f32[256,224]{0,1:T(8,128)} %param.8) | copy-start | bytes 688132
  247.1 7.2 %collective-permute-start.22 = (f32[224,128]{1,0:T(8,128)S(1)}, f32[224,128]{1,0:T(8,128)S(1)}, u32[]{:S(2)}, u32[]{:S(2)}) collective-permute-start(f32[224,128]{1,0:T(8,128)S(1)} %dynamic-slice_bitcast_fusion.8), channel_id=1, source_target_pairs={{0,32},{16,48},{32,0},{48,16},{1,33},{17,49},{33,1},{49,17},{2,34}... | collective-permute-start | bytes 344072 | tf_op jit(solution)/shard_map/ppermute | solution.py:18
  248.7 38.1 %copy-start.3 = (bf16[2,2,4,4,128,256]{5,4,0,2,1,3:T(8,128)(2,1)S(1)}, bf16[2,2,4,4,128,256]{5,4,0,2,1,3:T(8,128)(2,1)}, u32[]{:S(2)}) copy-start(bf16[2,2,4,4,128,256]{5,4,0,2,1,3:T(8,128)(2,1)} %copy-done.2) | copy-start | bytes 12582916
  248.7 7.6 %collective-permute-start.8 = (f32[224,128]{1,0:T(8,128)S(1)}, f32[224,128]{1,0:T(8,128)S(1)}, u32[]{:S(2)}, u32[]{:S(2)}) collective-permute-start(f32[224,128]{1,0:T(8,128)S(1)} %dynamic-slice_bitcast_fusion.11), channel_id=1, source_target_pairs={{0,32},{16,48},{32,0},{48,16},{1,33},{17,49},{33,1},{49,17},{2,34}... | collective-permute-start | bytes 344072 | tf_op jit(solution)/shard_map/ppermute | solution.py:18
  251.8 7.6 %collective-permute-start.12 = (f32[224,128]{1,0:T(8,128)S(1)}, f32[224,128]{1,0:T(8,128)S(1)}, u32[]{:S(2)}, u32[]{:S(2)}) collective-permute-start(f32[224,128]{1,0:T(8,128)S(1)} %dynamic-slice_bitcast_fusion.10), channel_id=1, source_target_pairs={{0,32},{16,48},{32,0},{48,16},{1,33},{17,49},{33,1},{49,17},{2,34}... | collective-permute-start | bytes 344072 | tf_op jit(solution)/shard_map/ppermute | solution.py:18
  252.5 7.9 %collective-permute-start.19 = (f32[112,128]{1,0:T(8,128)S(1)}, f32[112,128]{1,0:T(8,128)S(1)}, u32[]{:S(2)}, u32[]{:S(2)}) collective-permute-start(f32[112,128]{1,0:T(8,128)S(1)} %dynamic-slice_bitcast_fusion.13), channel_id=1, source_target_pairs={{0,16},{16,0},{32,48},{48,32},{1,17},{17,1},{33,49},{49,33},{2,18}... | collective-permute-start | bytes 172040 | tf_op jit(solution)/shard_map/ppermute | solution.py:18
  254.3 6.2 %collective-permute-start.23 = (f32[112,128]{1,0:T(8,128)S(1)}, f32[112,128]{1,0:T(8,128)S(1)}, u32[]{:S(2)}, u32[]{:S(2)}) collective-permute-start(f32[112,128]{1,0:T(8,128)S(1)} %dynamic-slice_bitcast_fusion.12), channel_id=1, source_target_pairs={{0,16},{16,0},{32,48},{48,32},{1,17},{17,1},{33,49},{49,33},{2,18}... | collective-permute-start | bytes 172040 | tf_op jit(solution)/shard_map/ppermute | solution.py:18
  256.3 7.1 %collective-permute-start.9 = (f32[112,128]{1,0:T(8,128)S(1)}, f32[112,128]{1,0:T(8,128)S(1)}, u32[]{:S(2)}, u32[]{:S(2)}) collective-permute-start(f32[112,128]{1,0:T(8,128)S(1)} %dynamic-slice_bitcast_fusion.15), channel_id=1, source_target_pairs={{0,16},{16,0},{32,48},{48,32},{1,17},{17,1},{33,49},{49,33},{2,18}... | collective-permute-start | bytes 172040 | tf_op jit(solution)/shard_map/ppermute | solution.py:18
  259.5 4.3 %collective-permute-start.13 = (f32[112,128]{1,0:T(8,128)S(1)}, f32[112,128]{1,0:T(8,128)S(1)}, u32[]{:S(2)}, u32[]{:S(2)}) collective-permute-start(f32[112,128]{1,0:T(8,128)S(1)} %dynamic-slice_bitcast_fusion.14), channel_id=1, source_target_pairs={{0,16},{16,0},{32,48},{48,32},{1,17},{17,1},{33,49},{49,33},{2,18}... | collective-permute-start | bytes 172040 | tf_op jit(solution)/shard_map/ppermute | solution.py:18
  260.6 12.1 %collective-permute-start.24 = (f32[224,128]{1,0:T(8,128)S(1)}, f32[224,128]{1,0:T(8,128)S(1)}, u32[]{:S(2)}, u32[]{:S(2)}) collective-permute-start(f32[224,128]{1,0:T(8,128)S(1)} %pad_maximum_fusion.7), channel_id=1, source_target_pairs={{0,64},{64,0},{128,192},{192,128},{1,65},{65,1},{129,193},{193,129... | collective-permute-start | bytes 344072 | tf_op jit(solution)/shard_map/ppermute | solution.py:49
  263.8 14.0 %collective-permute-start.14 = (f32[224,128]{1,0:T(8,128)S(1)}, f32[224,128]{1,0:T(8,128)S(1)}, u32[]{:S(2)}, u32[]{:S(2)}) collective-permute-start(f32[224,128]{1,0:T(8,128)S(1)} %pad_maximum_fusion.6), channel_id=1, source_target_pairs={{0,64},{64,0},{128,192},{192,128},{1,65},{65,1},{129,193},{193,129... | collective-permute-start | bytes 344072 | tf_op jit(solution)/shard_map/ppermute | solution.py:49
  272.7 9.1 %collective-permute-start.25 = (f32[224,128]{1,0:T(8,128)S(1)}, f32[224,128]{1,0:T(8,128)S(1)}, u32[]{:S(2)}, u32[]{:S(2)}) collective-permute-start(f32[224,128]{1,0:T(8,128)S(1)} %fusion.10), channel_id=1, source_target_pairs={{0,128},{64,192},{128,0},{192,64},{1,129},{65,193},{129,1},{193,65... | collective-permute-start | bytes 344072 | tf_op jit(solution)/shard_map/ppermute | solution.py:49
  277.8 8.8 %collective-permute-start.15 = (f32[224,128]{1,0:T(8,128)S(1)}, f32[224,128]{1,0:T(8,128)S(1)}, u32[]{:S(2)}, u32[]{:S(2)}) collective-permute-start(f32[224,128]{1,0:T(8,128)S(1)} %fusion.11), channel_id=1, source_target_pairs={{0,128},{64,192},{128,0},{192,64},{1,129},{65,193},{129,1},{193,65... | collective-permute-start | bytes 344072 | tf_op jit(solution)/shard_map/ppermute | solution.py:49
  286.7 3.4 %copy-start.12 = (f32[256,224]{0,1:T(8,128)}, f32[256,224]{0,1:T(8,128)S(1)}, u32[]{:S(2)}) copy-start(f32[256,224]{0,1:T(8,128)S(1)} %get-tuple-element.17) | copy-start | bytes 688132
  286.8 3.4 %copy-start.13 = (f32[256,224]{0,1:T(8,128)}, f32[256,224]{0,1:T(8,128)S(1)}, u32[]{:S(2)}) copy-start(f32[256,224]{0,1:T(8,128)S(1)} %get-tuple-element.18) | copy-start | bytes 688132
  286.8 3.4 %copy-start.1 = (bf16[192,8192]{1,0:T(8,128)(2,1)S(1)}, bf16[192,8192]{1,0:T(8,128)(2,1)}, u32[]{:S(2)}) copy-start(bf16[192,8192]{1,0:T(8,128)(2,1)} %param.5) | copy-start | bytes 9437188
Sparse Core Ops, SparseCore 0:
  109.8 31.6 reduce-scatter.8
  144.0 29.8 reduce-scatter.10
  176.5 29.8 reduce-scatter.4
  209.4 29.8 reduce-scatter.6

commit v8 on v6

--- a/solution.py
+++ b/solution.py
@@ -33,12 +33,11 @@
 
 def gather_projector(projector, sizes):
     rows, width = projector.shape
-    full = swap_stack(swap_stack(projector, "y", 1), "y", 2)
-    full = swap_stack(swap_stack(full, "x", 1), "x", 2)
+    full = swap_stack(swap_stack(projector, "y", 2), "y", 1)
+    full = swap_stack(swap_stack(full, "x", 2), "x", 1)
     full = swap_stack(full, "zl")
     full = swap_stack(full, "core")
-    full = full.reshape(sizes["core"], sizes["zl"], sizes["x"], sizes["y"], rows, width)
-    full = jnp.transpose(full, (3, 1, 2, 0, 4, 5))
+    full = jnp.transpose(full, (5, 4, 1, 3, 2, 0, 6, 7))
     return full.reshape(-1, width)
 
 
@@ -54,14 +53,14 @@
 def reduce_terms(terms, sizes):
     ff, rank = terms.shape
     cols = ff // (sizes["y"] * sizes["zl"] * sizes["x"] * sizes["core"])
-    terms = terms.reshape(sizes["y"], sizes["zl"], sizes["x"], sizes["core"], cols, rank)
-    terms = jnp.transpose(terms, (3, 2, 1, 0, 4, 5)).reshape(sizes["core"], -1, rank)
+    terms = terms.reshape(2, 2, sizes["zl"], sizes["x"], sizes["core"], cols, rank)
+    terms = jnp.transpose(terms, (4, 3, 2, 1, 0, 5, 6)).reshape(sizes["core"], -1, rank)
     terms = pair_sum_scatter(terms, "core")
     terms = terms.reshape(sizes["x"], -1, rank)
     terms = lax.psum_scatter(terms, "x", scatter_dimension=0, tiled=True)
     terms = pair_sum_scatter(terms.reshape(sizes["zl"], -1, rank), "zl")
+    terms = pair_sum_scatter(terms.reshape(2, -1, rank), "y", 1)
     terms = pair_sum_scatter(terms.reshape(2, -1, rank), "y", 2)
-    terms = pair_sum_scatter(terms.reshape(2, -1, rank), "y", 1)
     return terms.reshape(cols, rank)
 
 

time: 276 us -> 273 us (0.989); the launches traced: 271 us -> 272 us
    another operation x11 -> x12, other arithmetic: 8.56 us -> 11 us  [swap_stack(): return jnp.stack([jnp.where(first, x, other), jnp.where(first, other, x)])]
where the time goes in v8:
time: 273 us; the launch traced here: 272 us
  waiting for transfers between devices  144 us (53%)
  starting transfers between devices  40.6 us (15%)
  local copies, waits for them, and re-layouts  37.2 us (14%)
  other arithmetic  20.9 us (8%)
  matrix products  15.1 us (6%)
  between operations  14.4 us (5%)
    ppermute x14, waiting for transfers between devices, pair_swap(): return lax.ppermute(x, name, [(i, i ^ bit) for i in range(size)])  69.6 us
    reduce_scatter x2, waiting for transfers between devices, reduce_terms(): terms = lax.psum_scatter(terms, 'x', scatter_dimension=0, tiled=True)  63.4 us
    ppermute x14, starting transfers between devices, pair_swap(): return lax.ppermute(x, name, [(i, i ^ bit) for i in range(size)])  24.2 us
    dot_general x2, local copies, waits for them, and re-layouts, body(): lax.dot_general(cotangent, low[:, k * width:(k + 1) * width], (((0,), (0,...  17.2 us
    ppermute x4, starting transfers between devices, all_sum_rep(): x = x + lax.ppermute(x, 'rep', [(i, i ^ step) for i in range(size)])  16.4 us
    another operation x12, other arithmetic, swap_stack(): return jnp.stack([jnp.where(first, x, other), jnp.where(first, other, x)])  11 us
    ppermute x4, waiting for transfers between devices, all_sum_rep(): x = x + lax.ppermute(x, 'rep', [(i, i ^ step) for i in range(size)])  10.8 us
    dot_general x2, matrix products, body(): lax.dot_general(cotangent, low[:, k * width:(k + 1) * width], (((0,), (0,...  10.7 us
  transfers between devices with their start and end apart: 20, of which 16 were waited for; matrix products, arithmetic and copies ran while one was open for 10% of the time, Pallas kernels for 0%

profile of v8, /device:TPU:2, one launch (start us, length us, event | category | flops | bytes accessed | tf_op | source)
XLA Modules:
  0.0 272.1 jit_solution(11641989635866694818)
XLA Ops:
  7.2 3.3 %collective-permute-start = (bf16[128,256]{1,0:T(8,128)(2,1)}, bf16[128,256]{1,0:T(8,128)(2,1)S(1)}, u32[]{:S(2)}, u32[]{:S(2)}) collective-permute-start(bf16[128,256]{1,0:T(8,128)(2,1)} %param.7), channel_id=1, source_target_pairs={{0,32},{16,48},{32,0},{48,16},{1,33},{17,49},{33,1},{49,17},{2,34}... | collective-permute-start | bytes 196616 | tf_op jit(solution)/shard_map/ppermute | solution.py:18
  10.5 2.8 %collective-permute-done = bf16[128,256]{1,0:T(8,128)(2,1)S(1)} collective-permute-done((bf16[128,256]{1,0:T(8,128)(2,1)}, bf16[128,256]{1,0:T(8,128)(2,1)S(1)}, u32[]{:S(2)}, u32[]{:S(2)}) %collective-permute-start) | collective-permute-done | bytes 65568 | tf_op jit(solution)/shard_map/ppermute | solution.py:18
  13.3 0.9 select_bitcast_fusion.11
  14.2 1.7 collective-permute-start.1
  15.8 3.4 %collective-permute-done.1 = bf16[2,128,256]{2,1,0:T(8,128)(2,1)S(1)} collective-permute-done((bf16[2,128,256]{2,1,0:T(8,128)(2,1)S(1)}, bf16[2,128,256]{2,1,0:T(8,128)(2,1)S(1)}, u32[]{:S(2)}, u32[]{:S(2)}) %collective-permute-start.1) | collective-permute-done | bytes 131104 | tf_op jit(solution)/shard_map/ppermute | solution.py:18
  19.3 0.6 copy-done.10
  19.9 2.2 collective-permute-start.2
  22.2 5.9 %collective-permute-done.2 = bf16[2,2,128,256]{3,2,0,1:T(8,128)(2,1)} collective-permute-done((bf16[2,2,128,256]{3,2,0,1:T(8,128)(2,1)S(1)}, bf16[2,2,128,256]{3,2,0,1:T(8,128)(2,1)}, u32[]{:S(2)}, u32[]{:S(2)}) %collective-permute-start.2) | collective-permute-done | bytes 262176 | tf_op jit(solution)/shard_map/ppermute | solution.py:18
  28.0 1.0 select_bitcast_fusion.7
  29.0 0.7 copy-done.9
  29.8 0.8 pad_maximum_fusion.3
  30.6 2.2 collective-permute-start.3
  32.8 8.3 %collective-permute-done.3 = bf16[2,2,2,128,256]{4,3,0,1,2:T(8,128)(2,1)} collective-permute-done((bf16[2,2,2,128,256]{4,3,0,1,2:T(8,128)(2,1)}, bf16[2,2,2,128,256]{4,3,0,1,2:T(8,128)(2,1)}, u32[]{:S(2)}, u32[]{:S(2)}) %collective-permute-start.3) | collective-permute-done | bytes 524320 | tf_op jit(solution)/shard_map/ppermute | solution.py:18
  41.1 1.2 select_bitcast_fusion.5
  42.3 0.8 copy-done.7
  43.1 1.1 pad_maximum_fusion.2
  44.2 1.9 collective-permute-start.4
  46.1 19.2 %collective-permute-done.4 = bf16[2,2,2,2,128,256]{5,4,0,1,2,3:T(8,128)(2,1)} collective-permute-done((bf16[2,2,2,2,128,256]{5,4,0,1,2,3:T(8,128)(2,1)}, bf16[2,2,2,2,128,256]{5,4,0,1,2,3:T(8,128)(2,1)}, u32[]{:S(2)}, u32[]{:S(2)}) %collective-permute-start.4) | collective-permute-done | bytes 1048608 | tf_op jit(solution)/shard_map/ppermute | solution.py:18
  65.3 1.7 select_bitcast_fusion.3
  66.9 1.0 copy-done.5
  67.9 1.5 pad_maximum_fusion.1
  69.4 4.5 %collective-permute-done.5 = bf16[2,2,2,2,2,128,256]{6,5,1,2,0,3,4:T(8,128)(2,1)} collective-permute-done((bf16[2,2,2,2,2,128,256]{6,5,1,2,0,3,4:T(8,128)(2,1)}, bf16[2,2,2,2,2,128,256]{6,5,1,2,0,3,4:T(8,128)(2,1)}, u32[]{:S(2)}, u32[]{:S(2)}) %collective-permute-start.5) | collective-permute-done | bytes 2097184 | tf_op jit(solution)/shard_map/ppermute | solution.py:18
  73.9 2.4 select_bitcast_fusion.1
  76.4 0.4 pad_maximum_fusion
  76.8 1.1 fusion
  77.9 1.0 copy-done.2
  78.9 1.6 slice-done
  80.5 0.4 slice-done.1
  80.9 4.0 %convolution_bitcast_fusion = f32[14336,128]{0,1:T(8,128)} fusion(bf16[192,14336]{1,0:T(8,128)(2,1)S(1)} %bitcast.105, bf16[192,256]{1,0:T(8,128)(2,1)S(1)} %fusion), kind=kOutput, calls=%fused_computation | convolution fusion | flops 704643072 | bytes 12894208 | tf_op jit(solution)/shard_map/dot_general | solution.py:76
  84.9 8.6 %copy.15 = f32[14336,128]{1,0:T(8,128)} copy(f32[14336,128]{0,1:T(8,128)} %convolution_bitcast_fusion) | data formatting | bytes 14680064 | tf_op jit(solution)/shard_map/dot_general | solution.py:76
  93.5 3.7 %copy.16 = f32[2,4,2,2,2,224,128]{6,5,4,3,2,1,0:T(8,128)S(1)} copy(f32[2,4,2,2,2,224,128]{6,5,0,1,2,3,4:T(8,128)} %bitcast.106) | data formatting | bytes 14680064 | tf_op jit(solution)/shard_map/transpose | solution.py:57
  97.3 2.3 dynamic-slice_bitcast_fusion
  99.5 1.7 copy-done.4
  101.4 6.6 %collective-permute-done.12 = f32[7168,128]{1,0:T(8,128)} collective-permute-done((f32[7168,128]{1,0:T(8,128)}, f32[7168,128]{1,0:T(8,128)}, u32[]{:S(2)}, u32[]{:S(2)}) %collective-permute-start.12) | collective-permute-done | bytes 3670048 | tf_op jit(solution)/shard_map/ppermute | solution.py:18
  108.0 5.4 %bitcast_add_fusion = f32[7168,128]{1,0:T(8,128)} fusion(f32[7168,128]{1,0:T(8,128)} %collective-permute-done.12, f32[2,7168,128]{2,1,0:T(8,128)} %bitcast.109, s32[]{:T(128)S(6)} %select_n.196), kind=kLoop, calls=%fused_computation.4 | loop fusion | flops 917504 | bytes 11010052 | tf_op jit(solution)/shard_map/add | solution.py:31
  113.4 6.6 %convolution_bitcast_fusion.1 = f32[14336,128]{0,1:T(8,128)} fusion(bf16[192,14336]{1,0:T(8,128)(2,1)} %param.6, bf16[192,256]{1,0:T(8,128)(2,1)S(1)} %fusion), kind=kOutput, calls=%fused_computation.1 | convolution fusion | flops 704643072 | bytes 12894208 | tf_op jit(solution)/shard_map/dot_general | solution.py:76
  120.1 8.6 %copy.13 = f32[14336,128]{1,0:T(8,128)} copy(f32[14336,128]{0,1:T(8,128)} %convolution_bitcast_fusion.1) | data formatting | bytes 14680064 | tf_op jit(solution)/shard_map/dot_general | solution.py:76
  128.7 3.7 %copy.14 = f32[2,4,2,2,2,224,128]{6,5,4,3,2,1,0:T(8,128)S(1)} copy(f32[2,4,2,2,2,224,128]{6,5,0,1,2,3,4:T(8,128)} %bitcast.107) | data formatting | bytes 14680064 | tf_op jit(solution)/shard_map/transpose | solution.py:57
  132.7 0.4 collective-permute-start.6
  133.1 6.3 %collective-permute-done.6 = f32[7168,128]{1,0:T(8,128)S(1)} collective-permute-done((f32[7168,128]{1,0:T(8,128)S(1)}, f32[7168,128]{1,0:T(8,128)S(1)}, u32[]{:S(2)}, u32[]{:S(2)}) %collective-permute-start.6) | collective-permute-done | bytes 3670048 | tf_op jit(solution)/shard_map/ppermute | solution.py:18
  139.3 2.2 bitcast_add_fusion.1
  141.5 18.7 %reduce-scatter.5.cloned.1.call-done = f32[1,1792,128]{2,1,0:T(8,128)} async-done(((f32[4,1792,128]{2,1,0:T(8,128)}), f32[1,1792,128]{2,1,0:T(8,128)}) %reduce-scatter.5.cloned.1.call-update) | async-done | bytes 917520 | tf_op jit(solution)/shard_map/reduce_scatter | solution.py:60
  160.2 1.0 dynamic-slice_bitcast_fusion.2
  161.2 1.6 collective-permute-start.13
  162.9 44.8 %reduce-scatter.3.cloned.1.call-done = f32[1,1792,128]{2,1,0:T(8,128)} async-done(((f32[4,1792,128]{2,1,0:T(8,128)}), f32[1,1792,128]{2,1,0:T(8,128)}) %reduce-scatter.3.cloned.1.call-update) | async-done | bytes 917520 | tf_op jit(solution)/shard_map/reduce_scatter | solution.py:60
  207.6 1.0 dynamic-slice_bitcast_fusion.3
  208.7 1.6 collective-permute-start.7
  210.3 1.1 bitcast_add_fusion.2
  211.5 1.6 collective-permute-start.14
  213.1 7.9 %collective-permute-done.7 = f32[896,128]{1,0:T(8,128)S(1)} collective-permute-done((f32[896,128]{1,0:T(8,128)S(1)}, f32[896,128]{1,0:T(8,128)S(1)}, u32[]{:S(2)}, u32[]{:S(2)}) %collective-permute-start.7) | collective-permute-done | bytes 458784 | tf_op jit(solution)/shard_map/ppermute | solution.py:18
  221.0 1.1 bitcast_add_fusion.3
  222.1 1.6 collective-permute-start.8
  223.7 2.8 %collective-permute-start.15 = (f32[224,128]{1,0:T(8,128)S(1)}, f32[224,128]{1,0:T(8,128)S(1)}, u32[]{:S(2)}, u32[]{:S(2)}) collective-permute-start(f32[224,128]{1,0:T(8,128)S(1)} %dynamic-slice_bitcast_fusion.6), channel_id=1, source_target_pairs={{0,32},{16,48},{32,0},{48,16},{1,33},{17,49},{33,1},{49,17},{2,34}... | collective-permute-start | bytes 344072 | tf_op jit(solution)/shard_map/ppermute | solution.py:18
  226.5 3.3 %collective-permute-done.8 = f32[448,128]{1,0:T(8,128)S(1)} collective-permute-done((f32[448,128]{1,0:T(8,128)S(1)}, f32[448,128]{1,0:T(8,128)S(1)}, u32[]{:S(2)}, u32[]{:S(2)}) %collective-permute-start.8) | collective-permute-done | bytes 229408 | tf_op jit(solution)/shard_map/ppermute | solution.py:18
  229.9 3.1 %collective-permute-start.9 = (f32[224,128]{1,0:T(8,128)S(1)}, f32[224,128]{1,0:T(8,128)S(1)}, u32[]{:S(2)}, u32[]{:S(2)}) collective-permute-start(f32[224,128]{1,0:T(8,128)S(1)} %dynamic-slice_bitcast_fusion.7), channel_id=1, source_target_pairs={{0,32},{16,48},{32,0},{48,16},{1,33},{17,49},{33,1},{49,17},{2,34}... | collective-permute-start | bytes 344072 | tf_op jit(solution)/shard_map/ppermute | solution.py:18
  232.9 1.5 collective-permute-done.15
  234.4 2.6 collective-permute-start.16
  237.1 1.8 collective-permute-start.10
  238.9 3.3 %collective-permute-done.16 = f32[224,128]{1,0:T(8,128)S(1)} collective-permute-done((f32[224,128]{1,0:T(8,128)S(1)}, f32[224,128]{1,0:T(8,128)S(1)}, u32[]{:S(2)}, u32[]{:S(2)}) %collective-permute-start.16) | collective-permute-done | bytes 114720 | tf_op jit(solution)/shard_map/ppermute | solution.py:48
  242.2 9.6 %collective-permute-start.17 = (f32[224,128]{1,0:T(8,128)S(1)}, f32[224,128]{1,0:T(8,128)S(1)}, u32[]{:S(2)}, u32[]{:S(2)}) collective-permute-start(f32[224,128]{1,0:T(8,128)S(1)} %add.149), channel_id=1, source_target_pairs={{0,128},{64,192},{128,0},{192,64},{1,129},{65,193},{129,1},{193,65... | collective-permute-start | bytes 344072 | tf_op jit(solution)/shard_map/ppermute | solution.py:48
  251.9 2.3 collective-permute-start.11
  254.2 3.1 %collective-permute-done.17 = f32[224,128]{1,0:T(8,128)S(1)} collective-permute-done((f32[224,128]{1,0:T(8,128)S(1)}, f32[224,128]{1,0:T(8,128)S(1)}, u32[]{:S(2)}, u32[]{:S(2)}) %collective-permute-start.17) | collective-permute-done | bytes 114720 | tf_op jit(solution)/shard_map/ppermute | solution.py:48
  257.3 4.4 %collective-permute-done.11 = f32[224,128]{1,0:T(8,128)S(1)} collective-permute-done((f32[224,128]{1,0:T(8,128)S(1)}, f32[224,128]{1,0:T(8,128)S(1)}, u32[]{:S(2)}, u32[]{:S(2)}) %collective-permute-start.11) | collective-permute-done | bytes 114720 | tf_op jit(solution)/shard_map/ppermute | solution.py:48
  261.9 3.3 %convolution_convert_fusion = bf16[8192,224]{0,1:T(8,128)(2,1)} fusion(bf16[8192,256]{1,0:T(8,128)(2,1)S(1)} %bitcast.103, f32[256,224]{0,1:T(8,128)S(1)} %get-tuple-element.13, f32[256,224]{0,1:T(8,128)S(1)} %get-tuple-element.14), kind=kOutput, calls=%fused_computation.2 | convolution fusion | flops 941645824 | bytes 8323072 | tf_op jit(solution)/shard_map/dot_general | solution.py:90
  (54 shorter events, 1.0 us)
Async XLA Ops:
  7.2 69.6 %copy-start = (bf16[192,8192]{1,0:T(8,128)(2,1)S(1)}, bf16[192,8192]{1,0:T(8,128)(2,1)}, u32[]{:S(2)}) copy-start(bf16[192,8192]{1,0:T(8,128)(2,1)} %param.5) | copy-start | bytes 9437188
  7.2 153.0 %reduce-scatter.5.cloned.1.call-start = ((), (), s32[]{:S(2)}) async-start(), calls=%async_computation.3 | async-start | bytes 4587520 | tf_op jit(solution)/shard_map/reduce_scatter | solution.py:60
  7.2 6.1 %collective-permute-start = (bf16[128,256]{1,0:T(8,128)(2,1)}, bf16[128,256]{1,0:T(8,128)(2,1)S(1)}, u32[]{:S(2)}, u32[]{:S(2)}) collective-permute-start(bf16[128,256]{1,0:T(8,128)(2,1)} %param.7), channel_id=1, source_target_pairs={{0,32},{16,48},{32,0},{48,16},{1,33},{17,49},{33,1},{49,17},{2,34}... | collective-permute-start | bytes 196616 | tf_op jit(solution)/shard_map/ppermute | solution.py:18
  14.2 5.1 %collective-permute-start.1 = (bf16[2,128,256]{2,1,0:T(8,128)(2,1)S(1)}, bf16[2,128,256]{2,1,0:T(8,128)(2,1)S(1)}, u32[]{:S(2)}, u32[]{:S(2)}) collective-permute-start(bf16[2,128,256]{2,1,0:T(8,128)(2,1)S(1)} %pad_maximum_fusion.5), channel_id=1, source_target_pairs={{0,16},{16,0},{32,48},{48,32},{1,17},{17,1},{33,49},{49,33},{2,18}... | collective-permute-start | bytes 393224 | tf_op jit(solution)/shard_map/ppermute | solution.py:18
  19.3 0.7 copy-start.10
  19.9 8.1 %collective-permute-start.2 = (bf16[2,2,128,256]{3,2,0,1:T(8,128)(2,1)S(1)}, bf16[2,2,128,256]{3,2,0,1:T(8,128)(2,1)}, u32[]{:S(2)}, u32[]{:S(2)}) collective-permute-start(bf16[2,2,128,256]{3,2,0,1:T(8,128)(2,1)S(1)} %pad_maximum_fusion.4), channel_id=1, source_target_pairs={{0,4},{2,6},{4,0},{6,2},{1,5},{3,7},{5,1},{7,3},{8,12},{10,14},{12... | collective-permute-start | bytes 786440 | tf_op jit(solution)/shard_map/ppermute | solution.py:18
  29.0 0.7 copy-start.9
  30.6 10.5 %collective-permute-start.3 = (bf16[2,2,2,128,256]{4,3,0,1,2:T(8,128)(2,1)}, bf16[2,2,2,128,256]{4,3,0,1,2:T(8,128)(2,1)}, u32[]{:S(2)}, u32[]{:S(2)}) collective-permute-start(bf16[2,2,2,128,256]{4,3,0,1,2:T(8,128)(2,1)} %pad_maximum_fusion.3), channel_id=1, source_target_pairs={{0,2},{2,0},{4,6},{6,4},{1,3},{3,1},{5,7},{7,5},{8,10},{10,8},{12,... | collective-permute-start | bytes 1572872 | tf_op jit(solution)/shard_map/ppermute | solution.py:18
  42.3 0.8 copy-start.7
  42.3 1.9 copy-start.8
  44.2 21.1 %collective-permute-start.4 = (bf16[2,2,2,2,128,256]{5,4,0,1,2,3:T(8,128)(2,1)}, bf16[2,2,2,2,128,256]{5,4,0,1,2,3:T(8,128)(2,1)}, u32[]{:S(2)}, u32[]{:S(2)}) collective-permute-start(bf16[2,2,2,2,128,256]{5,4,0,1,2,3:T(8,128)(2,1)} %pad_maximum_fusion.2), channel_id=1, source_target_pairs={{0,8},{8,0},{1,9},{9,1},{2,10},{10,2},{3,11},{11,3},{4,12},{12,4},... | collective-permute-start | bytes 3145736 | tf_op jit(solution)/shard_map/ppermute | solution.py:18
  66.9 1.0 copy-start.5
  66.9 2.5 copy-start.6
  69.4 4.5 %collective-permute-start.5 = (bf16[2,2,2,2,2,128,256]{6,5,1,2,0,3,4:T(8,128)(2,1)}, bf16[2,2,2,2,2,128,256]{6,5,1,2,0,3,4:T(8,128)(2,1)}, u32[]{:S(2)}, u32[]{:S(2)}) collective-permute-start(bf16[2,2,2,2,2,128,256]{6,5,1,2,0,3,4:T(8,128)(2,1)} %pad_maximum_fusion.1), channel_id=1, source_target_pairs={{0,1},{1,0},{2,3},{3,2},{4,5},{5,4},{6,7},{7,6},{8,9},{9,8},{10,11... | collective-permute-start | bytes 6291464 | tf_op jit(solution)/shard_map/ppermute | solution.py:18
  76.8 2.1 copy-start.2
  76.8 3.7 %slice-start = ((s8[5505024]{0:T(1024)(128)(4,1)}), s8[4194304]{0:T(1024)(128)(4,1)S(1)}, s32[]{:S(2)}) async-start(s8[5505024]{0:T(1024)(128)(4,1)} %bitcast.104), calls=%async_computation.4 | async-start | bytes 8388608
  76.8 4.1 %slice-start.1 = ((s8[5505024]{0:T(1024)(128)(4,1)}), s8[1310720]{0:T(1024)(128)(4,1)S(1)}, s32[]{:S(2)}) async-start(s8[5505024]{0:T(1024)(128)(4,1)} %bitcast.104), calls=%async_computation.5 | async-start | bytes 2621440
  97.3 4.0 %copy-start.4 = (f32[2,4,2,2,2,224,128]{6,5,4,3,2,1,0:T(8,128)}, f32[2,4,2,2,2,224,128]{6,5,4,3,2,1,0:T(8,128)S(1)}, u32[]{:S(2)}) copy-start(f32[2,4,2,2,2,224,128]{6,5,4,3,2,1,0:T(8,128)S(1)} %copy.16) | copy-start | bytes 22020100
  101.2 6.8 %collective-permute-start.12 = (f32[7168,128]{1,0:T(8,128)}, f32[7168,128]{1,0:T(8,128)}, u32[]{:S(2)}, u32[]{:S(2)}) collective-permute-start(f32[7168,128]{1,0:T(8,128)} %dynamic-slice_bitcast_fusion), channel_id=1, source_target_pairs={{0,1},{1,0},{2,3},{3,2},{4,5},{5,4},{6,7},{7,6},{8,9},{9,8},{10,11... | collective-permute-start | bytes 11010056 | tf_op jit(solution)/shard_map/ppermute | solution.py:18
  113.4 94.2 %reduce-scatter.3.cloned.1.call-start = ((), (), s32[]{:S(2)}) async-start(), calls=%async_computation.2 | async-start | bytes 4587520 | tf_op jit(solution)/shard_map/reduce_scatter | solution.py:60
  132.7 6.7 %collective-permute-start.6 = (f32[7168,128]{1,0:T(8,128)S(1)}, f32[7168,128]{1,0:T(8,128)S(1)}, u32[]{:S(2)}, u32[]{:S(2)}) collective-permute-start(f32[7168,128]{1,0:T(8,128)S(1)} %dynamic-slice_bitcast_fusion.1), channel_id=1, source_target_pairs={{0,1},{1,0},{2,3},{3,2},{4,5},{5,4},{6,7},{7,6},{8,9},{9,8},{10,11... | collective-permute-start | bytes 11010056 | tf_op jit(solution)/shard_map/ppermute | solution.py:18
  161.2 49.1 %collective-permute-start.13 = (f32[896,128]{1,0:T(8,128)S(1)}, f32[896,128]{1,0:T(8,128)S(1)}, u32[]{:S(2)}, u32[]{:S(2)}) collective-permute-start(f32[896,128]{1,0:T(8,128)S(1)} %dynamic-slice_bitcast_fusion.2), channel_id=1, source_target_pairs={{0,8},{8,0},{1,9},{9,1},{2,10},{10,2},{3,11},{11,3},{4,12},{12,4},... | collective-permute-start | bytes 1376264 | tf_op jit(solution)/shard_map/ppermute | solution.py:18
  208.7 12.3 %collective-permute-start.7 = (f32[896,128]{1,0:T(8,128)S(1)}, f32[896,128]{1,0:T(8,128)S(1)}, u32[]{:S(2)}, u32[]{:S(2)}) collective-permute-start(f32[896,128]{1,0:T(8,128)S(1)} %dynamic-slice_bitcast_fusion.3), channel_id=1, source_target_pairs={{0,8},{8,0},{1,9},{9,1},{2,10},{10,2},{3,11},{11,3},{4,12},{12,4},... | collective-permute-start | bytes 1376264 | tf_op jit(solution)/shard_map/ppermute | solution.py:18
  210.3 51.4 %copy-start.13 = (f32[256,224]{0,1:T(8,128)S(1)}, f32[256,224]{0,1:T(8,128)}, u32[]{:S(2)}) copy-start(f32[256,224]{0,1:T(8,128)} %param.9) | copy-start | bytes 688132
  210.3 51.5 %copy-start.14 = (f32[256,224]{0,1:T(8,128)S(1)}, f32[256,224]{0,1:T(8,128)}, u32[]{:S(2)}) copy-start(f32[256,224]{0,1:T(8,128)} %param.8) | copy-start | bytes 688132
  211.4 50.4 %copy-start.3 = (bf16[2,2,2,2,2,2,128,256]{7,6,0,2,3,1,4,5:T(8,128)(2,1)S(1)}, bf16[2,2,2,2,2,2,128,256]{7,6,0,2,3,1,4,5:T(8,128)(2,1)}, u32[]{:S(2)}) copy-start(bf16[2,2,2,2,2,2,128,256]{7,6,0,2,3,1,4,5:T(8,128)(2,1)} %copy-done.2) | copy-start | bytes 12582916
  211.5 12.2 %collective-permute-start.14 = (f32[448,128]{1,0:T(8,128)S(1)}, f32[448,128]{1,0:T(8,128)S(1)}, u32[]{:S(2)}, u32[]{:S(2)}) collective-permute-start(f32[448,128]{1,0:T(8,128)S(1)} %dynamic-slice_bitcast_fusion.4), channel_id=1, source_target_pairs={{0,16},{16,0},{32,48},{48,32},{1,17},{17,1},{33,49},{49,33},{2,18}... | collective-permute-start | bytes 688136 | tf_op jit(solution)/shard_map/ppermute | solution.py:18
  222.1 7.7 %collective-permute-start.8 = (f32[448,128]{1,0:T(8,128)S(1)}, f32[448,128]{1,0:T(8,128)S(1)}, u32[]{:S(2)}, u32[]{:S(2)}) collective-permute-start(f32[448,128]{1,0:T(8,128)S(1)} %dynamic-slice_bitcast_fusion.5), channel_id=1, source_target_pairs={{0,16},{16,0},{32,48},{48,32},{1,17},{17,1},{33,49},{49,33},{2,18}... | collective-permute-start | bytes 688136 | tf_op jit(solution)/shard_map/ppermute | solution.py:18
  223.7 10.7 %collective-permute-start.15 = (f32[224,128]{1,0:T(8,128)S(1)}, f32[224,128]{1,0:T(8,128)S(1)}, u32[]{:S(2)}, u32[]{:S(2)}) collective-permute-start(f32[224,128]{1,0:T(8,128)S(1)} %dynamic-slice_bitcast_fusion.6), channel_id=1, source_target_pairs={{0,32},{16,48},{32,0},{48,16},{1,33},{17,49},{33,1},{49,17},{2,34}... | collective-permute-start | bytes 344072 | tf_op jit(solution)/shard_map/ppermute | solution.py:18
  229.9 7.2 %collective-permute-start.9 = (f32[224,128]{1,0:T(8,128)S(1)}, f32[224,128]{1,0:T(8,128)S(1)}, u32[]{:S(2)}, u32[]{:S(2)}) collective-permute-start(f32[224,128]{1,0:T(8,128)S(1)} %dynamic-slice_bitcast_fusion.7), channel_id=1, source_target_pairs={{0,32},{16,48},{32,0},{48,16},{1,33},{17,49},{33,1},{49,17},{2,34}... | collective-permute-start | bytes 344072 | tf_op jit(solution)/shard_map/ppermute | solution.py:18
  234.4 7.8 %collective-permute-start.16 = (f32[224,128]{1,0:T(8,128)S(1)}, f32[224,128]{1,0:T(8,128)S(1)}, u32[]{:S(2)}, u32[]{:S(2)}) collective-permute-start(f32[224,128]{1,0:T(8,128)S(1)} %bitcast_add_fusion.6), channel_id=1, source_target_pairs={{0,64},{64,0},{128,192},{192,128},{1,65},{65,1},{129,193},{193,129... | collective-permute-start | bytes 344072 | tf_op jit(solution)/shard_map/ppermute | solution.py:48
  237.1 14.8 %collective-permute-start.10 = (f32[224,128]{1,0:T(8,128)S(1)}, f32[224,128]{1,0:T(8,128)S(1)}, u32[]{:S(2)}, u32[]{:S(2)}) collective-permute-start(f32[224,128]{1,0:T(8,128)S(1)} %bitcast_add_fusion.7), channel_id=1, source_target_pairs={{0,64},{64,0},{128,192},{192,128},{1,65},{65,1},{129,193},{193,129... | collective-permute-start | bytes 344072 | tf_op jit(solution)/shard_map/ppermute | solution.py:48
  242.2 15.1 %collective-permute-start.17 = (f32[224,128]{1,0:T(8,128)S(1)}, f32[224,128]{1,0:T(8,128)S(1)}, u32[]{:S(2)}, u32[]{:S(2)}) collective-permute-start(f32[224,128]{1,0:T(8,128)S(1)} %add.149), channel_id=1, source_target_pairs={{0,128},{64,192},{128,0},{192,64},{1,129},{65,193},{129,1},{193,65... | collective-permute-start | bytes 344072 | tf_op jit(solution)/shard_map/ppermute | solution.py:48
  251.9 9.8 %collective-permute-start.11 = (f32[224,128]{1,0:T(8,128)S(1)}, f32[224,128]{1,0:T(8,128)S(1)}, u32[]{:S(2)}, u32[]{:S(2)}) collective-permute-start(f32[224,128]{1,0:T(8,128)S(1)} %add.143), channel_id=1, source_target_pairs={{0,128},{64,192},{128,0},{192,64},{1,129},{65,193},{129,1},{193,65... | collective-permute-start | bytes 344072 | tf_op jit(solution)/shard_map/ppermute | solution.py:48
  261.9 3.4 %copy-start.11 = (f32[256,224]{0,1:T(8,128)}, f32[256,224]{0,1:T(8,128)S(1)}, u32[]{:S(2)}) copy-start(f32[256,224]{0,1:T(8,128)S(1)} %get-tuple-element.13) | copy-start | bytes 688132
  261.9 3.4 %copy-start.12 = (f32[256,224]{0,1:T(8,128)}, f32[256,224]{0,1:T(8,128)S(1)}, u32[]{:S(2)}) copy-start(f32[256,224]{0,1:T(8,128)S(1)} %get-tuple-element.14) | copy-start | bytes 688132
  261.9 3.4 %copy-start.1 = (bf16[192,8192]{1,0:T(8,128)(2,1)S(1)}, bf16[192,8192]{1,0:T(8,128)(2,1)}, u32[]{:S(2)}) copy-start(bf16[192,8192]{1,0:T(8,128)(2,1)} %param.5) | copy-start | bytes 9437188
Sparse Core Ops, SparseCore 0:
  113.5 46.6 reduce-scatter.4
  162.7 44.8 reduce-scatter.2

commit v9 on v8

--- a/solution.py
+++ b/solution.py
@@ -54,9 +54,11 @@
     ff, rank = terms.shape
     cols = ff // (sizes["y"] * sizes["zl"] * sizes["x"] * sizes["core"])
     terms = terms.reshape(2, 2, sizes["zl"], sizes["x"], sizes["core"], cols, rank)
-    terms = jnp.transpose(terms, (4, 3, 2, 1, 0, 5, 6)).reshape(sizes["core"], -1, rank)
-    terms = pair_sum_scatter(terms, "core")
-    terms = terms.reshape(sizes["x"], -1, rank)
+    c = lax.axis_index("core")
+    mine = lax.dynamic_index_in_dim(terms, c, 4, keepdims=False)
+    theirs = lax.dynamic_index_in_dim(terms, 1 - c, 4, keepdims=False)
+    terms = mine + pair_swap(theirs, "core")
+    terms = jnp.transpose(terms, (3, 2, 1, 0, 4, 5)).reshape(sizes["x"], -1, rank)
     terms = lax.psum_scatter(terms, "x", scatter_dimension=0, tiled=True)
     terms = pair_sum_scatter(terms.reshape(sizes["zl"], -1, rank), "zl")
     terms = pair_sum_scatter(terms.reshape(2, -1, rank), "y", 1)

time: 273 us -> 270 us (0.989)
  other arithmetic: 20.9 us -> 17.4 us
    add x8 -> x6, other arithmetic: 9.79 us -> 2.27 us  [pair_sum_scatter(): return mine + pair_swap(theirs, name, bit)]
    squeeze x0 -> x2, local copies, waits for them, and re-layouts: none -> 6.65 us  [reduce_terms(): theirs = lax.dynamic_index_in_dim(terms, 1 - c, 4, keepdims=False)]
    transpose x0 -> x2, other arithmetic: none -> 4.01 us  [reduce_terms(): jnp.transpose(terms, (3, 2, 1, 0, 4, 5)).reshape(sizes['x'], -1, rank)]
    transpose x2, local copies, waits for them, and re-layouts: 7.46 us -> 4.24 us  [reduce_terms(): jnp.transpose(terms, (3, 2, 1, 0, 4, 5)).reshape(sizes['x'], -1, rank)]
  transfers between devices with their start and end apart: 20 -> 20, of which waited for: 16 -> 16; matrix products, arithmetic and copies ran while one was open for 10% -> 9% of each run, Pallas kernels for 0% -> 0%
where the time goes in v9:
time: 270 us; the launch traced here: 269 us
  waiting for transfers between devices  145 us (54%)
  starting transfers between devices  40.7 us (15%)
  local copies, waits for them, and re-layouts  36.4 us (13%)
  other arithmetic  17.4 us (6%)
  matrix products  15.2 us (6%)
  between operations  14.4 us (5%)
    ppermute x14, waiting for transfers between devices, pair_swap(): return lax.ppermute(x, name, [(i, i ^ bit) for i in range(size)])  69.5 us
    reduce_scatter x2, waiting for transfers between devices, reduce_terms(): terms = lax.psum_scatter(terms, 'x', scatter_dimension=0, tiled=True)  64.6 us
    ppermute x14, starting transfers between devices, pair_swap(): return lax.ppermute(x, name, [(i, i ^ bit) for i in range(size)])  24.2 us
    dot_general x2, local copies, waits for them, and re-layouts, body(): lax.dot_general(cotangent, low[:, k * width:(k + 1) * width], (((0,), (0,...  17.2 us
    ppermute x4, starting transfers between devices, all_sum_rep(): x = x + lax.ppermute(x, 'rep', [(i, i ^ step) for i in range(size)])  16.4 us
    another operation x12, other arithmetic, swap_stack(): return jnp.stack([jnp.where(first, x, other), jnp.where(first, other, x)])  11 us
    ppermute x4, waiting for transfers between devices, all_sum_rep(): x = x + lax.ppermute(x, 'rep', [(i, i ^ step) for i in range(size)])  10.8 us
    dot_general x2, matrix products, body(): lax.dot_general(cotangent, low[:, k * width:(k + 1) * width], (((0,), (0,...  10.8 us
  transfers between devices with their start and end apart: 20, of which 16 were waited for; matrix products, arithmetic and copies ran while one was open for 9% of the time, Pallas kernels for 0%

profile of v9, /device:TPU:2, one launch (start us, length us, event | category | flops | bytes accessed | tf_op | source)
XLA Modules:
  0.0 269.0 jit_solution(12449724601279021174)
XLA Ops:
  7.2 3.3 %collective-permute-start = (bf16[128,256]{1,0:T(8,128)(2,1)}, bf16[128,256]{1,0:T(8,128)(2,1)S(1)}, u32[]{:S(2)}, u32[]{:S(2)}) collective-permute-start(bf16[128,256]{1,0:T(8,128)(2,1)} %param.7), channel_id=1, source_target_pairs={{0,32},{16,48},{32,0},{48,16},{1,33},{17,49},{33,1},{49,17},{2,34}... | collective-permute-start | bytes 196616 | tf_op jit(solution)/shard_map/ppermute | solution.py:18
  10.5 2.8 %collective-permute-done = bf16[128,256]{1,0:T(8,128)(2,1)S(1)} collective-permute-done((bf16[128,256]{1,0:T(8,128)(2,1)}, bf16[128,256]{1,0:T(8,128)(2,1)S(1)}, u32[]{:S(2)}, u32[]{:S(2)}) %collective-permute-start) | collective-permute-done | bytes 65568 | tf_op jit(solution)/shard_map/ppermute | solution.py:18
  13.3 0.9 select_bitcast_fusion.11
  14.2 1.7 collective-permute-start.1
  15.8 3.4 %collective-permute-done.1 = bf16[2,128,256]{2,1,0:T(8,128)(2,1)S(1)} collective-permute-done((bf16[2,128,256]{2,1,0:T(8,128)(2,1)S(1)}, bf16[2,128,256]{2,1,0:T(8,128)(2,1)S(1)}, u32[]{:S(2)}, u32[]{:S(2)}) %collective-permute-start.1) | collective-permute-done | bytes 131104 | tf_op jit(solution)/shard_map/ppermute | solution.py:18
  19.3 0.6 copy-done.10
  19.9 2.2 collective-permute-start.2
  22.2 5.9 %collective-permute-done.2 = bf16[2,2,128,256]{3,2,0,1:T(8,128)(2,1)} collective-permute-done((bf16[2,2,128,256]{3,2,0,1:T(8,128)(2,1)S(1)}, bf16[2,2,128,256]{3,2,0,1:T(8,128)(2,1)}, u32[]{:S(2)}, u32[]{:S(2)}) %collective-permute-start.2) | collective-permute-done | bytes 262176 | tf_op jit(solution)/shard_map/ppermute | solution.py:18
  28.0 1.0 select_bitcast_fusion.7
  29.0 0.7 copy-done.9
  29.8 0.8 pad_maximum_fusion.3
  30.6 2.2 collective-permute-start.3
  32.8 8.3 %collective-permute-done.3 = bf16[2,2,2,128,256]{4,3,0,1,2:T(8,128)(2,1)} collective-permute-done((bf16[2,2,2,128,256]{4,3,0,1,2:T(8,128)(2,1)}, bf16[2,2,2,128,256]{4,3,0,1,2:T(8,128)(2,1)}, u32[]{:S(2)}, u32[]{:S(2)}) %collective-permute-start.3) | collective-permute-done | bytes 524320 | tf_op jit(solution)/shard_map/ppermute | solution.py:18
  41.1 1.2 select_bitcast_fusion.5
  42.3 0.8 copy-done.7
  43.1 1.1 pad_maximum_fusion.2
  44.2 1.9 collective-permute-start.4
  46.1 19.2 %collective-permute-done.4 = bf16[2,2,2,2,128,256]{5,4,0,1,2,3:T(8,128)(2,1)} collective-permute-done((bf16[2,2,2,2,128,256]{5,4,0,1,2,3:T(8,128)(2,1)}, bf16[2,2,2,2,128,256]{5,4,0,1,2,3:T(8,128)(2,1)}, u32[]{:S(2)}, u32[]{:S(2)}) %collective-permute-start.4) | collective-permute-done | bytes 1048608 | tf_op jit(solution)/shard_map/ppermute | solution.py:18
  65.3 1.7 select_bitcast_fusion.3
  66.9 1.0 copy-done.5
  67.9 1.5 pad_maximum_fusion.1
  69.4 4.5 %collective-permute-done.5 = bf16[2,2,2,2,2,128,256]{6,5,1,2,0,3,4:T(8,128)(2,1)} collective-permute-done((bf16[2,2,2,2,2,128,256]{6,5,1,2,0,3,4:T(8,128)(2,1)}, bf16[2,2,2,2,2,128,256]{6,5,1,2,0,3,4:T(8,128)(2,1)}, u32[]{:S(2)}, u32[]{:S(2)}) %collective-permute-start.5) | collective-permute-done | bytes 2097184 | tf_op jit(solution)/shard_map/ppermute | solution.py:18
  73.9 2.4 select_bitcast_fusion.1
  76.4 0.4 pad_maximum_fusion
  76.8 1.1 fusion.2
  77.9 1.0 copy-done.2
  78.9 1.6 slice-done
  80.5 0.4 slice-done.1
  80.9 4.1 %convolution_bitcast_fusion = f32[14336,128]{0,1:T(8,128)} fusion(bf16[192,14336]{1,0:T(8,128)(2,1)S(1)} %bitcast.107, bf16[192,256]{1,0:T(8,128)(2,1)S(1)} %fusion.2), kind=kOutput, calls=%fused_computation | convolution fusion | flops 704643072 | bytes 12894208 | tf_op jit(solution)/shard_map/dot_general | solution.py:78
  85.0 8.6 %copy.15 = f32[14336,128]{1,0:T(8,128)} copy(f32[14336,128]{0,1:T(8,128)} %convolution_bitcast_fusion) | data formatting | bytes 14680064 | tf_op jit(solution)/shard_map/dot_general | solution.py:78
  93.6 4.2 %dynamic-slice_bitcast_fusion = f32[2,2,2,4,224,128]{5,4,3,2,1,0:T(8,128)} fusion(f32[2,2,2,4,2,224,128]{6,5,4,3,2,1,0:T(8,128)} %bitcast.108, s32[]{:T(128)S(6)} %select_n.191), kind=kLoop, calls=%fused_computation.8 | loop fusion | bytes 7340036 | tf_op jit(solution)/shard_map/jit(dynamic_index_in_dim)/squeeze | solution.py:59
  98.0 6.6 %collective-permute-done.12 = f32[2,2,2,4,224,128]{5,4,3,2,1,0:T(8,128)} collective-permute-done((f32[2,2,2,4,224,128]{5,4,3,2,1,0:T(8,128)}, f32[2,2,2,4,224,128]{5,4,3,2,1,0:T(8,128)}, u32[]{:S(2)}, u32[]{:S(2)}) %collective-permute-start.12) | collective-permute-done | bytes 3670048 | tf_op jit(solution)/shard_map/ppermute | solution.py:18
  104.5 3.6 %fusion = f32[4,2,2,2,224,128]{5,4,0,1,2,3:T(8,128)S(1)} fusion(f32[2,2,2,4,224,128]{5,4,3,2,1,0:T(8,128)} %collective-permute-done.12, f32[2,2,2,4,2,224,128]{6,5,4,3,2,1,0:T(8,128)} %bitcast.109, s32[]{:T(128)S(6)} %select_n.190), kind=kLoop, calls=%fused_computation.5 | loop fusion | flops 917504 | bytes 11010052 | tf_op jit(solution)/shard_map/transpose | solution.py:61
  108.1 2.1 copy.16
  110.3 6.6 %convolution_bitcast_fusion.1 = f32[14336,128]{0,1:T(8,128)} fusion(bf16[192,14336]{1,0:T(8,128)(2,1)} %param.6, bf16[192,256]{1,0:T(8,128)(2,1)S(1)} %fusion.2), kind=kOutput, calls=%fused_computation.1 | convolution fusion | flops 704643072 | bytes 12894208 | tf_op jit(solution)/shard_map/dot_general | solution.py:78
  117.0 8.6 %copy.13 = f32[14336,128]{1,0:T(8,128)} copy(f32[14336,128]{0,1:T(8,128)} %convolution_bitcast_fusion.1) | data formatting | bytes 14680064 | tf_op jit(solution)/shard_map/dot_general | solution.py:78
  125.6 2.5 dynamic-slice_bitcast_fusion.1
  128.1 0.4 collective-permute-start.6
  128.5 6.2 %collective-permute-done.6 = f32[2,2,2,4,224,128]{5,4,3,2,1,0:T(8,128)S(1)} collective-permute-done((f32[2,2,2,4,224,128]{5,4,3,2,1,0:T(8,128)S(1)}, f32[2,2,2,4,224,128]{5,4,3,2,1,0:T(8,128)S(1)}, u32[]{:S(2)}, u32[]{:S(2)}) %collective-permute-start.6) | collective-permute-done | bytes 3670048 | tf_op jit(solution)/shard_map/ppermute | solution.py:18
  134.7 0.4 fusion.1
  135.2 2.1 copy.14
  137.3 19.8 %reduce-scatter.5.cloned.1.call-done = f32[1,1792,128]{2,1,0:T(8,128)} async-done(((f32[4,1792,128]{2,1,0:T(8,128)}), f32[1,1792,128]{2,1,0:T(8,128)}) %reduce-scatter.5.cloned.1.call-update) | async-done | bytes 917520 | tf_op jit(solution)/shard_map/reduce_scatter | solution.py:62
  157.1 1.0 dynamic-slice_bitcast_fusion.2
  158.2 1.6 collective-permute-start.13
  159.8 44.8 %reduce-scatter.3.cloned.1.call-done = f32[1,1792,128]{2,1,0:T(8,128)} async-done(((f32[4,1792,128]{2,1,0:T(8,128)}), f32[1,1792,128]{2,1,0:T(8,128)}) %reduce-scatter.3.cloned.1.call-update) | async-done | bytes 917520 | tf_op jit(solution)/shard_map/reduce_scatter | solution.py:62
  204.5 1.0 dynamic-slice_bitcast_fusion.3
  205.6 1.6 collective-permute-start.7
  207.2 1.1 bitcast_add_fusion.2
  208.4 1.6 collective-permute-start.14
  210.0 7.9 %collective-permute-done.7 = f32[896,128]{1,0:T(8,128)S(1)} collective-permute-done((f32[896,128]{1,0:T(8,128)S(1)}, f32[896,128]{1,0:T(8,128)S(1)}, u32[]{:S(2)}, u32[]{:S(2)}) %collective-permute-start.7) | collective-permute-done | bytes 458784 | tf_op jit(solution)/shard_map/ppermute | solution.py:18
  217.9 1.1 bitcast_add_fusion.3
  219.0 1.5 collective-permute-start.8
  220.6 2.8 %collective-permute-start.15 = (f32[224,128]{1,0:T(8,128)S(1)}, f32[224,128]{1,0:T(8,128)S(1)}, u32[]{:S(2)}, u32[]{:S(2)}) collective-permute-start(f32[224,128]{1,0:T(8,128)S(1)} %dynamic-slice_bitcast_fusion.6), channel_id=1, source_target_pairs={{0,32},{16,48},{32,0},{48,16},{1,33},{17,49},{33,1},{49,17},{2,34}... | collective-permute-start | bytes 344072 | tf_op jit(solution)/shard_map/ppermute | solution.py:18
  223.4 3.3 %collective-permute-done.8 = f32[448,128]{1,0:T(8,128)S(1)} collective-permute-done((f32[448,128]{1,0:T(8,128)S(1)}, f32[448,128]{1,0:T(8,128)S(1)}, u32[]{:S(2)}, u32[]{:S(2)}) %collective-permute-start.8) | collective-permute-done | bytes 229408 | tf_op jit(solution)/shard_map/ppermute | solution.py:18
  226.8 3.1 %collective-permute-start.9 = (f32[224,128]{1,0:T(8,128)S(1)}, f32[224,128]{1,0:T(8,128)S(1)}, u32[]{:S(2)}, u32[]{:S(2)}) collective-permute-start(f32[224,128]{1,0:T(8,128)S(1)} %dynamic-slice_bitcast_fusion.7), channel_id=1, source_target_pairs={{0,32},{16,48},{32,0},{48,16},{1,33},{17,49},{33,1},{49,17},{2,34}... | collective-permute-start | bytes 344072 | tf_op jit(solution)/shard_map/ppermute | solution.py:18
  229.8 1.5 collective-permute-done.15
  231.4 2.6 collective-permute-start.16
  234.0 1.8 collective-permute-start.10
  235.8 3.3 %collective-permute-done.16 = f32[224,128]{1,0:T(8,128)S(1)} collective-permute-done((f32[224,128]{1,0:T(8,128)S(1)}, f32[224,128]{1,0:T(8,128)S(1)}, u32[]{:S(2)}, u32[]{:S(2)}) %collective-permute-start.16) | collective-permute-done | bytes 114720 | tf_op jit(solution)/shard_map/ppermute | solution.py:48
  239.2 9.6 %collective-permute-start.17 = (f32[224,128]{1,0:T(8,128)S(1)}, f32[224,128]{1,0:T(8,128)S(1)}, u32[]{:S(2)}, u32[]{:S(2)}) collective-permute-start(f32[224,128]{1,0:T(8,128)S(1)} %add.147), channel_id=1, source_target_pairs={{0,128},{64,192},{128,0},{192,64},{1,129},{65,193},{129,1},{193,65... | collective-permute-start | bytes 344072 | tf_op jit(solution)/shard_map/ppermute | solution.py:48
  248.8 2.3 collective-permute-start.11
  251.1 3.1 %collective-permute-done.17 = f32[224,128]{1,0:T(8,128)S(1)} collective-permute-done((f32[224,128]{1,0:T(8,128)S(1)}, f32[224,128]{1,0:T(8,128)S(1)}, u32[]{:S(2)}, u32[]{:S(2)}) %collective-permute-start.17) | collective-permute-done | bytes 114720 | tf_op jit(solution)/shard_map/ppermute | solution.py:48
  254.2 4.4 %collective-permute-done.11 = f32[224,128]{1,0:T(8,128)S(1)} collective-permute-done((f32[224,128]{1,0:T(8,128)S(1)}, f32[224,128]{1,0:T(8,128)S(1)}, u32[]{:S(2)}, u32[]{:S(2)}) %collective-permute-start.11) | collective-permute-done | bytes 114720 | tf_op jit(solution)/shard_map/ppermute | solution.py:48
  258.8 3.3 %convolution_convert_fusion = bf16[8192,224]{0,1:T(8,128)(2,1)} fusion(bf16[8192,256]{1,0:T(8,128)(2,1)S(1)} %bitcast.105, f32[256,224]{0,1:T(8,128)S(1)} %get-tuple-element.13, f32[256,224]{0,1:T(8,128)S(1)} %get-tuple-element.14), kind=kOutput, calls=%fused_computation.2 | convolution fusion | flops 941645824 | bytes 8323072 | tf_op jit(solution)/shard_map/dot_general | solution.py:92
  (54 shorter events, 0.7 us)
Async XLA Ops:
  7.2 69.6 %copy-start = (bf16[192,8192]{1,0:T(8,128)(2,1)S(1)}, bf16[192,8192]{1,0:T(8,128)(2,1)}, u32[]{:S(2)}) copy-start(bf16[192,8192]{1,0:T(8,128)(2,1)} %param.5) | copy-start | bytes 9437188
  7.2 149.9 %reduce-scatter.5.cloned.1.call-start = ((), (), s32[]{:S(2)}) async-start(), calls=%async_computation.3 | async-start | bytes 4587520 | tf_op jit(solution)/shard_map/reduce_scatter | solution.py:62
  7.2 6.1 %collective-permute-start = (bf16[128,256]{1,0:T(8,128)(2,1)}, bf16[128,256]{1,0:T(8,128)(2,1)S(1)}, u32[]{:S(2)}, u32[]{:S(2)}) collective-permute-start(bf16[128,256]{1,0:T(8,128)(2,1)} %param.7), channel_id=1, source_target_pairs={{0,32},{16,48},{32,0},{48,16},{1,33},{17,49},{33,1},{49,17},{2,34}... | collective-permute-start | bytes 196616 | tf_op jit(solution)/shard_map/ppermute | solution.py:18
  14.2 5.1 %collective-permute-start.1 = (bf16[2,128,256]{2,1,0:T(8,128)(2,1)S(1)}, bf16[2,128,256]{2,1,0:T(8,128)(2,1)S(1)}, u32[]{:S(2)}, u32[]{:S(2)}) collective-permute-start(bf16[2,128,256]{2,1,0:T(8,128)(2,1)S(1)} %pad_maximum_fusion.5), channel_id=1, source_target_pairs={{0,16},{16,0},{32,48},{48,32},{1,17},{17,1},{33,49},{49,33},{2,18}... | collective-permute-start | bytes 393224 | tf_op jit(solution)/shard_map/ppermute | solution.py:18
  19.3 0.7 copy-start.10
  19.9 8.1 %collective-permute-start.2 = (bf16[2,2,128,256]{3,2,0,1:T(8,128)(2,1)S(1)}, bf16[2,2,128,256]{3,2,0,1:T(8,128)(2,1)}, u32[]{:S(2)}, u32[]{:S(2)}) collective-permute-start(bf16[2,2,128,256]{3,2,0,1:T(8,128)(2,1)S(1)} %pad_maximum_fusion.4), channel_id=1, source_target_pairs={{0,4},{2,6},{4,0},{6,2},{1,5},{3,7},{5,1},{7,3},{8,12},{10,14},{12... | collective-permute-start | bytes 786440 | tf_op jit(solution)/shard_map/ppermute | solution.py:18
  29.0 0.7 copy-start.9
  30.6 10.5 %collective-permute-start.3 = (bf16[2,2,2,128,256]{4,3,0,1,2:T(8,128)(2,1)}, bf16[2,2,2,128,256]{4,3,0,1,2:T(8,128)(2,1)}, u32[]{:S(2)}, u32[]{:S(2)}) collective-permute-start(bf16[2,2,2,128,256]{4,3,0,1,2:T(8,128)(2,1)} %pad_maximum_fusion.3), channel_id=1, source_target_pairs={{0,2},{2,0},{4,6},{6,4},{1,3},{3,1},{5,7},{7,5},{8,10},{10,8},{12,... | collective-permute-start | bytes 1572872 | tf_op jit(solution)/shard_map/ppermute | solution.py:18
  42.3 0.8 copy-start.7
  42.3 1.9 copy-start.8
  44.2 21.1 %collective-permute-start.4 = (bf16[2,2,2,2,128,256]{5,4,0,1,2,3:T(8,128)(2,1)}, bf16[2,2,2,2,128,256]{5,4,0,1,2,3:T(8,128)(2,1)}, u32[]{:S(2)}, u32[]{:S(2)}) collective-permute-start(bf16[2,2,2,2,128,256]{5,4,0,1,2,3:T(8,128)(2,1)} %pad_maximum_fusion.2), channel_id=1, source_target_pairs={{0,8},{8,0},{1,9},{9,1},{2,10},{10,2},{3,11},{11,3},{4,12},{12,4},... | collective-permute-start | bytes 3145736 | tf_op jit(solution)/shard_map/ppermute | solution.py:18
  66.9 1.0 copy-start.5
  66.9 2.5 copy-start.6
  69.4 4.5 %collective-permute-start.5 = (bf16[2,2,2,2,2,128,256]{6,5,1,2,0,3,4:T(8,128)(2,1)}, bf16[2,2,2,2,2,128,256]{6,5,1,2,0,3,4:T(8,128)(2,1)}, u32[]{:S(2)}, u32[]{:S(2)}) collective-permute-start(bf16[2,2,2,2,2,128,256]{6,5,1,2,0,3,4:T(8,128)(2,1)} %pad_maximum_fusion.1), channel_id=1, source_target_pairs={{0,1},{1,0},{2,3},{3,2},{4,5},{5,4},{6,7},{7,6},{8,9},{9,8},{10,11... | collective-permute-start | bytes 6291464 | tf_op jit(solution)/shard_map/ppermute | solution.py:18
  76.8 2.1 copy-start.2
  76.8 3.7 %slice-start = ((s8[5505024]{0:T(1024)(128)(4,1)}), s8[4194304]{0:T(1024)(128)(4,1)S(1)}, s32[]{:S(2)}) async-start(s8[5505024]{0:T(1024)(128)(4,1)} %bitcast.106), calls=%async_computation.4 | async-start | bytes 8388608
  76.8 4.1 %slice-start.1 = ((s8[5505024]{0:T(1024)(128)(4,1)}), s8[1310720]{0:T(1024)(128)(4,1)S(1)}, s32[]{:S(2)}) async-start(s8[5505024]{0:T(1024)(128)(4,1)} %bitcast.106), calls=%async_computation.5 | async-start | bytes 2621440
  97.8 6.8 %collective-permute-start.12 = (f32[2,2,2,4,224,128]{5,4,3,2,1,0:T(8,128)}, f32[2,2,2,4,224,128]{5,4,3,2,1,0:T(8,128)}, u32[]{:S(2)}, u32[]{:S(2)}) collective-permute-start(f32[2,2,2,4,224,128]{5,4,3,2,1,0:T(8,128)} %dynamic-slice_bitcast_fusion), channel_id=1, source_target_pairs={{0,1},{1,0},{2,3},{3,2},{4,5},{5,4},{6,7},{7,6},{8,9},{9,8},{10,11... | collective-permute-start | bytes 11010056 | tf_op jit(solution)/shard_map/ppermute | solution.py:18
  110.3 94.2 %reduce-scatter.3.cloned.1.call-start = ((), (), s32[]{:S(2)}) async-start(), calls=%async_computation.2 | async-start | bytes 4587520 | tf_op jit(solution)/shard_map/reduce_scatter | solution.py:62
  125.6 9.2 %copy-start.4 = (f32[14336,128]{1,0:T(8,128)S(1)}, f32[14336,128]{1,0:T(8,128)}, u32[]{:S(2)}) copy-start(f32[14336,128]{1,0:T(8,128)} %copy.13) | copy-start | bytes 22020100
  128.1 6.7 %collective-permute-start.6 = (f32[2,2,2,4,224,128]{5,4,3,2,1,0:T(8,128)S(1)}, f32[2,2,2,4,224,128]{5,4,3,2,1,0:T(8,128)S(1)}, u32[]{:S(2)}, u32[]{:S(2)}) collective-permute-start(f32[2,2,2,4,224,128]{5,4,3,2,1,0:T(8,128)S(1)} %dynamic-slice_bitcast_fusion.1), channel_id=1, source_target_pairs={{0,1},{1,0},{2,3},{3,2},{4,5},{5,4},{6,7},{7,6},{8,9},{9,8},{10,11... | collective-permute-start | bytes 11010056 | tf_op jit(solution)/shard_map/ppermute | solution.py:18
  158.2 49.1 %collective-permute-start.13 = (f32[896,128]{1,0:T(8,128)S(1)}, f32[896,128]{1,0:T(8,128)S(1)}, u32[]{:S(2)}, u32[]{:S(2)}) collective-permute-start(f32[896,128]{1,0:T(8,128)S(1)} %dynamic-slice_bitcast_fusion.2), channel_id=1, source_target_pairs={{0,8},{8,0},{1,9},{9,1},{2,10},{10,2},{3,11},{11,3},{4,12},{12,4},... | collective-permute-start | bytes 1376264 | tf_op jit(solution)/shard_map/ppermute | solution.py:18
  205.6 12.3 %collective-permute-start.7 = (f32[896,128]{1,0:T(8,128)S(1)}, f32[896,128]{1,0:T(8,128)S(1)}, u32[]{:S(2)}, u32[]{:S(2)}) collective-permute-start(f32[896,128]{1,0:T(8,128)S(1)} %dynamic-slice_bitcast_fusion.3), channel_id=1, source_target_pairs={{0,8},{8,0},{1,9},{9,1},{2,10},{10,2},{3,11},{11,3},{4,12},{12,4},... | collective-permute-start | bytes 1376264 | tf_op jit(solution)/shard_map/ppermute | solution.py:18
  207.2 51.4 %copy-start.13 = (f32[256,224]{0,1:T(8,128)S(1)}, f32[256,224]{0,1:T(8,128)}, u32[]{:S(2)}) copy-start(f32[256,224]{0,1:T(8,128)} %param.9) | copy-start | bytes 688132
  207.2 51.4 %copy-start.14 = (f32[256,224]{0,1:T(8,128)S(1)}, f32[256,224]{0,1:T(8,128)}, u32[]{:S(2)}) copy-start(f32[256,224]{0,1:T(8,128)} %param.8) | copy-start | bytes 688132
  208.4 50.4 %copy-start.3 = (bf16[2,2,2,2,2,2,128,256]{7,6,0,2,3,1,4,5:T(8,128)(2,1)S(1)}, bf16[2,2,2,2,2,2,128,256]{7,6,0,2,3,1,4,5:T(8,128)(2,1)}, u32[]{:S(2)}) copy-start(bf16[2,2,2,2,2,2,128,256]{7,6,0,2,3,1,4,5:T(8,128)(2,1)} %copy-done.2) | copy-start | bytes 12582916
  208.4 12.1 %collective-permute-start.14 = (f32[448,128]{1,0:T(8,128)S(1)}, f32[448,128]{1,0:T(8,128)S(1)}, u32[]{:S(2)}, u32[]{:S(2)}) collective-permute-start(f32[448,128]{1,0:T(8,128)S(1)} %dynamic-slice_bitcast_fusion.4), channel_id=1, source_target_pairs={{0,16},{16,0},{32,48},{48,32},{1,17},{17,1},{33,49},{49,33},{2,18}... | collective-permute-start | bytes 688136 | tf_op jit(solution)/shard_map/ppermute | solution.py:18
  219.0 7.7 %collective-permute-start.8 = (f32[448,128]{1,0:T(8,128)S(1)}, f32[448,128]{1,0:T(8,128)S(1)}, u32[]{:S(2)}, u32[]{:S(2)}) collective-permute-start(f32[448,128]{1,0:T(8,128)S(1)} %dynamic-slice_bitcast_fusion.5), channel_id=1, source_target_pairs={{0,16},{16,0},{32,48},{48,32},{1,17},{17,1},{33,49},{49,33},{2,18}... | collective-permute-start | bytes 688136 | tf_op jit(solution)/shard_map/ppermute | solution.py:18
  220.6 10.7 %collective-permute-start.15 = (f32[224,128]{1,0:T(8,128)S(1)}, f32[224,128]{1,0:T(8,128)S(1)}, u32[]{:S(2)}, u32[]{:S(2)}) collective-permute-start(f32[224,128]{1,0:T(8,128)S(1)} %dynamic-slice_bitcast_fusion.6), channel_id=1, source_target_pairs={{0,32},{16,48},{32,0},{48,16},{1,33},{17,49},{33,1},{49,17},{2,34}... | collective-permute-start | bytes 344072 | tf_op jit(solution)/shard_map/ppermute | solution.py:18
  226.8 7.2 %collective-permute-start.9 = (f32[224,128]{1,0:T(8,128)S(1)}, f32[224,128]{1,0:T(8,128)S(1)}, u32[]{:S(2)}, u32[]{:S(2)}) collective-permute-start(f32[224,128]{1,0:T(8,128)S(1)} %dynamic-slice_bitcast_fusion.7), channel_id=1, source_target_pairs={{0,32},{16,48},{32,0},{48,16},{1,33},{17,49},{33,1},{49,17},{2,34}... | collective-permute-start | bytes 344072 | tf_op jit(solution)/shard_map/ppermute | solution.py:18
  231.4 7.8 %collective-permute-start.16 = (f32[224,128]{1,0:T(8,128)S(1)}, f32[224,128]{1,0:T(8,128)S(1)}, u32[]{:S(2)}, u32[]{:S(2)}) collective-permute-start(f32[224,128]{1,0:T(8,128)S(1)} %bitcast_add_fusion.6), channel_id=1, source_target_pairs={{0,64},{64,0},{128,192},{192,128},{1,65},{65,1},{129,193},{193,129... | collective-permute-start | bytes 344072 | tf_op jit(solution)/shard_map/ppermute | solution.py:48
  234.0 14.8 %collective-permute-start.10 = (f32[224,128]{1,0:T(8,128)S(1)}, f32[224,128]{1,0:T(8,128)S(1)}, u32[]{:S(2)}, u32[]{:S(2)}) collective-permute-start(f32[224,128]{1,0:T(8,128)S(1)} %bitcast_add_fusion.7), channel_id=1, source_target_pairs={{0,64},{64,0},{128,192},{192,128},{1,65},{65,1},{129,193},{193,129... | collective-permute-start | bytes 344072 | tf_op jit(solution)/shard_map/ppermute | solution.py:48
  239.2 15.1 %collective-permute-start.17 = (f32[224,128]{1,0:T(8,128)S(1)}, f32[224,128]{1,0:T(8,128)S(1)}, u32[]{:S(2)}, u32[]{:S(2)}) collective-permute-start(f32[224,128]{1,0:T(8,128)S(1)} %add.147), channel_id=1, source_target_pairs={{0,128},{64,192},{128,0},{192,64},{1,129},{65,193},{129,1},{193,65... | collective-permute-start | bytes 344072 | tf_op jit(solution)/shard_map/ppermute | solution.py:48
  248.8 9.8 %collective-permute-start.11 = (f32[224,128]{1,0:T(8,128)S(1)}, f32[224,128]{1,0:T(8,128)S(1)}, u32[]{:S(2)}, u32[]{:S(2)}) collective-permute-start(f32[224,128]{1,0:T(8,128)S(1)} %add.141), channel_id=1, source_target_pairs={{0,128},{64,192},{128,0},{192,64},{1,129},{65,193},{129,1},{193,65... | collective-permute-start | bytes 344072 | tf_op jit(solution)/shard_map/ppermute | solution.py:48
  258.8 3.4 %copy-start.11 = (f32[256,224]{0,1:T(8,128)}, f32[256,224]{0,1:T(8,128)S(1)}, u32[]{:S(2)}) copy-start(f32[256,224]{0,1:T(8,128)S(1)} %get-tuple-element.13) | copy-start | bytes 688132
  258.8 3.4 %copy-start.12 = (f32[256,224]{0,1:T(8,128)}, f32[256,224]{0,1:T(8,128)S(1)}, u32[]{:S(2)}) copy-start(f32[256,224]{0,1:T(8,128)S(1)} %get-tuple-element.14) | copy-start | bytes 688132
  258.8 3.4 %copy-start.1 = (bf16[192,8192]{1,0:T(8,128)(2,1)S(1)}, bf16[192,8192]{1,0:T(8,128)(2,1)}, u32[]{:S(2)}) copy-start(bf16[192,8192]{1,0:T(8,128)(2,1)} %param.5) | copy-start | bytes 9437188
Sparse Core Ops, SparseCore 0:
  110.4 46.6 reduce-scatter.4
  159.7 44.8 reduce-scatter.2
